TPU v7x, 256 devices: a whole 4x4x8 slice. The times are simulated.
256 devices in a mesh: chan: 16 (over y, x_hi, core), win: 16 (over z, x_lo).
Axes of the slice: x: 4 (x_hi: 2, x_lo: 2; x = x_hi * 2 + x_lo), y: 4, z: 8, core: 2. Of those that a mesh axis runs over, the one named last changes fastest.
Arguments:
- spectra: bfloat16 [64, 512, 4096], P('win', 'chan'), may hold values from -80 to 80
- quality: int32 [512], P('chan'), may hold values 0 or 1
- source_block: int32 [2], replicated, may hold values from 0 to 63
Outputs:
- correlations: bfloat16 [2, 512, 8, 512], P(None, ('chan', 'win'))
All inputs are finite; a program needn't handle non-finite values. No bound on the sum of `quality` on one device may be relied on, other than what follows from the above.
Results may differ from a plain program's by a relative error of at most 0.0045.
Values may be sent and summed in bfloat16 or wider, within the bound.
A program may use at most 192 MiB of HBM per device.

v0:
```python
import math

import jax
import jax.numpy as jnp
from jax import lax
from jax.sharding import PartitionSpec as P

L = 512
SRC = 8
STEPS = 2


def from_root(value, axis, source):
    kept = jnp.where(lax.axis_index(axis) == source, value, 0).astype(value.dtype)
    return lax.psum(kept, axis)


def lag_table(bins, lags, factor):
    bin_index = lax.iota(jnp.int32, bins)[:, None]
    shifts = lax.iota(jnp.int32, lags)[None, :] - lags // 2
    residue = jnp.mod(bin_index * shifts, 2 * bins)
    phase_angle = residue.astype(jnp.float32) * (2.0 * math.pi / (2 * bins))
    return jnp.concatenate([jnp.cos(phase_angle), -jnp.sin(phase_angle)], axis=0) * factor


def whiten(block, quality):
    values = block.astype(jnp.float32)
    bins = values.shape[-1] // 2
    energy = jnp.sum(values * values, axis=-1) / bins
    weights = quality.astype(jnp.float32)[None, :] / jnp.sqrt(energy + 1e-06)
    return (values * weights[:, :, None]).astype(jnp.bfloat16)


def cross_spectra(sources, receivers):
    bins = sources.shape[-1] // 2
    src_real = sources[:, :, :bins]
    src_imag = sources[:, :, bins:]
    rec_real = receivers[:, :, :bins]
    rec_imag = receivers[:, :, bins:]
    real_part = jnp.einsum("wsf,wrf->rsf", src_real, rec_real, preferred_element_type=jnp.float32)
    real_part = real_part + jnp.einsum(
        "wsf,wrf->rsf", src_imag, rec_imag, preferred_element_type=jnp.float32
    )
    imag_part = jnp.einsum("wsf,wrf->rsf", src_real, rec_imag, preferred_element_type=jnp.float32)
    imag_part = imag_part - jnp.einsum(
        "wsf,wrf->rsf", src_imag, rec_real, preferred_element_type=jnp.float32
    )
    return jnp.concatenate([real_part, imag_part], axis=-1)


def apply_lags(cross, transform):
    lagged = jnp.dot(
        cross.reshape(-1, cross.shape[-1]),
        transform,
        precision=lax.Precision.HIGHEST,
        preferred_element_type=jnp.float32,
    )
    return lagged.reshape(cross.shape[0], cross.shape[1], transform.shape[1])


def body(spectra, quality, source_block):
    window_count, channel_count, row_width = spectra.shape
    bins = row_width // 2
    total_windows = window_count * lax.axis_size("win")
    transform = lag_table(bins, L, 1.0 / math.sqrt(row_width * total_windows))
    whitened = whiten(spectra, quality)
    per_group = channel_count // SRC
    results = []
    for step in range(STEPS):
        block_index = source_block[step]
        root_group = block_index // per_group
        offset = block_index % per_group * SRC
        own_block = lax.dynamic_slice_in_dim(whitened, offset, SRC, 1)
        sources = from_root(own_block, "chan", root_group)
        partial_cross = cross_spectra(sources, whitened)
        stacked = lax.psum_scatter(partial_cross, "win", scatter_dimension=0, tiled=True)
        lagged = apply_lags(stacked, transform)
        results.append(lagged.astype(jnp.bfloat16))
    return jnp.stack(results)


def solution(mesh):
    return jax.shard_map(
        body,
        mesh=mesh,
        in_specs=(P("win", "chan", None), P("chan"), P()),
        out_specs=P(None, ("chan", "win"), None, None),
        check_vma=False,
    )
```

profile of v0, /device:TPU:32, one launch (start us, length us, event | category | flops | bytes accessed | tf_op | source)
XLA Modules:
  0.0 441.8 jit_solution(556799293227208969)
XLA Ops:
  17.8 2.5 copy.4
  21.7 142.9 %all-reduce.3.cloned.1.call-done = (bf16[4,8,4096]{2,1,0:T(8,128)(2,1)}, bf16[4,8,4096]{2,1,0:T(8,128)(2,1)}) async-done(((bf16[4,8,4096]{2,1,0:T(8,128)(2,1)}, bf16[4,8,4096]{2,1,0:T(8,128)(2,1)}), (bf16[4,8,4096]{2,1,0:T(8,128)(2,1)}, bf16[4,8,4096]{2,1,0:T(8,128)(2,1)})) %all-reduce.3.cloned.1.call-update) | async-done | bytes 524304 | tf_op jit(solution)/shard_map/psum | solution.py:15
  170.6 7.4 %fusion.36 = f32[2048,32,8]{1,2,0:T(8,128)} fusion(bf16[4,32,2048]{1,0,2:T(4,128)(2,1)} %copy.4, bf16[4,8,2048]{1,0,2:T(4,128)(2,1)} %copy.5), kind=kOutput, calls=%fused_computation.44 | convolution fusion | flops 4194304 | bytes 2752512 | tf_op jit(solution)/shard_map/wsf,wrf->rsf/dot_general | solution.py:40
  177.9 4.8 %fusion.38 = f32[2048,32,8]{1,2,0:T(8,128)} fusion(bf16[4,32,2048]{1,0,2:T(4,128)(2,1)S(1)} %copy.7, bf16[4,8,2048]{1,0,2:T(4,128)(2,1)S(1)} %copy-done.2), kind=kOutput, calls=%fused_computation.46 | convolution fusion | flops 4194304 | bytes 2752512 | tf_op jit(solution)/shard_map/wsf,wrf->rsf/dot_general | solution.py:44
  182.8 4.8 %fusion.37 = f32[2048,32,8]{1,2,0:T(8,128)} fusion(bf16[4,32,2048]{1,0,2:T(4,128)(2,1)S(1)} %copy.7, bf16[4,8,2048]{1,0,2:T(4,128)(2,1)S(1)} %copy-done.1), kind=kOutput, calls=%fused_computation.45 | convolution fusion | flops 4194304 | bytes 2752512 | tf_op jit(solution)/shard_map/wsf,wrf->rsf/dot_general | solution.py:41
  187.5 4.8 %fusion.39 = f32[2048,32,8]{1,2,0:T(8,128)} fusion(bf16[4,32,2048]{1,0,2:T(4,128)(2,1)S(1)} %copy-done, bf16[4,8,2048]{1,0,2:T(4,128)(2,1)S(1)} %copy-done.1), kind=kOutput, calls=%fused_computation.47 | convolution fusion | flops 4194304 | bytes 2752512 | tf_op jit(solution)/shard_map/wsf,wrf->rsf/dot_general | solution.py:45
  192.3 6.7 %copy.6 = f32[2048,32,8]{0,2,1:T(8,128)} copy(f32[2048,32,8]{1,2,0:T(8,128)} %fusion.36) | data formatting | bytes 4194304 | tf_op jit(solution)/shard_map/wsf,wrf->rsf/dot_general | solution.py:40
  199.0 6.6 %copy.9 = f32[2048,32,8]{0,2,1:T(8,128)} copy(f32[2048,32,8]{1,2,0:T(8,128)} %fusion.37) | data formatting | bytes 4194304 | tf_op jit(solution)/shard_map/wsf,wrf->rsf/dot_general | solution.py:41
  205.6 6.6 %copy.10 = f32[2048,32,8]{0,2,1:T(8,128)} copy(f32[2048,32,8]{1,2,0:T(8,128)} %fusion.38) | data formatting | bytes 4194304 | tf_op jit(solution)/shard_map/wsf,wrf->rsf/dot_general | solution.py:44
  212.2 6.6 %copy.11 = f32[2048,32,8]{0,2,1:T(8,128)} copy(f32[2048,32,8]{1,2,0:T(8,128)} %fusion.39) | data formatting | bytes 4194304 | tf_op jit(solution)/shard_map/wsf,wrf->rsf/dot_general | solution.py:45
  218.8 2.7 add_bitcast_fusion.1
  227.7 7.2 %fusion.40 = f32[2048,32,8]{1,2,0:T(8,128)} fusion(bf16[4,32,2048]{1,0,2:T(4,128)(2,1)} %copy.4, bf16[4,8,2048]{1,0,2:T(4,128)(2,1)} %copy.12), kind=kOutput, calls=%fused_computation.48 | convolution fusion | flops 4194304 | bytes 2752512 | tf_op jit(solution)/shard_map/wsf,wrf->rsf/dot_general | solution.py:40
  234.9 6.6 %copy.13 = f32[2048,32,8]{0,2,1:T(8,128)} copy(f32[2048,32,8]{1,2,0:T(8,128)} %fusion.40) | data formatting | bytes 4194304 | tf_op jit(solution)/shard_map/wsf,wrf->rsf/dot_general | solution.py:40
  244.0 6.0 %fusion.41 = f32[2048,32,8]{1,2,0:T(8,128)} fusion(bf16[4,32,2048]{1,0,2:T(4,128)(2,1)S(1)} %copy.7, bf16[4,8,2048]{1,0,2:T(4,128)(2,1)} %copy.14), kind=kOutput, calls=%fused_computation.49 | convolution fusion | flops 4194304 | bytes 2752512 | tf_op jit(solution)/shard_map/wsf,wrf->rsf/dot_general | solution.py:41
  250.0 6.6 %copy.15 = f32[2048,32,8]{0,2,1:T(8,128)} copy(f32[2048,32,8]{1,2,0:T(8,128)} %fusion.41) | data formatting | bytes 4194304 | tf_op jit(solution)/shard_map/wsf,wrf->rsf/dot_general | solution.py:41
  256.6 7.3 %fusion.43 = f32[2048,32,8]{1,2,0:T(8,128)} fusion(bf16[4,32,2048]{1,0,2:T(4,128)(2,1)} %copy.4, bf16[4,8,2048]{1,0,2:T(4,128)(2,1)} %copy.14), kind=kOutput, calls=%fused_computation.51 | convolution fusion | flops 4194304 | bytes 2752512 | tf_op jit(solution)/shard_map/wsf,wrf->rsf/dot_general | solution.py:45
  263.9 6.7 %copy.17 = f32[2048,32,8]{0,2,1:T(8,128)} copy(f32[2048,32,8]{1,2,0:T(8,128)} %fusion.43) | data formatting | bytes 4194304 | tf_op jit(solution)/shard_map/wsf,wrf->rsf/dot_general | solution.py:45
  270.5 6.0 %fusion.42 = f32[2048,32,8]{1,2,0:T(8,128)} fusion(bf16[4,32,2048]{1,0,2:T(4,128)(2,1)S(1)} %copy.7, bf16[4,8,2048]{1,0,2:T(4,128)(2,1)} %copy.12), kind=kOutput, calls=%fused_computation.50 | convolution fusion | flops 4194304 | bytes 2752512 | tf_op jit(solution)/shard_map/wsf,wrf->rsf/dot_general | solution.py:44
  276.6 6.8 %copy.16 = f32[2048,32,8]{0,2,1:T(8,128)} copy(f32[2048,32,8]{1,2,0:T(8,128)} %fusion.42) | data formatting | bytes 4194304 | tf_op jit(solution)/shard_map/wsf,wrf->rsf/dot_general | solution.py:44
  289.0 18.0 %fusion.15 = (f32[2048,512]{1,0:T(8,128)}, f32[2048,512]{1,0:T(8,128)}) fusion(s32[512]{0:T(512)S(1)} %iota_add_fusion), kind=kLoop, calls=%fused_computation.24 | loop fusion | flops 15728640 | bytes 8390656 | tf_op jit(solution)/shard_map/cos | solution.py:23
  307.0 17.3 %reduce-scatter.3.cloned.1.call-done = f32[2,8,4096]{2,1,0:T(8,128)} async-done(((f32[32,8,4096]{2,1,0:T(8,128)}), f32[2,8,4096]{2,1,0:T(8,128)}) %reduce-scatter.3.cloned.1.call-update) | async-done | bytes 262160 | tf_op jit(solution)/shard_map/reduce_scatter | solution.py:76
  324.3 7.8 %fusion.25 = bf16[1,2,8,512]{3,2,1,0:T(8,128)(2,1)S(1)} fusion(f32[2,8,4096]{2,1,0:T(8,128)} %reduce-scatter.3.cloned.1.call-done, f32[2048,512]{1,0:T(8,128)} %get-tuple-element.16, f32[2048,512]{1,0:T(8,128)} %get-tuple-element.15), kind=kOutput, calls=%fused_computation.30 | convolution fusion | flops 406855680 | bytes 8667136 | tf_op jit(solution)/shard_map/dot_general | solution.py:52
  332.1 94.7 %reduce-scatter.5.cloned.1.call-done = f32[2,8,4096]{2,1,0:T(8,128)} async-done(((f32[32,8,4096]{2,1,0:T(8,128)}), f32[2,8,4096]{2,1,0:T(8,128)}) %reduce-scatter.5.cloned.1.call-update) | async-done | bytes 262160 | tf_op jit(solution)/shard_map/reduce_scatter | solution.py:76
  426.8 7.8 %fusion.22 = bf16[1,2,8,512]{3,2,1,0:T(8,128)(2,1)S(1)} fusion(f32[2,8,4096]{2,1,0:T(8,128)} %reduce-scatter.5.cloned.1.call-done, f32[2048,512]{1,0:T(8,128)} %get-tuple-element.16, f32[2048,512]{1,0:T(8,128)} %get-tuple-element.15), kind=kOutput, calls=%fused_computation.29 | convolution fusion | flops 406855680 | bytes 8667136 | tf_op jit(solution)/shard_map/dot_general | solution.py:52
  (42 shorter events, 28.2 us)
Async XLA Ops:
  6.5 158.0 %all-reduce.3.cloned.1.call-start = ((), (), s32[]{:S(2)}) async-start(), calls=%async_computation.4 | async-start | bytes 1048576 | tf_op jit(solution)/shard_map/psum | solution.py:15
  17.7 306.7 %reduce-scatter.3.cloned.1.call-start = ((), (), s32[]{:S(2)}) async-start(), calls=%async_computation.2 | async-start | bytes 4456448 | tf_op jit(solution)/shard_map/reduce_scatter | solution.py:76
  170.6 7.4 %copy-start.2 = (bf16[4,8,2048]{1,0,2:T(4,128)(2,1)S(1)}, bf16[4,8,2048]{1,0,2:T(4,128)(2,1)}, u32[]{:S(2)}) copy-start(bf16[4,8,2048]{1,0,2:T(4,128)(2,1)} %copy.5) | copy-start | bytes 393220
  177.9 4.8 %copy-start.1 = (bf16[4,8,2048]{1,0,2:T(4,128)(2,1)S(1)}, bf16[4,8,2048]{1,0,2:T(4,128)(2,1)}, u32[]{:S(2)}) copy-start(bf16[4,8,2048]{1,0,2:T(4,128)(2,1)} %copy.8) | copy-start | bytes 393220
  182.8 4.8 %copy-start = (bf16[4,32,2048]{1,0,2:T(4,128)(2,1)S(1)}, bf16[4,32,2048]{1,0,2:T(4,128)(2,1)}, u32[]{:S(2)}) copy-start(bf16[4,32,2048]{1,0,2:T(4,128)(2,1)} %copy.4) | copy-start | bytes 1572868
  218.8 2.9 copy-start.5
  218.8 3.5 copy-start.6
  225.0 201.8 %reduce-scatter.5.cloned.1.call-start = ((), (), s32[]{:S(2)}) async-start(), calls=%async_computation.3 | async-start | bytes 4456448 | tf_op jit(solution)/shard_map/reduce_scatter | solution.py:76
  276.6 6.8 %copy-start.3 = (f32[2048,32,8]{0,2,1:T(8,128)S(1)}, f32[2048,32,8]{0,2,1:T(8,128)}, u32[]{:S(2)}) copy-start(f32[2048,32,8]{0,2,1:T(8,128)} %copy.13) | copy-start | bytes 6291460
  283.4 2.2 copy-start.4
  283.4 2.9 copy-start.7
Sparse Core Ops, SparseCore 0:
  17.8 146.7 all-reduce.2
  225.1 99.1 reduce-scatter.2
  327.0 99.7 reduce-scatter.4
where the time goes:
time: 445 us; the launch traced here: 442 us
  waiting for transfers between devices  255 us (57%)
  local copies, waits for them, and re-layouts  71.1 us (16%)
  matrix products  63.8 us (14%)
  other arithmetic  33.2 us (7%)
  between operations  18.4 us (4%)
    psum x1, waiting for transfers between devices, from_root(): return lax.psum(kept, axis)  143 us
    reduce_scatter x2, waiting for transfers between devices, body(): lax.psum_scatter(partial_cross, 'win', scatter_dimension=0, tiled=True)  112 us
    cos x1, other arithmetic, lag_table(): jnp.cos(phase_angle)  18 us
    dot_general x2, matrix products, apply_lags(): jnp.dot(cross.reshape(-1, cross.shape[-1]), transform, precision=lax.Prec...  15.6 us
    dot_general x2, matrix products, cross_spectra(): jnp.einsum('wsf,wrf->rsf', src_real, rec_real, preferred_element_type=jnp...  14.6 us
    dot_general x2, local copies, waits for them, and re-layouts, cross_spectra(): jnp.einsum('wsf,wrf->rsf', src_real, rec_imag, preferred_element_type=jnp...  13.5 us
    dot_general x2, local copies, waits for them, and re-layouts, cross_spectra(): jnp.einsum('wsf,wrf->rsf', src_real, rec_real, preferred_element_type=jnp...  13.3 us
    dot_general x2, local copies, waits for them, and re-layouts, cross_spectra(): jnp.einsum('wsf,wrf->rsf', src_imag, rec_real, preferred_element_type=jnp...  13.3 us
  transfers between devices with their start and end apart: 3, of which 3 were waited for; matrix products, arithmetic and copies ran while one was open for 21% of the time, Pallas kernels for 0%

commit v1 on v0

v1 whole, which is shorter than its diff:
```python
import math

import jax
import jax.numpy as jnp
from jax import lax
from jax.experimental import pallas as pl
from jax.sharding import PartitionSpec as P

L = 512
SRC = 8
STEPS = 2


def from_root(value, axis, source):
    kept = jnp.where(lax.axis_index(axis) == source, value, 0).astype(value.dtype)
    return lax.psum(kept, axis)


def lag_table(bins, lags, factor):
    inner = 64
    period = 2 * bins
    shifts = lax.iota(jnp.int32, lags)[None, :] - lags // 2
    hi = lax.iota(jnp.int32, bins // inner)[:, None] * inner
    lo = lax.iota(jnp.int32, inner)[:, None]
    scale = 2.0 * math.pi / period
    angle_hi = jnp.mod(hi * shifts, period).astype(jnp.float32) * scale
    angle_lo = jnp.mod(lo * shifts, period).astype(jnp.float32) * scale
    cos_hi, sin_hi = jnp.cos(angle_hi)[:, None, :], jnp.sin(angle_hi)[:, None, :]
    cos_lo, sin_lo = jnp.cos(angle_lo)[None, :, :], jnp.sin(angle_lo)[None, :, :]
    cos_t = (cos_hi * cos_lo - sin_hi * sin_lo).reshape(bins, lags)
    sin_t = (sin_hi * cos_lo + cos_hi * sin_lo).reshape(bins, lags)
    return cos_t * factor, -sin_t * factor


def whiten(block, quality):
    values = block.astype(jnp.float32)
    bins = values.shape[-1] // 2
    energy = jnp.sum(values * values, axis=-1) / bins
    weights = quality.astype(jnp.float32)[None, :] / jnp.sqrt(energy + 1e-06)
    return (values * weights[:, :, None]).astype(jnp.bfloat16)


def cross_spectra(sources, receivers):
    bins = sources.shape[-1] // 2
    sr = sources[:, None, :, :bins].astype(jnp.float32)
    si = sources[:, None, :, bins:].astype(jnp.float32)
    rr = receivers[:, :, None, :bins].astype(jnp.float32)
    ri = receivers[:, :, None, bins:].astype(jnp.float32)
    real_part = jnp.sum(sr * rr + si * ri, axis=0)
    imag_part = jnp.sum(sr * ri - si * rr, axis=0)
    return real_part, imag_part


def cast_kernel(x_ref, o_ref):
    o_ref[...] = x_ref[...].astype(o_ref.dtype)


def to_bf16(x):
    return pl.pallas_call(
        cast_kernel, out_shape=jax.ShapeDtypeStruct(x.shape, jnp.bfloat16)
    )(x)


def body(spectra, quality, source_block):
    window_count, channel_count, row_width = spectra.shape
    bins = row_width // 2
    total_windows = window_count * lax.axis_size("win")
    cos_t, sin_t = lag_table(bins, L, 1.0 / math.sqrt(row_width * total_windows))
    whitened = whiten(spectra, quality)
    per_group = channel_count // SRC
    own = []
    roots = []
    for step in range(STEPS):
        block_index = source_block[step]
        offset = block_index % per_group * SRC
        own.append(lax.dynamic_slice_in_dim(whitened, offset, SRC, 1))
        roots.append(block_index // per_group)
    me = lax.axis_index("chan")
    kept = jnp.stack(
        [jnp.where(me == roots[k], own[k], jnp.zeros_like(own[k])) for k in range(STEPS)]
    )
    sources = lax.psum(kept, "chan")
    win_size = lax.axis_size("win")
    per_dest = channel_count // win_size
    reals, imags = [], []
    for step in range(STEPS):
        real_part, imag_part = cross_spectra(sources[step], whitened)
        reals.append(real_part.reshape(win_size, per_dest, SRC, bins))
        imags.append(imag_part.reshape(win_size, per_dest, SRC, bins))
    rows = channel_count * SRC * STEPS
    real_rows = jnp.stack(reals, axis=1).reshape(rows, bins)
    imag_rows = jnp.stack(imags, axis=1).reshape(rows, bins)
    out = jnp.dot(
        real_rows, cos_t, precision=lax.Precision.HIGHEST, preferred_element_type=jnp.float32
    )
    out = out + jnp.dot(
        imag_rows, sin_t, precision=lax.Precision.HIGHEST, preferred_element_type=jnp.float32
    )
    out = out.reshape(win_size, STEPS * per_dest * SRC * L)
    stacked = lax.psum_scatter(out, "win", scatter_dimension=0, tiled=True)
    return to_bf16(stacked.reshape(STEPS * per_dest * SRC, L)).reshape(STEPS, per_dest, SRC, L)


def solution(mesh):
    return jax.shard_map(
        body,
        mesh=mesh,
        in_specs=(P("win", "chan", None), P("chan"), P()),
        out_specs=P(None, ("chan", "win"), None, None),
        check_vma=False,
    )
```

time: 445 us -> 342 us (0.77)
  local copies, waits for them, and re-layouts: 71.1 us -> 8.46 us
  matrix products: 63.8 us -> 13.7 us
  waiting for transfers between devices: 255 us -> 280 us
  other arithmetic: 33.2 us -> 17.6 us
    unnamed x3, waiting for transfers between devices: 0.05 us -> 139 us
    reduce_scatter x2 -> x0, waiting for transfers between devices: 112 us -> none  [body(): lax.psum_scatter(partial_cross, 'win', scatter_dimension=0, tiled=True)]
    dot_general x8 -> x0, local copies, waits for them, and re-layouts: 53.2 us -> none  [the longest x2 13.5 us: cross_spectra(): jnp.einsum('wsf,wrf->rsf', src_real, rec_imag, preferred_element_type=jnp...]
    dot_general x10 -> x2, matrix products: 63.8 us -> 13.7 us  [the longest x1 6.84 us: body(): jnp.dot(real_rows, cos_t, precision=lax.Precision.HIGHEST, preferred_elem...]
    cos x1 -> x2, other arithmetic: 18 us -> 0.87 us  [the longest x1 0.53 us: lag_table(): jnp.cos(angle_lo)[None, :, :]]
    slice x8 -> x0, local copies, waits for them, and re-layouts: 14.8 us -> none  [the longest x3 5.98 us: cross_spectra(): src_imag = sources[:, :, bins:]]
    reduce_sum x0 -> x1, other arithmetic: none -> 6.44 us  [cross_spectra(): imag_part = jnp.sum(sr * ri - si * rr, axis=0)]
    concatenate x2 -> x0, other arithmetic: 4.85 us -> none  [cross_spectra(): return jnp.concatenate([real_part, imag_part], axis=-1)]
  transfers between devices with their start and end apart: 3 -> 2, of which waited for: 3 -> 2; matrix products, arithmetic and copies ran while one was open for 21% -> 2% of each run, Pallas kernels for 0% -> 0%
where the time goes in v1:
time: 342 us; the launch traced here: 340 us
  waiting for transfers between devices  280 us (82%)
  between operations  19 us (6%)
  other arithmetic  17.6 us (5%)
  matrix products  13.7 us (4%)
  local copies, waits for them, and re-layouts  8.46 us (2%)
    psum x1, waiting for transfers between devices, body(): sources = lax.psum(kept, 'chan')  141 us
    unnamed x3, waiting for transfers between devices  139 us
    dot_general x1, matrix products, body(): jnp.dot(real_rows, cos_t, precision=lax.Precision.HIGHEST, preferred_elem...  6.84 us
  transfers between devices with their start and end apart: 2, of which 2 were waited for; matrix products, arithmetic and copies ran while one was open for 2% of the time, Pallas kernels for 0%

profile of v1, /device:TPU:32, one launch (start us, length us, event | category | flops | bytes accessed | tf_op | source)
XLA Modules:
  0.0 339.7 jit_solution(15127616954680309977)
XLA Ops:
  6.5 1.4 fusion.15
  13.3 1.5 fusion
  14.9 0.7 convert_element_type.60
  15.5 1.5 fusion.1
  17.1 0.9 pad_maximum_fusion.2
  18.1 0.5 fusion.12
  18.7 0.3 fusion.14
  19.0 4.5 %negate_multiply_fusion = (f32[32,64,512]{2,1,0:T(8,128)}, f32[32,64,512]{2,1,0:T(8,128)}) fusion(f32[64,512]{1,0:T(8,128)S(1)} %get-tuple-element.26, f32[32,512]{1,0:T(8,128)S(1)} %get-tuple-element.24, f32[64,512]{1,0:T(8,128)S(1)} %get-tuple-element.25, f32[32,512]{1,0:T(8,128)S(1)} %get-tuple-element.23), kind=kLoop, calls=%fused_computation.6 | loop fusion | flops 9437184 | bytes 8781824 | tf_op jit(solution)/shard_map/mul | solution.py:32
  23.5 0.2 slice_convert_fusion.1
  23.8 141.0 %all-reduce.4.cloned.1.call-done = bf16[2,4,8,4096]{3,2,1,0:T(8,128)(2,1)} async-done(((bf16[2,4,8,4096]{3,2,1,0:T(8,128)(2,1)}), bf16[2,4,8,4096]{3,2,1,0:T(8,128)(2,1)}) %all-reduce.4.cloned.1.call-update) | async-done | bytes 524304 | tf_op jit(solution)/shard_map/psum | solution.py:82
  164.7 1.1 slice_bitcast_fusion
  165.8 0.1 slice_convert_fusion.3
  165.9 6.4 %subtract_reduce_fusion.1 = (f32[32,8,2048]{2,1,0:T(8,128)S(1)}, f32[32,8,2048]{2,1,0:T(8,128)S(1)}, f32[32,8,2048]{2,1,0:T(8,128)S(1)}, f32[32,8,2048]{2,1,0:T(8,128)S(1)}) fusion(f32[4,32,2048]{2,1,0:T(8,128)S(1)} %get-tuple-element.12, f32[4,8,2048]{2,1,0:T(8,128)S(1)} %get-tuple-element.29, f32[4,32,2048]{2,1,0:T(8,128)S(1)} %get-tuple-element.11, ...), kind=kLoop, calls=%fused_computation.1 | loop fusion | flops 31457280 | bytes 11534336 | tf_op jit(solution)/shard_map/reduce_sum | solution.py:50
  172.3 0.3 pad_maximum_fusion.1
  172.6 0.5 pad_maximum_fusion
  173.1 1.7 copy-done
  174.8 6.8 %fusion.16 = f32[512,512]{1,0:T(8,128)S(1)} fusion(f32[512,2048]{1,0:T(8,128)S(1)} %bitcast.32, f32[2048,512]{1,0:T(8,128)S(1)} %bitcast.33), kind=kOutput, calls=%fused_computation.50 | convolution fusion | flops 6442450944 | bytes 9437184 | tf_op jit(solution)/shard_map/dot_general | solution.py:93
  181.7 6.8 %convolution_add_fusion = f32[512,512]{1,0:T(8,128)S(1)} fusion(f32[512,512]{1,0:T(8,128)S(1)} %fusion.16, f32[512,2048]{1,0:T(8,128)S(1)} %bitcast.35, f32[2048,512]{1,0:T(8,128)S(1)} %bitcast.34), kind=kOutput, calls=%fused_computation.12 | convolution fusion | flops 6442713088 | bytes 10485760 | tf_op jit(solution)/shard_map/dot_general | solution.py:96
  188.5 1.2 reshape.211
  189.8 0.6 dynamic-slice
  190.4 138.5 %all-reduce.6.cloned.1.call-done = f32[16,16384]{1,0:T(8,128)} async-done(((f32[16,16384]{1,0:T(8,128)}), f32[16,16384]{1,0:T(8,128)}) %all-reduce.6.cloned.1.call-update) | async-done | bytes 1048592
  328.9 1.9 dynamic-slice_reduce_fusion
  330.8 0.6 reshape.212.x_ref
  331.4 1.5 shard_map.37
  (13 shorter events, 0.2 us)
Async XLA Ops:
  6.5 158.2 %all-reduce.4.cloned.1.call-start = ((), (), s32[]{:S(2)}) async-start(), calls=%async_computation | async-start | bytes 1048576 | tf_op jit(solution)/shard_map/psum | solution.py:82
  18.1 310.9 %all-reduce.6.cloned.1.call-start = ((), (), s32[]{:S(2)}) async-start(), calls=%async_computation.1 | async-start | bytes 2097152
  172.6 2.2 copy-start
  174.8 6.9 %copy-start.1 = (f32[32,64,512]{2,1,0:T(8,128)S(1)}, f32[32,64,512]{2,1,0:T(8,128)}, u32[]{:S(2)}) copy-start(f32[32,64,512]{2,1,0:T(8,128)} %get-tuple-element.17) | copy-start | bytes 12582916
  181.7 8.1 %copy-start.2 = (u32[256]{0:T(256)S(1)}, u32[256]{0:T(256)}, u32[]{:S(2)}) copy-start(u32[256]{0:T(256)} %constant.91) | copy-start | bytes 3076
Sparse Core Ops, SparseCore 0:
  18.2 146.4 all-reduce.3
  189.9 138.9 all-reduce.5

commit v2 on v1

--- a/solution.py
+++ b/solution.py
@@ -1,9 +1,11 @@
+import functools
 import math
 
 import jax
 import jax.numpy as jnp
 from jax import lax
 from jax.experimental import pallas as pl
+from jax.experimental.pallas import tpu as pltpu
 from jax.sharding import PartitionSpec as P
 
 L = 512
@@ -51,6 +53,67 @@
     return real_part, imag_part
 
 
+def exchange_kernel(axis, n, single, x_ref, o_ref, buf, send_sem, recv_sem):
+    me = lax.axis_index(axis)
+    own = x_ref.at[0] if single else x_ref.at[me]
+    buf[me] = own[...]
+    barrier = pltpu.get_barrier_semaphore()
+    for k in range(1, n):
+        pl.semaphore_signal(barrier, inc=1, device_id={axis: (me + k) % n},
+                            device_id_type=pl.DeviceIdType.MESH)
+    pl.semaphore_wait(barrier, n - 1)
+    copies = []
+    for k in range(1, n):
+        peer = (me + k) % n
+        src = x_ref.at[0] if single else x_ref.at[peer]
+        copy = pltpu.make_async_remote_copy(
+            src_ref=src, dst_ref=buf.at[me], send_sem=send_sem.at[k],
+            recv_sem=recv_sem.at[me], device_id={axis: peer},
+            device_id_type=pl.DeviceIdType.MESH)
+        copy.start()
+        copies.append(copy)
+    for copy in copies:
+        copy.wait_send()
+    for k in range(1, n):
+        source = (me + n - k) % n
+        pltpu.make_async_remote_copy(
+            src_ref=buf.at[source], dst_ref=buf.at[source], send_sem=send_sem.at[k],
+            recv_sem=recv_sem.at[source], device_id={axis: source},
+            device_id_type=pl.DeviceIdType.MESH).wait_recv()
+    o_ref[...] = buf[...]
+
+
+def exchange(x, axis, n, cid):
+    single = x.shape[0] == 1
+    shape = (n,) + x.shape[1:]
+    return pl.pallas_call(
+        functools.partial(exchange_kernel, axis, n, single),
+        out_shape=jax.ShapeDtypeStruct(shape, x.dtype),
+        in_specs=[pl.BlockSpec(memory_space=pltpu.VMEM)],
+        out_specs=pl.BlockSpec(memory_space=pltpu.VMEM),
+        scratch_shapes=[pltpu.VMEM(shape, x.dtype), pltpu.SemaphoreType.DMA((n,)),
+                        pltpu.SemaphoreType.DMA((n,))],
+        compiler_params=pltpu.CompilerParams(collective_id=cid, has_side_effects=True),
+    )(x)
+
+
+def chunks(value, n):
+    return value.reshape(n, 16, -1)
+
+
+def broadcast_sum(value, axis):
+    n = lax.axis_size(axis)
+    mine = jnp.sum(exchange(chunks(value, n), axis, n, 0), axis=0, dtype=jnp.float32)
+    gathered = exchange(mine.astype(value.dtype)[None], axis, n, 1)
+    return gathered.reshape(value.shape)
+
+
+def scatter_sum(rows, axis):
+    n = rows.shape[0]
+    got = exchange(chunks(rows, n), axis, n, 2)
+    return jnp.sum(got, axis=0).reshape(rows.shape[1:])
+
+
 def cast_kernel(x_ref, o_ref):
     o_ref[...] = x_ref[...].astype(o_ref.dtype)
 
@@ -79,7 +142,7 @@
     kept = jnp.stack(
         [jnp.where(me == roots[k], own[k], jnp.zeros_like(own[k])) for k in range(STEPS)]
     )
-    sources = lax.psum(kept, "chan")
+    sources = broadcast_sum(kept, "chan")
     win_size = lax.axis_size("win")
     per_dest = channel_count // win_size
     reals, imags = [], []
@@ -97,7 +160,7 @@
         imag_rows, sin_t, precision=lax.Precision.HIGHEST, preferred_element_type=jnp.float32
     )
     out = out.reshape(win_size, STEPS * per_dest * SRC * L)
-    stacked = lax.psum_scatter(out, "win", scatter_dimension=0, tiled=True)
+    stacked = scatter_sum(out, "win")
     return to_bf16(stacked.reshape(STEPS * per_dest * SRC, L)).reshape(STEPS, per_dest, SRC, L)
 
 

time: 342 us -> 107 us (0.31)
  waiting for transfers between devices: 280 us -> 0 us
  Pallas kernels: 1.46 us -> 64 us
  between operations: 19 us -> 5.57 us
    psum x1 -> x0, waiting for transfers between devices: 141 us -> none  [body(): sources = lax.psum(kept, 'chan')]
    unnamed x3 -> x0, waiting for transfers between devices: 139 us -> none
    pallas_call x0 -> x3, Pallas kernels: none -> 62.6 us  [exchange(): pl.pallas_call(functools.partial(exchange_kernel, axis, n, single), out_s...]
    unnamed x8 -> x0, local copies, waits for them, and re-layouts: 4.15 us -> none
  transfers between devices with their start and end apart: 2 -> 0, of which waited for: 2 -> 0; matrix products, arithmetic and copies ran while one was open for 2% -> 0% of each run, Pallas kernels for 0% -> 0%
where the time goes in v2:
time: 107 us; the launch traced here: 105 us
  Pallas kernels  64 us (60%)
  other arithmetic  16.4 us (15%)
  matrix products  13.7 us (13%)
  local copies, waits for them, and re-layouts  5.85 us (5%)
  between operations  5.57 us (5%)
    pallas_call x3, Pallas kernels, exchange(): pl.pallas_call(functools.partial(exchange_kernel, axis, n, single), out_s...  62.6 us
    dot_general x1, matrix products, body(): jnp.dot(real_rows, cos_t, precision=lax.Precision.HIGHEST, preferred_elem...  6.84 us
    dot_general x1, matrix products, body(): jnp.dot(imag_rows, sin_t, precision=lax.Precision.HIGHEST, preferred_elem...  6.84 us
    reduce_sum x1, other arithmetic, cross_spectra(): imag_part = jnp.sum(sr * ri - si * rr, axis=0)  6.44 us

profile of v2, /device:TPU:32, one launch (start us, length us, event | category | flops | bytes accessed | tf_op | source)
XLA Modules:
  0.0 105.5 jit_solution(15644413800803475554)
XLA Ops:
  0.0 0.7 convert_element_type.62
  0.7 1.4 %fusion.16 = (s32[1]{0:T(128)}, s32[1]{0:T(128)}) fusion(s32[2]{0:T(128)} %param.5), kind=kLoop, calls=%fused_computation.47 | loop fusion | bytes 16 | tf_op jit(solution)/shard_map/slice | solution.py:137
  7.5 1.5 %fusion = f32[4,32]{1,0:T(4,128)S(1)} fusion(bf16[4,32,4096]{2,1,0:T(8,128)(2,1)} %param.3), kind=kLoop, calls=%fused_computation.10 | loop fusion | flops 1572736 | bytes 1049088 | tf_op jit(solution)/shard_map/reduce_sum | solution.py:40
  9.0 0.3 fusion.14
  9.4 0.5 fusion.12
  9.9 1.5 %fusion.1 = bf16[4,32,4096]{2,1,0:T(8,128)(2,1)S(1)} fusion(bf16[4,32,4096]{2,1,0:T(8,128)(2,1)} %param.3, f32[4,32]{1,0:T(4,128)S(1)} %rsqrt_multiply_fusion), kind=kLoop, calls=%fused_computation.11 | loop fusion | flops 1572864 | bytes 2097664 | tf_op jit(solution)/shard_map/convert_element_type | solution.py:42
  11.5 1.1 %reshape.211.x_ref = bf16[16,16,1024]{2,1,0:T(8,128)(2,1)} reshape(bf16[2,4,8,4096]{3,2,1,0:T(8,128)(2,1)S(1)} %pad_maximum_fusion.2) | data formatting | bytes 1048576 | tf_op jit(solution)/shard_map/reshape | solution.py:101
  12.6 15.1 %shard_map.37 = bf16[16,16,1024]{2,1,0:T(8,128)(2,1)} custom-call(bf16[16,16,1024]{2,1,0:T(8,128)(2,1)} %reshape.211.x_ref), custom_call_target="tpu_custom_call" | custom-call | tf_op jit(solution)/shard_map/pallas_call | solution.py:89
  27.7 1.7 %reduce_sum.67 = bf16[16,1024]{1,0:T(8,128)(2,1)} reduce(bf16[16,16,1024]{2,1,0:T(8,128)(2,1)} %shard_map.37, bf16[]{:T(256)} %constant.82.clone.1), dimensions={0}, to_apply=%region_1.2 | reduce | flops 245760 | bytes 557058 | tf_op jit(solution)/shard_map/reduce_sum | solution.py:106
  29.5 14.1 %shard_map.38 = bf16[16,16,1024]{2,1,0:T(8,128)(2,1)} custom-call(bf16[1,16,1024]{2,1,0:T(8,128)(2,1)} %bitcast.38), custom_call_target="tpu_custom_call" | custom-call | tf_op jit(solution)/shard_map/pallas_call | solution.py:89
  43.6 1.1 %fusion.15 = (bf16[8,16,1024]{2,1,0:T(8,128)(2,1)S(1)}, bf16[8,16,1024]{2,1,0:T(8,128)(2,1)S(1)}) fusion(bf16[16,16,1024]{2,1,0:T(8,128)(2,1)} %shard_map.38), kind=kLoop, calls=%fused_computation.46 | loop fusion | bytes 1048576 | tf_op jit(solution)/shard_map/slice | solution.py:150
  44.6 0.2 squeeze.15
  45.1 0.2 slice_convert_fusion.1
  45.3 6.4 %subtract_reduce_fusion.1 = (f32[32,8,2048]{2,1,0:T(8,128)S(1)}, f32[32,8,2048]{2,1,0:T(8,128)S(1)}, f32[32,8,2048]{2,1,0:T(8,128)S(1)}, f32[32,8,2048]{2,1,0:T(8,128)S(1)}) fusion(f32[4,32,2048]{2,1,0:T(8,128)S(1)} %get-tuple-element.12, f32[4,8,2048]{2,1,0:T(8,128)S(1)} %get-tuple-element.29, f32[4,32,2048]{2,1,0:T(8,128)S(1)} %get-tuple-element.11, ...), kind=kLoop, calls=%fused_computation.1 | loop fusion | flops 31457280 | bytes 11534336 | tf_op jit(solution)/shard_map/reduce_sum | solution.py:52
  51.8 0.3 pad_maximum_fusion.1
  52.0 0.5 pad_maximum_fusion
  52.5 1.1 %negate_multiply_fusion = (f32[32,64,512]{2,1,0:T(8,128)S(1)}, f32[32,64,512]{2,1,0:T(8,128)S(1)}) fusion(f32[64,512]{1,0:T(8,128)S(1)} %get-tuple-element.26, f32[32,512]{1,0:T(8,128)S(1)} %get-tuple-element.24, f32[64,512]{1,0:T(8,128)S(1)} %get-tuple-element.25, f32[32,512]{1,0:T(8,128)S(1)} %get-tuple-element.23), kind=kLoop, calls=%fused_computation.6 | loop fusion | flops 9437184 | bytes 8781824 | tf_op jit(solution)/shard_map/mul | solution.py:34
  53.7 6.8 %fusion.17 = f32[512,512]{1,0:T(8,128)S(1)} fusion(f32[512,2048]{1,0:T(8,128)S(1)} %bitcast.30, f32[2048,512]{1,0:T(8,128)S(1)} %bitcast.31), kind=kOutput, calls=%fused_computation.48 | convolution fusion | flops 6442450944 | bytes 9437184 | tf_op jit(solution)/shard_map/dot_general | solution.py:156
  60.5 6.8 %convolution_add_fusion = f32[512,512]{1,0:T(8,128)S(1)} fusion(f32[512,512]{1,0:T(8,128)S(1)} %fusion.17, f32[512,2048]{1,0:T(8,128)S(1)} %bitcast.32, f32[2048,512]{1,0:T(8,128)S(1)} %bitcast.33), kind=kOutput, calls=%fused_computation.12 | convolution fusion | flops 6442713088 | bytes 10485760 | tf_op jit(solution)/shard_map/dot_general | solution.py:159
  67.3 1.3 %reshape_reshape.6.x_ref = f32[16,16,1024]{2,1,0:T(8,128)} reshape(f32[512,512]{1,0:T(8,128)S(1)} %convolution_add_fusion) | data formatting | bytes 2097152 | tf_op jit(solution)/shard_map/reshape;reshape | solution.py:101
  68.7 33.4 %shard_map.39 = f32[16,16,1024]{2,1,0:T(8,128)} custom-call(f32[16,16,1024]{2,1,0:T(8,128)} %reshape_reshape.6.x_ref), custom_call_target="tpu_custom_call" | custom-call | tf_op jit(solution)/shard_map/pallas_call | solution.py:89
  102.1 1.3 %reduce_sum.72 = f32[16,1024]{1,0:T(8,128)S(1)} reduce(f32[16,16,1024]{2,1,0:T(8,128)} %shard_map.39, f32[]{:T(128)} %constant.76.clone.1), dimensions={0}, to_apply=%region_6.7 | reduce | flops 245760 | bytes 1114116 | tf_op jit(solution)/shard_map/reduce_sum | solution.py:114
  103.4 0.6 reshape_reshape.7.x_ref
  104.0 1.5 %shard_map.40 = bf16[32,512]{1,0:T(8,128)(2,1)} custom-call(f32[32,512]{1,0:T(8,128)} %reshape_reshape.7.x_ref), custom_call_target="tpu_custom_call" | custom-call | tf_op jit(solution)/shard_map/pallas_call | solution.py:122
  (7 shorter events, 0.4 us)

commit v3 on v2

--- a/solution.py
+++ b/solution.py
@@ -154,10 +154,10 @@
     real_rows = jnp.stack(reals, axis=1).reshape(rows, bins)
     imag_rows = jnp.stack(imags, axis=1).reshape(rows, bins)
     out = jnp.dot(
-        real_rows, cos_t, precision=lax.Precision.HIGHEST, preferred_element_type=jnp.float32
+        real_rows, cos_t, precision=lax.Precision.HIGH, preferred_element_type=jnp.float32
     )
     out = out + jnp.dot(
-        imag_rows, sin_t, precision=lax.Precision.HIGHEST, preferred_element_type=jnp.float32
+        imag_rows, sin_t, precision=lax.Precision.HIGH, preferred_element_type=jnp.float32
     )
     out = out.reshape(win_size, STEPS * per_dest * SRC * L)
     stacked = scatter_sum(out, "win")

time: 107 us -> 101 us (0.944)
  matrix products: 13.7 us -> 7.25 us
    dot_general x2, matrix products: 13.7 us -> 7.25 us  [the longest x1 3.7 us: body(): jnp.dot(real_rows, cos_t, precision=lax.Precision.HIGH, preferred_element...]
where the time goes in v3:
time: 101 us; the launch traced here: 99 us
  Pallas kernels  64 us (63%)
  other arithmetic  16.4 us (16%)
  matrix products  7.25 us (7%)
  local copies, waits for them, and re-layouts  5.85 us (6%)
  between operations  5.57 us (6%)
    pallas_call x3, Pallas kernels, exchange(): pl.pallas_call(functools.partial(exchange_kernel, axis, n, single), out_s...  62.6 us
    reduce_sum x1, other arithmetic, cross_spectra(): imag_part = jnp.sum(sr * ri - si * rr, axis=0)  6.44 us
    dot_general x1, matrix products, body(): jnp.dot(real_rows, cos_t, precision=lax.Precision.HIGH, preferred_element...  3.7 us
    dot_general x1, matrix products, body(): jnp.dot(imag_rows, sin_t, precision=lax.Precision.HIGH, preferred_element...  3.54 us

profile of v3, /device:TPU:32, one launch (start us, length us, event | category | flops | bytes accessed | tf_op | source)
XLA Modules:
  0.0 99.0 jit_solution(487883421269553214)
XLA Ops:
  0.0 0.7 convert_element_type.62
  0.7 1.4 %fusion.16 = (s32[1]{0:T(128)}, s32[1]{0:T(128)}) fusion(s32[2]{0:T(128)} %param.5), kind=kLoop, calls=%fused_computation.47 | loop fusion | bytes 16 | tf_op jit(solution)/shard_map/slice | solution.py:137
  7.5 1.5 %fusion = f32[4,32]{1,0:T(4,128)S(1)} fusion(bf16[4,32,4096]{2,1,0:T(8,128)(2,1)} %param.3), kind=kLoop, calls=%fused_computation.10 | loop fusion | flops 1572736 | bytes 1049088 | tf_op jit(solution)/shard_map/reduce_sum | solution.py:40
  9.0 0.3 fusion.14
  9.4 0.5 fusion.12
  9.9 1.5 %fusion.1 = bf16[4,32,4096]{2,1,0:T(8,128)(2,1)S(1)} fusion(bf16[4,32,4096]{2,1,0:T(8,128)(2,1)} %param.3, f32[4,32]{1,0:T(4,128)S(1)} %rsqrt_multiply_fusion), kind=kLoop, calls=%fused_computation.11 | loop fusion | flops 1572864 | bytes 2097664 | tf_op jit(solution)/shard_map/convert_element_type | solution.py:42
  11.5 1.1 %reshape.211.x_ref = bf16[16,16,1024]{2,1,0:T(8,128)(2,1)} reshape(bf16[2,4,8,4096]{3,2,1,0:T(8,128)(2,1)S(1)} %pad_maximum_fusion.2) | data formatting | bytes 1048576 | tf_op jit(solution)/shard_map/reshape | solution.py:101
  12.6 15.1 %shard_map.37 = bf16[16,16,1024]{2,1,0:T(8,128)(2,1)} custom-call(bf16[16,16,1024]{2,1,0:T(8,128)(2,1)} %reshape.211.x_ref), custom_call_target="tpu_custom_call" | custom-call | tf_op jit(solution)/shard_map/pallas_call | solution.py:89
  27.7 1.7 %reduce_sum.67 = bf16[16,1024]{1,0:T(8,128)(2,1)} reduce(bf16[16,16,1024]{2,1,0:T(8,128)(2,1)} %shard_map.37, bf16[]{:T(256)} %constant.82.clone.1), dimensions={0}, to_apply=%region_1.2 | reduce | flops 245760 | bytes 557058 | tf_op jit(solution)/shard_map/reduce_sum | solution.py:106
  29.5 14.1 %shard_map.38 = bf16[16,16,1024]{2,1,0:T(8,128)(2,1)} custom-call(bf16[1,16,1024]{2,1,0:T(8,128)(2,1)} %bitcast.38), custom_call_target="tpu_custom_call" | custom-call | tf_op jit(solution)/shard_map/pallas_call | solution.py:89
  43.6 1.1 %fusion.15 = (bf16[8,16,1024]{2,1,0:T(8,128)(2,1)S(1)}, bf16[8,16,1024]{2,1,0:T(8,128)(2,1)S(1)}) fusion(bf16[16,16,1024]{2,1,0:T(8,128)(2,1)} %shard_map.38), kind=kLoop, calls=%fused_computation.46 | loop fusion | bytes 1048576 | tf_op jit(solution)/shard_map/slice | solution.py:150
  44.6 0.2 squeeze.15
  45.1 0.2 slice_convert_fusion.1
  45.3 6.4 %subtract_reduce_fusion.1 = (f32[32,8,2048]{2,1,0:T(8,128)S(1)}, f32[32,8,2048]{2,1,0:T(8,128)S(1)}, f32[32,8,2048]{2,1,0:T(8,128)S(1)}, f32[32,8,2048]{2,1,0:T(8,128)S(1)}) fusion(f32[4,32,2048]{2,1,0:T(8,128)S(1)} %get-tuple-element.12, f32[4,8,2048]{2,1,0:T(8,128)S(1)} %get-tuple-element.29, f32[4,32,2048]{2,1,0:T(8,128)S(1)} %get-tuple-element.11, ...), kind=kLoop, calls=%fused_computation.1 | loop fusion | flops 31457280 | bytes 11534336 | tf_op jit(solution)/shard_map/reduce_sum | solution.py:52
  51.8 0.3 pad_maximum_fusion.1
  52.0 0.5 pad_maximum_fusion
  52.5 1.1 %negate_multiply_fusion = (f32[32,64,512]{2,1,0:T(8,128)S(1)}, f32[32,64,512]{2,1,0:T(8,128)S(1)}) fusion(f32[64,512]{1,0:T(8,128)S(1)} %get-tuple-element.26, f32[32,512]{1,0:T(8,128)S(1)} %get-tuple-element.24, f32[64,512]{1,0:T(8,128)S(1)} %get-tuple-element.25, f32[32,512]{1,0:T(8,128)S(1)} %get-tuple-element.23), kind=kLoop, calls=%fused_computation.6 | loop fusion | flops 9437184 | bytes 8781824 | tf_op jit(solution)/shard_map/mul | solution.py:34
  53.7 3.7 %fusion.17 = f32[512,512]{1,0:T(8,128)S(1)} fusion(f32[512,2048]{1,0:T(8,128)S(1)} %bitcast.31, f32[2048,512]{1,0:T(8,128)S(1)} %bitcast.33), kind=kOutput, calls=%fused_computation.48 | convolution fusion | flops 3221225472 | bytes 9437184 | tf_op jit(solution)/shard_map/dot_general | solution.py:156
  57.4 3.5 %convolution_add_fusion = f32[512,512]{1,0:T(8,128)S(1)} fusion(f32[512,512]{1,0:T(8,128)S(1)} %fusion.17, f32[512,2048]{1,0:T(8,128)S(1)} %bitcast.30, f32[2048,512]{1,0:T(8,128)S(1)} %bitcast.32), kind=kOutput, calls=%fused_computation.12 | convolution fusion | flops 3221487616 | bytes 10485760 | tf_op jit(solution)/shard_map/dot_general | solution.py:159
  60.9 1.3 %reshape_reshape.6.x_ref = f32[16,16,1024]{2,1,0:T(8,128)} reshape(f32[512,512]{1,0:T(8,128)S(1)} %convolution_add_fusion) | data formatting | bytes 2097152 | tf_op jit(solution)/shard_map/reshape;reshape | solution.py:101
  62.2 33.4 %shard_map.39 = f32[16,16,1024]{2,1,0:T(8,128)} custom-call(f32[16,16,1024]{2,1,0:T(8,128)} %reshape_reshape.6.x_ref), custom_call_target="tpu_custom_call" | custom-call | tf_op jit(solution)/shard_map/pallas_call | solution.py:89
  95.7 1.3 %reduce_sum.72 = f32[16,1024]{1,0:T(8,128)S(1)} reduce(f32[16,16,1024]{2,1,0:T(8,128)} %shard_map.39, f32[]{:T(128)} %constant.76.clone.1), dimensions={0}, to_apply=%region_6.7 | reduce | flops 245760 | bytes 1114116 | tf_op jit(solution)/shard_map/reduce_sum | solution.py:114
  96.9 0.6 reshape_reshape.7.x_ref
  97.6 1.5 %shard_map.40 = bf16[32,512]{1,0:T(8,128)(2,1)} custom-call(f32[32,512]{1,0:T(8,128)} %reshape_reshape.7.x_ref), custom_call_target="tpu_custom_call" | custom-call | tf_op jit(solution)/shard_map/pallas_call | solution.py:122
  (7 shorter events, 0.4 us)

commit v4 on v3

--- a/solution.py
+++ b/solution.py
@@ -53,21 +53,20 @@
     return real_part, imag_part
 
 
-def exchange_kernel(axis, n, single, x_ref, o_ref, buf, send_sem, recv_sem):
-    me = lax.axis_index(axis)
-    own = x_ref.at[0] if single else x_ref.at[me]
-    buf[me] = own[...]
+def greet(axis, n, me):
     barrier = pltpu.get_barrier_semaphore()
     for k in range(1, n):
         pl.semaphore_signal(barrier, inc=1, device_id={axis: (me + k) % n},
                             device_id_type=pl.DeviceIdType.MESH)
     pl.semaphore_wait(barrier, n - 1)
+
+
+def all_to_all(axis, n, me, rows_of, landing, send_sem, recv_sem):
     copies = []
     for k in range(1, n):
         peer = (me + k) % n
-        src = x_ref.at[0] if single else x_ref.at[peer]
         copy = pltpu.make_async_remote_copy(
-            src_ref=src, dst_ref=buf.at[me], send_sem=send_sem.at[k],
+            src_ref=rows_of(peer), dst_ref=landing.at[me], send_sem=send_sem.at[k],
             recv_sem=recv_sem.at[me], device_id={axis: peer},
             device_id_type=pl.DeviceIdType.MESH)
         copy.start()
@@ -77,24 +76,28 @@
     for k in range(1, n):
         source = (me + n - k) % n
         pltpu.make_async_remote_copy(
-            src_ref=buf.at[source], dst_ref=buf.at[source], send_sem=send_sem.at[k],
+            src_ref=landing.at[source], dst_ref=landing.at[source], send_sem=send_sem.at[k],
             recv_sem=recv_sem.at[source], device_id={axis: source},
             device_id_type=pl.DeviceIdType.MESH).wait_recv()
-    o_ref[...] = buf[...]
 
 
-def exchange(x, axis, n, cid):
-    single = x.shape[0] == 1
-    shape = (n,) + x.shape[1:]
-    return pl.pallas_call(
-        functools.partial(exchange_kernel, axis, n, single),
-        out_shape=jax.ShapeDtypeStruct(shape, x.dtype),
-        in_specs=[pl.BlockSpec(memory_space=pltpu.VMEM)],
-        out_specs=pl.BlockSpec(memory_space=pltpu.VMEM),
-        scratch_shapes=[pltpu.VMEM(shape, x.dtype), pltpu.SemaphoreType.DMA((n,)),
-                        pltpu.SemaphoreType.DMA((n,))],
-        compiler_params=pltpu.CompilerParams(collective_id=cid, has_side_effects=True),
-    )(x)
+def broadcast_kernel(axis, n, x_ref, o_ref, parts, mine, gathered, sems):
+    me = lax.axis_index(axis)
+    parts[me] = x_ref[me]
+    greet(axis, n, me)
+    all_to_all(axis, n, me, lambda peer: x_ref.at[peer], parts, sems.at[0], sems.at[1])
+    mine[...] = jnp.sum(parts[...].astype(jnp.float32), axis=0).astype(mine.dtype)
+    gathered[me] = mine[...]
+    all_to_all(axis, n, me, lambda peer: mine, gathered, sems.at[2], sems.at[3])
+    o_ref[...] = gathered[...]
+
+
+def reduce_kernel(axis, n, x_ref, o_ref, parts, sems):
+    me = lax.axis_index(axis)
+    parts[me] = x_ref[me]
+    greet(axis, n, me)
+    all_to_all(axis, n, me, lambda peer: x_ref.at[peer], parts, sems.at[0], sems.at[1])
+    o_ref[...] = jnp.sum(parts[...], axis=0).astype(o_ref.dtype)
 
 
 def chunks(value, n):
@@ -103,25 +106,31 @@
 
 def broadcast_sum(value, axis):
     n = lax.axis_size(axis)
-    mine = jnp.sum(exchange(chunks(value, n), axis, n, 0), axis=0, dtype=jnp.float32)
-    gathered = exchange(mine.astype(value.dtype)[None], axis, n, 1)
-    return gathered.reshape(value.shape)
+    x = chunks(value, n)
+    out = pl.pallas_call(
+        functools.partial(broadcast_kernel, axis, n),
+        out_shape=jax.ShapeDtypeStruct(x.shape, x.dtype),
+        in_specs=[pl.BlockSpec(memory_space=pltpu.VMEM)],
+        out_specs=pl.BlockSpec(memory_space=pltpu.VMEM),
+        scratch_shapes=[pltpu.VMEM(x.shape, x.dtype), pltpu.VMEM(x.shape[1:], x.dtype),
+                        pltpu.VMEM(x.shape, x.dtype), pltpu.SemaphoreType.DMA((4, n))],
+        compiler_params=pltpu.CompilerParams(collective_id=0, has_side_effects=True),
+    )(x)
+    return out.reshape(value.shape)
 
 
-def scatter_sum(rows, axis):
+def scatter_sum(rows, axis, dtype):
     n = rows.shape[0]
-    got = exchange(chunks(rows, n), axis, n, 2)
-    return jnp.sum(got, axis=0).reshape(rows.shape[1:])
-
-
-def cast_kernel(x_ref, o_ref):
-    o_ref[...] = x_ref[...].astype(o_ref.dtype)
-
-
-def to_bf16(x):
-    return pl.pallas_call(
-        cast_kernel, out_shape=jax.ShapeDtypeStruct(x.shape, jnp.bfloat16)
+    x = chunks(rows, n)
+    out = pl.pallas_call(
+        functools.partial(reduce_kernel, axis, n),
+        out_shape=jax.ShapeDtypeStruct(x.shape[1:], dtype),
+        in_specs=[pl.BlockSpec(memory_space=pltpu.VMEM)],
+        out_specs=pl.BlockSpec(memory_space=pltpu.VMEM),
+        scratch_shapes=[pltpu.VMEM(x.shape, x.dtype), pltpu.SemaphoreType.DMA((2, n))],
+        compiler_params=pltpu.CompilerParams(collective_id=1, has_side_effects=True),
     )(x)
+    return out.reshape(rows.shape[1:])
 
 
 def body(spectra, quality, source_block):
@@ -160,8 +169,8 @@
         imag_rows, sin_t, precision=lax.Precision.HIGH, preferred_element_type=jnp.float32
     )
     out = out.reshape(win_size, STEPS * per_dest * SRC * L)
-    stacked = scatter_sum(out, "win")
-    return to_bf16(stacked.reshape(STEPS * per_dest * SRC, L)).reshape(STEPS, per_dest, SRC, L)
+    stacked = scatter_sum(out, "win", jnp.bfloat16)
+    return stacked.reshape(STEPS, per_dest, SRC, L)
 
 
 def solution(mesh):

time: 101 us -> 91.8 us (0.909)
  Pallas kernels: 64 us -> 57.7 us
  other arithmetic: 16.4 us -> 13.3 us
    pallas_call x4 -> x2, Pallas kernels: 64 us -> 57.7 us  [the longest x1 32.9 us: scatter_sum(): pl.pallas_call(functools.partial(reduce_kernel, axis, n), out_shape=jax.S...]
    reduce_sum x2 -> x0, other arithmetic: 3.03 us -> none  [the longest x1 1.75 us: broadcast_sum(): jnp.sum(exchange(chunks(value, n), axis, n, 0), axis=0, dtype=jnp.float32)]
where the time goes in v4:
time: 91.8 us; the launch traced here: 90.4 us
  Pallas kernels  57.7 us (63%)
  other arithmetic  13.3 us (14%)
  matrix products  7.25 us (8%)
  local copies, waits for them, and re-layouts  6.61 us (7%)
  between operations  5.56 us (6%)
    pallas_call x1, Pallas kernels, scatter_sum(): pl.pallas_call(functools.partial(reduce_kernel, axis, n), out_shape=jax.S...  32.9 us
    pallas_call x1, Pallas kernels, broadcast_sum(): pl.pallas_call(functools.partial(broadcast_kernel, axis, n), out_shape=ja...  24.8 us
    reduce_sum x1, other arithmetic, cross_spectra(): imag_part = jnp.sum(sr * ri - si * rr, axis=0)  6.44 us
    dot_general x1, matrix products, body(): jnp.dot(real_rows, cos_t, precision=lax.Precision.HIGH, preferred_element...  3.7 us
    dot_general x1, matrix products, body(): jnp.dot(imag_rows, sin_t, precision=lax.Precision.HIGH, preferred_element...  3.54 us

profile of v4, /device:TPU:32, one launch (start us, length us, event | category | flops | bytes accessed | tf_op | source)
XLA Modules:
  0.0 90.4 jit_solution(14355194495495409771)
XLA Ops:
  0.0 0.7 convert_element_type.60
  0.7 1.4 %fusion.16 = (s32[1]{0:T(128)}, s32[1]{0:T(128)}) fusion(s32[2]{0:T(128)} %param.5), kind=kLoop, calls=%fused_computation.47 | loop fusion | bytes 16 | tf_op jit(solution)/shard_map/slice | solution.py:146
  7.5 1.5 %fusion = f32[4,32]{1,0:T(4,128)S(1)} fusion(bf16[4,32,4096]{2,1,0:T(8,128)(2,1)} %param.3), kind=kLoop, calls=%fused_computation.10 | loop fusion | flops 1572736 | bytes 1049088 | tf_op jit(solution)/shard_map/reduce_sum | solution.py:40
  9.0 0.3 fusion.14
  9.4 0.5 fusion.12
  9.9 1.5 %fusion.1 = bf16[4,32,4096]{2,1,0:T(8,128)(2,1)S(1)} fusion(bf16[4,32,4096]{2,1,0:T(8,128)(2,1)} %param.3, f32[4,32]{1,0:T(4,128)S(1)} %rsqrt_multiply_fusion), kind=kLoop, calls=%fused_computation.11 | loop fusion | flops 1572864 | bytes 2097664 | tf_op jit(solution)/shard_map/convert_element_type | solution.py:42
  11.4 0.1 select_bitcast_fusion.1
  11.5 0.1 pad_maximum_fusion.2
  11.5 1.1 %reshape.208.x_ref = bf16[16,16,1024]{2,1,0:T(8,128)(2,1)} reshape(bf16[2,4,8,4096]{3,2,1,0:T(8,128)(2,1)S(1)} %pad_maximum_fusion.2) | data formatting | bytes 1048576 | tf_op jit(solution)/shard_map/reshape | solution.py:104
  12.6 24.8 %shard_map.37 = bf16[16,16,1024]{2,1,0:T(8,128)(2,1)} custom-call(bf16[16,16,1024]{2,1,0:T(8,128)(2,1)} %reshape.208.x_ref), custom_call_target="tpu_custom_call" | custom-call | tf_op jit(solution)/shard_map/pallas_call | solution.py:110
  37.5 1.1 %fusion.15 = (bf16[8,16,1024]{2,1,0:T(8,128)(2,1)S(1)}, bf16[8,16,1024]{2,1,0:T(8,128)(2,1)S(1)}) fusion(bf16[16,16,1024]{2,1,0:T(8,128)(2,1)} %shard_map.37), kind=kLoop, calls=%fused_computation.46 | loop fusion | bytes 1048576 | tf_op jit(solution)/shard_map/slice | solution.py:159
  38.5 0.2 squeeze.15
  38.7 0.2 squeeze.14
  38.9 0.1 slice_convert_fusion.3
  39.0 0.2 slice_convert_fusion.1
  39.2 6.4 %subtract_reduce_fusion.1 = (f32[32,8,2048]{2,1,0:T(8,128)S(1)}, f32[32,8,2048]{2,1,0:T(8,128)S(1)}, f32[32,8,2048]{2,1,0:T(8,128)S(1)}, f32[32,8,2048]{2,1,0:T(8,128)S(1)}) fusion(f32[4,32,2048]{2,1,0:T(8,128)S(1)} %get-tuple-element.12, f32[4,8,2048]{2,1,0:T(8,128)S(1)} %get-tuple-element.29, f32[4,32,2048]{2,1,0:T(8,128)S(1)} %get-tuple-element.11, ...), kind=kLoop, calls=%fused_computation.1 | loop fusion | flops 31457280 | bytes 11534336 | tf_op jit(solution)/shard_map/reduce_sum | solution.py:52
  45.6 0.3 pad_maximum_fusion.1
  45.9 0.5 pad_maximum_fusion
  46.4 1.1 %negate_multiply_fusion = (f32[32,64,512]{2,1,0:T(8,128)S(1)}, f32[32,64,512]{2,1,0:T(8,128)S(1)}) fusion(f32[64,512]{1,0:T(8,128)S(1)} %get-tuple-element.26, f32[32,512]{1,0:T(8,128)S(1)} %get-tuple-element.24, f32[64,512]{1,0:T(8,128)S(1)} %get-tuple-element.25, f32[32,512]{1,0:T(8,128)S(1)} %get-tuple-element.23), kind=kLoop, calls=%fused_computation.6 | loop fusion | flops 9437184 | bytes 8781824 | tf_op jit(solution)/shard_map/mul | solution.py:34
  47.5 3.7 %fusion.17 = f32[512,512]{1,0:T(8,128)S(1)} fusion(f32[512,2048]{1,0:T(8,128)S(1)} %bitcast.29, f32[2048,512]{1,0:T(8,128)S(1)} %bitcast.31), kind=kOutput, calls=%fused_computation.48 | convolution fusion | flops 3221225472 | bytes 9437184 | tf_op jit(solution)/shard_map/dot_general | solution.py:165
  51.3 3.5 %convolution_add_fusion = f32[512,512]{1,0:T(8,128)S(1)} fusion(f32[512,512]{1,0:T(8,128)S(1)} %fusion.17, f32[512,2048]{1,0:T(8,128)S(1)} %bitcast.28, f32[2048,512]{1,0:T(8,128)S(1)} %bitcast.30), kind=kOutput, calls=%fused_computation.12 | convolution fusion | flops 3221487616 | bytes 10485760 | tf_op jit(solution)/shard_map/dot_general | solution.py:168
  54.8 1.3 %reshape_reshape.6.x_ref = f32[16,16,1024]{2,1,0:T(8,128)} reshape(f32[512,512]{1,0:T(8,128)S(1)} %convolution_add_fusion) | data formatting | bytes 2097152 | tf_op jit(solution)/shard_map/reshape;reshape | solution.py:104
  56.1 32.9 %shard_map.38 = bf16[16,1024]{1,0:T(8,128)(2,1)} custom-call(f32[16,16,1024]{2,1,0:T(8,128)} %reshape_reshape.6.x_ref), custom_call_target="tpu_custom_call" | custom-call | tf_op jit(solution)/shard_map/pallas_call | solution.py:125
  89.0 1.4 %reshape_reshape.7 = bf16[2,2,8,512]{3,2,1,0:T(8,128)(2,1)} reshape(bf16[16,1024]{1,0:T(8,128)(2,1)} %shard_map.38) | data formatting | bytes 65536 | tf_op jit(solution)/shard_map/reshape;reshape | solution.py:173
  (3 shorter events, 0.0 us)

commit v5 on v4

--- a/solution.py
+++ b/solution.py
@@ -140,17 +140,14 @@
     cos_t, sin_t = lag_table(bins, L, 1.0 / math.sqrt(row_width * total_windows))
     whitened = whiten(spectra, quality)
     per_group = channel_count // SRC
-    own = []
-    roots = []
-    for step in range(STEPS):
-        block_index = source_block[step]
-        offset = block_index % per_group * SRC
-        own.append(lax.dynamic_slice_in_dim(whitened, offset, SRC, 1))
-        roots.append(block_index // per_group)
     me = lax.axis_index("chan")
-    kept = jnp.stack(
-        [jnp.where(me == roots[k], own[k], jnp.zeros_like(own[k])) for k in range(STEPS)]
-    )
+    block_ids = me * per_group + lax.iota(jnp.int32, per_group)
+    chosen = block_ids[None, :] == source_block[:, None]
+    blocks = whitened.reshape(window_count, per_group, SRC, row_width)
+    kept = jnp.sum(
+        jnp.where(chosen[:, None, :, None, None], blocks[None], jnp.zeros((), blocks.dtype)),
+        axis=2, dtype=jnp.float32,
+    ).astype(jnp.bfloat16)
     sources = broadcast_sum(kept, "chan")
     win_size = lax.axis_size("win")
     per_dest = channel_count // win_size

time: 91.8 us -> 86.3 us (0.940)
  between operations: 5.56 us -> 0.15 us
  local copies, waits for them, and re-layouts: 6.61 us -> 5.22 us
  other arithmetic: 13.3 us -> 14.6 us
    broadcast_in_dim x0 -> x1, other arithmetic: none -> 1.48 us  [body(): jnp.where(chosen[:, None, :, None, None], blocks[None], jnp.zeros((), blo...]
    slice x1 -> x0, local copies, waits for them, and re-layouts: 1.39 us -> none  [body(): block_index = source_block[step]]
    convert_element_type x1, other arithmetic: 1.48 us -> 0.26 us  [whiten(): return (values * weights[:, :, None]).astype(jnp.bfloat16)]
where the time goes in v5:
time: 86.3 us; the launch traced here: 84.9 us
  Pallas kernels  57.7 us (67%)
  other arithmetic  14.6 us (17%)
  matrix products  7.25 us (8%)
  local copies, waits for them, and re-layouts  5.22 us (6%)
    pallas_call x1, Pallas kernels, scatter_sum(): pl.pallas_call(functools.partial(reduce_kernel, axis, n), out_shape=jax.S...  32.9 us
    pallas_call x1, Pallas kernels, broadcast_sum(): pl.pallas_call(functools.partial(broadcast_kernel, axis, n), out_shape=ja...  24.8 us
    reduce_sum x1, other arithmetic, cross_spectra(): imag_part = jnp.sum(sr * ri - si * rr, axis=0)  6.44 us
    dot_general x1, matrix products, body(): jnp.dot(real_rows, cos_t, precision=lax.Precision.HIGH, preferred_element...  3.7 us
    dot_general x1, matrix products, body(): jnp.dot(imag_rows, sin_t, precision=lax.Precision.HIGH, preferred_element...  3.54 us

profile of v5, /device:TPU:32, one launch (start us, length us, event | category | flops | bytes accessed | tf_op | source)
XLA Modules:
  0.0 84.9 jit_solution(1795746143005256021)
XLA Ops:
  0.0 0.7 broadcast_compare_fusion
  0.7 0.7 convert_element_type.62
  1.4 1.5 %fusion = f32[4,32]{1,0:T(4,128)S(1)} fusion(bf16[4,32,4096]{2,1,0:T(8,128)(2,1)} %param.3), kind=kLoop, calls=%fused_computation.10 | loop fusion | flops 1572736 | bytes 1049088 | tf_op jit(solution)/shard_map/reduce_sum | solution.py:40
  2.9 0.3 fusion.14
  3.3 0.5 fusion.12
  3.8 1.5 %fusion.21 = bf16[4,4,8,4096]{3,2,1,0:T(8,128)(2,1)S(1)} fusion(f32[4,32]{1,0:T(4,128)S(1)} %rsqrt_multiply_fusion, bf16[4,32,4096]{2,1,0:T(8,128)(2,1)} %param.3), kind=kLoop, calls=%fused_computation.48 | loop fusion | flops 1572864 | bytes 2097664 | tf_op jit(solution)/shard_map/jit(_where)/broadcast_in_dim | solution.py:148
  5.3 0.5 select_reduce_fusion
  5.8 1.1 %reshape.239.x_ref = bf16[16,16,1024]{2,1,0:T(8,128)(2,1)} reshape(bf16[2,4,8,4096]{3,2,1,0:T(8,128)(2,1)S(1)} %select_reduce_fusion) | data formatting | bytes 1048576 | tf_op jit(solution)/shard_map/reshape | solution.py:104
  6.9 24.8 %shard_map.37 = bf16[16,16,1024]{2,1,0:T(8,128)(2,1)} custom-call(bf16[16,16,1024]{2,1,0:T(8,128)(2,1)} %reshape.239.x_ref), custom_call_target="tpu_custom_call" | custom-call | tf_op jit(solution)/shard_map/pallas_call | solution.py:110
  31.7 1.1 %fusion.15 = (bf16[8,16,1024]{2,1,0:T(8,128)(2,1)S(1)}, bf16[8,16,1024]{2,1,0:T(8,128)(2,1)S(1)}) fusion(bf16[16,16,1024]{2,1,0:T(8,128)(2,1)} %shard_map.37), kind=kLoop, calls=%fused_computation.46 | loop fusion | bytes 1048576 | tf_op jit(solution)/shard_map/slice | solution.py:156
  32.8 0.2 squeeze.7
  32.9 0.2 squeeze.6
  33.1 0.1 slice_convert_fusion.3
  33.2 0.3 fusion.1
  33.5 0.2 slice_convert_fusion.1
  33.7 6.4 %subtract_reduce_fusion.1 = (f32[32,8,2048]{2,1,0:T(8,128)S(1)}, f32[32,8,2048]{2,1,0:T(8,128)S(1)}, f32[32,8,2048]{2,1,0:T(8,128)S(1)}, f32[32,8,2048]{2,1,0:T(8,128)S(1)}) fusion(f32[4,32,2048]{2,1,0:T(8,128)S(1)} %get-tuple-element.12, f32[4,8,2048]{2,1,0:T(8,128)S(1)} %get-tuple-element.25, f32[4,32,2048]{2,1,0:T(8,128)S(1)} %get-tuple-element.11, ...), kind=kLoop, calls=%fused_computation.1 | loop fusion | flops 31457280 | bytes 11534336 | tf_op jit(solution)/shard_map/reduce_sum | solution.py:52
  40.2 0.3 pad_maximum_fusion.1
  40.4 0.5 pad_maximum_fusion
  40.9 1.1 %negate_multiply_fusion = (f32[32,64,512]{2,1,0:T(8,128)S(1)}, f32[32,64,512]{2,1,0:T(8,128)S(1)}) fusion(f32[64,512]{1,0:T(8,128)S(1)} %get-tuple-element.24, f32[32,512]{1,0:T(8,128)S(1)} %get-tuple-element.22, f32[64,512]{1,0:T(8,128)S(1)} %get-tuple-element.23, f32[32,512]{1,0:T(8,128)S(1)} %get-tuple-element.21), kind=kLoop, calls=%fused_computation.6 | loop fusion | flops 9437184 | bytes 8781824 | tf_op jit(solution)/shard_map/mul | solution.py:34
  42.1 3.7 %fusion.16 = f32[512,512]{1,0:T(8,128)S(1)} fusion(f32[512,2048]{1,0:T(8,128)S(1)} %bitcast.25, f32[2048,512]{1,0:T(8,128)S(1)} %bitcast.27), kind=kOutput, calls=%fused_computation.47 | convolution fusion | flops 3221225472 | bytes 9437184 | tf_op jit(solution)/shard_map/dot_general | solution.py:162
  45.8 3.5 %convolution_add_fusion = f32[512,512]{1,0:T(8,128)S(1)} fusion(f32[512,512]{1,0:T(8,128)S(1)} %fusion.16, f32[512,2048]{1,0:T(8,128)S(1)} %bitcast.24, f32[2048,512]{1,0:T(8,128)S(1)} %bitcast.26), kind=kOutput, calls=%fused_computation.13 | convolution fusion | flops 3221487616 | bytes 10485760 | tf_op jit(solution)/shard_map/dot_general | solution.py:165
  49.3 1.3 %reshape_reshape.6.x_ref = f32[16,16,1024]{2,1,0:T(8,128)} reshape(f32[512,512]{1,0:T(8,128)S(1)} %convolution_add_fusion) | data formatting | bytes 2097152 | tf_op jit(solution)/shard_map/reshape;reshape | solution.py:104
  50.7 32.9 %shard_map.38 = bf16[16,1024]{1,0:T(8,128)(2,1)} custom-call(f32[16,16,1024]{2,1,0:T(8,128)} %reshape_reshape.6.x_ref), custom_call_target="tpu_custom_call" | custom-call | tf_op jit(solution)/shard_map/pallas_call | solution.py:125
  83.5 1.4 %reshape_reshape.7 = bf16[2,2,8,512]{3,2,1,0:T(8,128)(2,1)} reshape(bf16[16,1024]{1,0:T(8,128)(2,1)} %shard_map.38) | data formatting | bytes 65536 | tf_op jit(solution)/shard_map/reshape;reshape | solution.py:170
  (6 shorter events, 0.0 us)
Async XLA Ops:
  5.3 27.9 %copy-start = (bf16[4,32,4096]{2,1,0:T(8,128)(2,1)S(1)}, bf16[4,32,4096]{2,1,0:T(8,128)(2,1)}, u32[]{:S(2)}) copy-start(bf16[4,32,4096]{2,1,0:T(8,128)(2,1)} %param.3) | copy-start | bytes 3145732

commit v6 on v5

--- a/solution.py
+++ b/solution.py
@@ -83,54 +83,60 @@
 
 def broadcast_kernel(axis, n, x_ref, o_ref, parts, mine, gathered, sems):
     me = lax.axis_index(axis)
-    parts[me] = x_ref[me]
+    width = x_ref.shape[1] // n
+
+    def columns(peer):
+        return x_ref.at[:, pl.ds(pl.multiple_of(peer * width, width), width)]
+
+    parts[me] = columns(me)[...]
     greet(axis, n, me)
-    all_to_all(axis, n, me, lambda peer: x_ref.at[peer], parts, sems.at[0], sems.at[1])
+    all_to_all(axis, n, me, columns, parts, sems.at[0], sems.at[1])
     mine[...] = jnp.sum(parts[...].astype(jnp.float32), axis=0).astype(mine.dtype)
     gathered[me] = mine[...]
     all_to_all(axis, n, me, lambda peer: mine, gathered, sems.at[2], sems.at[3])
-    o_ref[...] = gathered[...]
+    for peer in range(n):
+        o_ref[:, peer * width:(peer + 1) * width] = gathered[peer]
 
 
 def reduce_kernel(axis, n, x_ref, o_ref, parts, sems):
     me = lax.axis_index(axis)
-    parts[me] = x_ref[me]
+    height = x_ref.shape[0] // n
+
+    def rows(peer):
+        return x_ref.at[pl.ds(pl.multiple_of(peer * height, height), height)]
+
+    parts[me] = rows(me)[...]
     greet(axis, n, me)
-    all_to_all(axis, n, me, lambda peer: x_ref.at[peer], parts, sems.at[0], sems.at[1])
-    o_ref[...] = jnp.sum(parts[...], axis=0).astype(o_ref.dtype)
-
-
-def chunks(value, n):
-    return value.reshape(n, 16, -1)
+    all_to_all(axis, n, me, rows, parts, sems.at[0], sems.at[1])
+    total = jnp.sum(parts[...], axis=0).reshape(o_ref.shape)
+    o_ref[...] = total.astype(o_ref.dtype)
 
 
 def broadcast_sum(value, axis):
     n = lax.axis_size(axis)
-    x = chunks(value, n)
-    out = pl.pallas_call(
+    chunk = (value.shape[0], value.shape[1] // n)
+    return pl.pallas_call(
         functools.partial(broadcast_kernel, axis, n),
-        out_shape=jax.ShapeDtypeStruct(x.shape, x.dtype),
+        out_shape=jax.ShapeDtypeStruct(value.shape, value.dtype),
         in_specs=[pl.BlockSpec(memory_space=pltpu.VMEM)],
         out_specs=pl.BlockSpec(memory_space=pltpu.VMEM),
-        scratch_shapes=[pltpu.VMEM(x.shape, x.dtype), pltpu.VMEM(x.shape[1:], x.dtype),
-                        pltpu.VMEM(x.shape, x.dtype), pltpu.SemaphoreType.DMA((4, n))],
+        scratch_shapes=[pltpu.VMEM((n,) + chunk, value.dtype), pltpu.VMEM(chunk, value.dtype),
+                        pltpu.VMEM((n,) + chunk, value.dtype), pltpu.SemaphoreType.DMA((4, n))],
         compiler_params=pltpu.CompilerParams(collective_id=0, has_side_effects=True),
-    )(x)
-    return out.reshape(value.shape)
+    )(value)
 
 
-def scatter_sum(rows, axis, dtype):
-    n = rows.shape[0]
-    x = chunks(rows, n)
-    out = pl.pallas_call(
+def scatter_sum(rows, axis, shape, dtype):
+    n = lax.axis_size(axis)
+    chunk = (rows.shape[0] // n, rows.shape[1])
+    return pl.pallas_call(
         functools.partial(reduce_kernel, axis, n),
-        out_shape=jax.ShapeDtypeStruct(x.shape[1:], dtype),
+        out_shape=jax.ShapeDtypeStruct(shape, dtype),
         in_specs=[pl.BlockSpec(memory_space=pltpu.VMEM)],
         out_specs=pl.BlockSpec(memory_space=pltpu.VMEM),
-        scratch_shapes=[pltpu.VMEM(x.shape, x.dtype), pltpu.SemaphoreType.DMA((2, n))],
+        scratch_shapes=[pltpu.VMEM((n,) + chunk, rows.dtype), pltpu.SemaphoreType.DMA((2, n))],
         compiler_params=pltpu.CompilerParams(collective_id=1, has_side_effects=True),
-    )(x)
-    return out.reshape(rows.shape[1:])
+    )(rows)
 
 
 def body(spectra, quality, source_block):
@@ -148,7 +154,9 @@
         jnp.where(chosen[:, None, :, None, None], blocks[None], jnp.zeros((), blocks.dtype)),
         axis=2, dtype=jnp.float32,
     ).astype(jnp.bfloat16)
-    sources = broadcast_sum(kept, "chan")
+    sources = broadcast_sum(
+        kept.reshape(STEPS * window_count * SRC, row_width), "chan"
+    ).reshape(STEPS, window_count, SRC, row_width)
     win_size = lax.axis_size("win")
     per_dest = channel_count // win_size
     reals, imags = [], []
@@ -165,9 +173,7 @@
     out = out + jnp.dot(
         imag_rows, sin_t, precision=lax.Precision.HIGH, preferred_element_type=jnp.float32
     )
-    out = out.reshape(win_size, STEPS * per_dest * SRC * L)
-    stacked = scatter_sum(out, "win", jnp.bfloat16)
-    return stacked.reshape(STEPS, per_dest, SRC, L)
+    return scatter_sum(out, "win", (STEPS, per_dest, SRC, L), jnp.bfloat16)
 
 
 def solution(mesh):

time: 86.3 us -> 85.2 us (0.987)
  local copies, waits for them, and re-layouts: 5.22 us -> 2.44 us
  matrix products: 7.25 us -> 8.25 us
  other arithmetic: 14.6 us -> 15.5 us
    another operation x2 -> x0, local copies, waits for them, and re-layouts: 2.72 us -> none  [the longest x1 1.39 us: body(): return stacked.reshape(STEPS, per_dest, SRC, L)]
    unnamed x2 -> x3, local copies, waits for them, and re-layouts: 0.01 us -> 1.38 us
    reshape x1 -> x0, local copies, waits for them, and re-layouts: 1.1 us -> none  [chunks(): return value.reshape(n, 16, -1)]
    slice x1 -> x0, local copies, waits for them, and re-layouts: 1.07 us -> none  [body(): real_part, imag_part = cross_spectra(sources[step], whitened)]
    dot_general x1, matrix products: 3.54 us -> 4.54 us  [body(): jnp.dot(imag_rows, sin_t, precision=lax.Precision.HIGH, preferred_element...]
where the time goes in v6:
time: 85.2 us; the launch traced here: 83.9 us
  Pallas kernels  57.7 us (68%)
  other arithmetic  15.5 us (18%)
  matrix products  8.25 us (10%)
  local copies, waits for them, and re-layouts  2.44 us (3%)
    pallas_call x1, Pallas kernels, scatter_sum(): pl.pallas_call(functools.partial(reduce_kernel, axis, n), out_shape=jax.S...  32.9 us
    pallas_call x1, Pallas kernels, broadcast_sum(): pl.pallas_call(functools.partial(broadcast_kernel, axis, n), out_shape=ja...  24.8 us
    reduce_sum x1, other arithmetic, cross_spectra(): imag_part = jnp.sum(sr * ri - si * rr, axis=0)  6.44 us
    dot_general x1, matrix products, body(): jnp.dot(imag_rows, sin_t, precision=lax.Precision.HIGH, preferred_element...  4.54 us
    dot_general x1, matrix products, body(): jnp.dot(real_rows, cos_t, precision=lax.Precision.HIGH, preferred_element...  3.7 us

profile of v6, /device:TPU:32, one launch (start us, length us, event | category | flops | bytes accessed | tf_op | source)
XLA Modules:
  0.0 83.9 jit_solution(4877980752122889670)
XLA Ops:
  0.0 0.7 broadcast_compare_fusion
  0.7 0.7 convert_element_type.62
  1.4 0.0 copy-start
  1.4 1.6 %fusion = f32[4,32]{1,0:T(4,128)S(1)} fusion(bf16[4,32,4096]{2,1,0:T(8,128)(2,1)} %param.3), kind=kLoop, calls=%fused_computation.10 | loop fusion | flops 1572736 | bytes 1049088 | tf_op jit(solution)/shard_map/reduce_sum | solution.py:40
  3.0 0.3 fusion.14
  3.4 0.5 fusion.12
  3.9 1.5 %fusion.20 = bf16[4,4,8,4096]{3,2,1,0:T(8,128)(2,1)S(1)} fusion(f32[4,32]{1,0:T(4,128)S(1)} %rsqrt_multiply_fusion, bf16[4,32,4096]{2,1,0:T(8,128)(2,1)} %param.3), kind=kLoop, calls=%fused_computation.49 | loop fusion | flops 1572864 | bytes 2097664 | tf_op jit(solution)/shard_map/jit(_where)/broadcast_in_dim | solution.py:154
  5.4 1.2 %select_reduce_fusion = bf16[2,4,8,4096]{3,2,1,0:T(8,128)(2,1)} fusion(pred[2,4]{1,0:T(4,128)(4,1)S(1)} %broadcast_compare_fusion, bf16[4,4,8,4096]{3,2,1,0:T(8,128)(2,1)S(1)} %fusion.20), kind=kLoop, calls=%fused_computation.12 | loop fusion | flops 1835008 | bytes 1572872 | tf_op jit(solution)/shard_map/reduce_sum | solution.py:153
  6.6 24.8 %shard_map.37 = bf16[64,4096]{1,0:T(8,128)(2,1)} custom-call(bf16[64,4096]{1,0:T(8,128)(2,1)} %bitcast.35), custom_call_target="tpu_custom_call" | custom-call | tf_op jit(solution)/shard_map/pallas_call | solution.py:118
  31.4 1.1 %slice_bitcast_fusion = (bf16[4,8,4096]{2,1,0:T(8,128)(2,1)S(1)}, bf16[4,8,4096]{2,1,0:T(8,128)(2,1)S(1)}) fusion(bf16[64,4096]{1,0:T(8,128)(2,1)} %shard_map.37), kind=kLoop, calls=%fused_computation.16 | loop fusion | bytes 1048576 | tf_op jit(solution)/shard_map/squeeze | solution.py:164
  32.5 0.1 slice_convert_fusion.3
  32.6 0.0 copy-done
  32.6 0.3 fusion.1
  32.8 0.2 slice_convert_fusion.1
  33.1 6.4 %subtract_reduce_fusion.1 = (f32[32,8,2048]{2,1,0:T(8,128)S(1)}, f32[32,8,2048]{2,1,0:T(8,128)S(1)}, f32[32,8,2048]{2,1,0:T(8,128)S(1)}, f32[32,8,2048]{2,1,0:T(8,128)S(1)}) fusion(f32[4,32,2048]{2,1,0:T(8,128)S(1)} %get-tuple-element.12, f32[4,8,2048]{2,1,0:T(8,128)S(1)} %get-tuple-element.25, f32[4,32,2048]{2,1,0:T(8,128)S(1)} %get-tuple-element.11, ...), kind=kLoop, calls=%fused_computation.1 | loop fusion | flops 31457280 | bytes 11534336 | tf_op jit(solution)/shard_map/reduce_sum | solution.py:52
  39.5 0.3 pad_maximum_fusion.1
  39.8 0.5 pad_maximum_fusion
  40.3 1.1 %negate_multiply_fusion = (f32[32,64,512]{2,1,0:T(8,128)S(1)}, f32[32,64,512]{2,1,0:T(8,128)S(1)}) fusion(f32[64,512]{1,0:T(8,128)S(1)} %get-tuple-element.24, f32[32,512]{1,0:T(8,128)S(1)} %get-tuple-element.22, f32[64,512]{1,0:T(8,128)S(1)} %get-tuple-element.23, f32[32,512]{1,0:T(8,128)S(1)} %get-tuple-element.21), kind=kLoop, calls=%fused_computation.6 | loop fusion | flops 9437184 | bytes 8781824 | tf_op jit(solution)/shard_map/mul | solution.py:34
  41.4 3.7 %fusion.15 = f32[512,512]{1,0:T(8,128)S(1)} fusion(f32[512,2048]{1,0:T(8,128)S(1)} %bitcast.28, f32[2048,512]{1,0:T(8,128)S(1)} %bitcast.30), kind=kOutput, calls=%fused_computation.48 | convolution fusion | flops 3221225472 | bytes 9437184 | tf_op jit(solution)/shard_map/dot_general | solution.py:170
  45.1 4.5 %convolution_add_fusion.x_ref = f32[512,512]{1,0:T(8,128)} fusion(f32[512,512]{1,0:T(8,128)S(1)} %fusion.15, f32[512,2048]{1,0:T(8,128)S(1)} %bitcast.27, f32[2048,512]{1,0:T(8,128)S(1)} %bitcast.29), kind=kOutput, calls=%fused_computation.13 | convolution fusion | flops 3221487616 | bytes 10485760 | tf_op jit(solution)/shard_map/dot_general | solution.py:173
  49.7 32.9 %shard_map.38 = bf16[2,2,8,512]{3,2,1,0:T(8,128)(2,1)} custom-call(f32[512,512]{1,0:T(8,128)} %convolution_add_fusion.x_ref), custom_call_target="tpu_custom_call" | custom-call | tf_op jit(solution)/shard_map/pallas_call | solution.py:132
  82.6 1.4 %copy.9 = bf16[2,2,8,512]{3,2,1,0:T(8,128)(2,1)} copy(bf16[2,2,8,512]{3,2,1,0:T(8,128)(2,1)} %shard_map.38) | data formatting | bytes 65536
  (4 shorter events, 0.0 us)
Async XLA Ops:
  1.4 31.2 %copy-start = (bf16[4,32,4096]{2,1,0:T(8,128)(2,1)S(1)}, bf16[4,32,4096]{2,1,0:T(8,128)(2,1)}, u32[]{:S(2)}) copy-start(bf16[4,32,4096]{2,1,0:T(8,128)(2,1)} %param.3) | copy-start | bytes 3145732

commit v7 on v1

--- a/solution.py
+++ b/solution.py
@@ -1,9 +1,11 @@
+import functools
 import math
 
 import jax
 import jax.numpy as jnp
 from jax import lax
 from jax.experimental import pallas as pl
+from jax.experimental.pallas import tpu as pltpu
 from jax.sharding import PartitionSpec as P
 
 L = 512
@@ -51,14 +53,126 @@
     return real_part, imag_part
 
 
-def cast_kernel(x_ref, o_ref):
-    o_ref[...] = x_ref[...].astype(o_ref.dtype)
-
-
-def to_bf16(x):
+def greet(groups):
+    barrier = pltpu.get_barrier_semaphore()
+    count = 0
+    for axis, n in groups:
+        me = lax.axis_index(axis)
+        for k in range(1, n):
+            pl.semaphore_signal(barrier, inc=1, device_id={axis: (me + k) % n},
+                                device_id_type=pl.DeviceIdType.MESH)
+        count += n - 1
+    pl.semaphore_wait(barrier, count)
+
+
+def start_all_to_all(axis, n, rows_of, landing, send_sem, recv_sem):
+    me = lax.axis_index(axis)
+    copies = []
+    for k in range(1, n):
+        peer = (me + k) % n
+        copy = pltpu.make_async_remote_copy(
+            src_ref=rows_of(peer), dst_ref=landing.at[me], send_sem=send_sem.at[k],
+            recv_sem=recv_sem.at[me], device_id={axis: peer},
+            device_id_type=pl.DeviceIdType.MESH)
+        copy.start()
+        copies.append(copy)
+
+    def wait():
+        for copy in copies:
+            copy.wait_send()
+        for k in range(1, n):
+            source = (me + n - k) % n
+            pltpu.make_async_remote_copy(
+                src_ref=landing.at[source], dst_ref=landing.at[source], send_sem=send_sem.at[k],
+                recv_sem=recv_sem.at[source], device_id={axis: source},
+                device_id_type=pl.DeviceIdType.MESH).wait_recv()
+
+    return wait
+
+
+def columns_of(ref, n):
+    width = ref.shape[1] // n
+    return lambda peer: ref.at[:, pl.ds(pl.multiple_of(peer * width, width), width)]
+
+
+def rows_of(ref, n):
+    height = ref.shape[0] // n
+    return lambda peer: ref.at[pl.ds(pl.multiple_of(peer * height, height), height)]
+
+
+def broadcast_phases(axis, n, x_ref, o_ref, parts, mine, gathered, sems):
+    me = lax.axis_index(axis)
+    columns = columns_of(x_ref, n)
+    parts[me] = columns(me)[...]
+    wait = start_all_to_all(axis, n, columns, parts, sems.at[0], sems.at[1])
+    yield
+    wait()
+    mine[...] = jnp.sum(parts[...].astype(jnp.float32), axis=0).astype(mine.dtype)
+    gathered[me] = mine[...]
+    wait = start_all_to_all(axis, n, lambda peer: mine, gathered, sems.at[2], sems.at[3])
+    yield
+    wait()
+    width = mine.shape[1]
+    for peer in range(n):
+        o_ref[:, peer * width:(peer + 1) * width] = gathered[peer]
+
+
+def reduce_phases(axis, n, x_ref, o_ref, parts, sems):
+    me = lax.axis_index(axis)
+    rows = rows_of(x_ref, n)
+    parts[me] = rows(me)[...]
+    wait = start_all_to_all(axis, n, rows, parts, sems.at[0], sems.at[1])
+    yield
+    wait()
+    total = jnp.sum(parts[...], axis=0).reshape(o_ref.shape)
+    o_ref[...] = total.astype(o_ref.dtype)
+
+
+def run(*phase_lists):
+    for phases in phase_lists:
+        next(phases)
+    for phases in phase_lists:
+        for _ in phases:
+            pass
+
+
+def broadcast_kernel(axis, n, x_ref, o_ref, parts, mine, gathered, sems):
+    greet([(axis, n)])
+    run(broadcast_phases(axis, n, x_ref, o_ref, parts, mine, gathered, sems))
+
+
+def reduce_kernel(axis, n, x_ref, o_ref, parts, sems):
+    greet([(axis, n)])
+    run(reduce_phases(axis, n, x_ref, o_ref, parts, sems))
+
+
+def both_kernel(red_axis, rn, bc_axis, bn, rx_ref, bx_ref, ro_ref, bo_ref, rparts, rsems,
+                bparts, bmine, bgathered, bsems):
+    greet([(red_axis, rn), (bc_axis, bn)])
+    run(reduce_phases(red_axis, rn, rx_ref, ro_ref, rparts, rsems),
+        broadcast_phases(bc_axis, bn, bx_ref, bo_ref, bparts, bmine, bgathered, bsems))
+
+
+def broadcast_scratch(value, n):
+    chunk = (value.shape[0], value.shape[1] // n)
+    return [pltpu.VMEM((n,) + chunk, value.dtype), pltpu.VMEM(chunk, value.dtype),
+            pltpu.VMEM((n,) + chunk, value.dtype), pltpu.SemaphoreType.DMA((4, n))]
+
+
+def reduce_scratch(rows, n):
+    chunk = (rows.shape[0] // n, rows.shape[1])
+    return [pltpu.VMEM((n,) + chunk, rows.dtype), pltpu.SemaphoreType.DMA((2, n))]
+
+
+def vmem_call(kernel, out_shape, scratch, cid, *args):
     return pl.pallas_call(
-        cast_kernel, out_shape=jax.ShapeDtypeStruct(x.shape, jnp.bfloat16)
-    )(x)
+        kernel,
+        out_shape=out_shape,
+        in_specs=[pl.BlockSpec(memory_space=pltpu.VMEM)] * len(args),
+        out_specs=jax.tree.map(lambda _: pl.BlockSpec(memory_space=pltpu.VMEM), out_shape),
+        scratch_shapes=scratch,
+        compiler_params=pltpu.CompilerParams(collective_id=cid, has_side_effects=True),
+    )(*args)
 
 
 def body(spectra, quality, source_block):
@@ -68,37 +182,39 @@
     cos_t, sin_t = lag_table(bins, L, 1.0 / math.sqrt(row_width * total_windows))
     whitened = whiten(spectra, quality)
     per_group = channel_count // SRC
-    own = []
-    roots = []
-    for step in range(STEPS):
-        block_index = source_block[step]
-        offset = block_index % per_group * SRC
-        own.append(lax.dynamic_slice_in_dim(whitened, offset, SRC, 1))
-        roots.append(block_index // per_group)
     me = lax.axis_index("chan")
-    kept = jnp.stack(
-        [jnp.where(me == roots[k], own[k], jnp.zeros_like(own[k])) for k in range(STEPS)]
-    )
-    sources = lax.psum(kept, "chan")
+    block_ids = me * per_group + lax.iota(jnp.int32, per_group)
+    chosen = block_ids[None, :] == source_block[:, None]
+    blocks = whitened.reshape(window_count, per_group, SRC, row_width)
+    kept = jnp.sum(
+        jnp.where(chosen[:, None, :, None, None], blocks[None], jnp.zeros((), blocks.dtype)),
+        axis=2, dtype=jnp.float32,
+    ).astype(jnp.bfloat16)
+    n = lax.axis_size("chan")
     win_size = lax.axis_size("win")
     per_dest = channel_count // win_size
-    reals, imags = [], []
-    for step in range(STEPS):
-        real_part, imag_part = cross_spectra(sources[step], whitened)
-        reals.append(real_part.reshape(win_size, per_dest, SRC, bins))
-        imags.append(imag_part.reshape(win_size, per_dest, SRC, bins))
-    rows = channel_count * SRC * STEPS
-    real_rows = jnp.stack(reals, axis=1).reshape(rows, bins)
-    imag_rows = jnp.stack(imags, axis=1).reshape(rows, bins)
-    out = jnp.dot(
-        real_rows, cos_t, precision=lax.Precision.HIGHEST, preferred_element_type=jnp.float32
-    )
-    out = out + jnp.dot(
-        imag_rows, sin_t, precision=lax.Precision.HIGHEST, preferred_element_type=jnp.float32
-    )
-    out = out.reshape(win_size, STEPS * per_dest * SRC * L)
-    stacked = lax.psum_scatter(out, "win", scatter_dimension=0, tiled=True)
-    return to_bf16(stacked.reshape(STEPS * per_dest * SRC, L)).reshape(STEPS, per_dest, SRC, L)
+    flat = kept.reshape(STEPS, window_count * SRC, row_width)
+    src_shape = jax.ShapeDtypeStruct(flat.shape[1:], flat.dtype)
+    out_shape = jax.ShapeDtypeStruct((per_dest, SRC, L), jnp.bfloat16)
+
+    def lagged(sources):
+        real_part, imag_part = cross_spectra(sources.reshape(window_count, SRC, row_width), whitened)
+        rows = channel_count * SRC
+        out = jnp.dot(real_part.reshape(rows, bins), cos_t,
+                      precision=lax.Precision.HIGH, preferred_element_type=jnp.float32)
+        return out + jnp.dot(imag_part.reshape(rows, bins), sin_t,
+                             precision=lax.Precision.HIGH, preferred_element_type=jnp.float32)
+
+    first = vmem_call(functools.partial(broadcast_kernel, "chan", n), src_shape,
+                      broadcast_scratch(flat[0], n), 0, flat[0])
+    rows0 = lagged(first)
+    red0, second = vmem_call(
+        functools.partial(both_kernel, "win", win_size, "chan", n), (out_shape, src_shape),
+        reduce_scratch(rows0, win_size) + broadcast_scratch(flat[1], n), 1, rows0, flat[1])
+    rows1 = lagged(second)
+    red1 = vmem_call(functools.partial(reduce_kernel, "win", win_size), out_shape,
+                     reduce_scratch(rows1, win_size), 2, rows1)
+    return jnp.stack([red0, red1])
 
 
 def solution(mesh):

time: 342 us -> 100 us (0.29)
  waiting for transfers between devices: 280 us -> 0 us
  Pallas kernels: 1.46 us -> 67.5 us
  between operations: 19 us -> 0.2 us
  local copies, waits for them, and re-layouts: 8.46 us -> 2.76 us
    psum x1 -> x0, waiting for transfers between devices: 141 us -> none  [body(): sources = lax.psum(kept, 'chan')]
    unnamed x3 -> x0, waiting for transfers between devices: 139 us -> none
    pallas_call x1 -> x3, Pallas kernels: 1.46 us -> 67.5 us  [vmem_call(): pl.pallas_call(kernel, out_shape=out_shape, in_specs=[pl.BlockSpec(memory...]
    dot_general x2 -> x4, matrix products: 13.7 us -> 10.3 us  [the longest x2 6.02 us: lagged(): jnp.dot(real_part.reshape(rows, bins), cos_t, precision=lax.Precision.HIG...]
  transfers between devices with their start and end apart: 2 -> 0, of which waited for: 2 -> 0; matrix products, arithmetic and copies ran while one was open for 2% -> 0% of each run, Pallas kernels for 0% -> 0%
where the time goes in v7:
time: 100 us; the launch traced here: 98.1 us
  Pallas kernels  67.5 us (68%)
  other arithmetic  17.3 us (17%)
  matrix products  10.3 us (10%)
  local copies, waits for them, and re-layouts  2.76 us (3%)
    pallas_call x3, Pallas kernels, vmem_call(): pl.pallas_call(kernel, out_shape=out_shape, in_specs=[pl.BlockSpec(memory...  67.5 us
    reduce_sum x2, other arithmetic, cross_spectra(): real_part = jnp.sum(sr * rr + si * ri, axis=0)  6.33 us
    dot_general x2, matrix products, lagged(): jnp.dot(real_part.reshape(rows, bins), cos_t, precision=lax.Precision.HIG...  6.02 us
    dot_general x2, matrix products, lagged(): jnp.dot(imag_part.reshape(rows, bins), sin_t, precision=lax.Precision.HIG...  4.31 us
    convert_element_type x2, other arithmetic, cross_spectra(): sr = sources[:, None, :, :bins].astype(jnp.float32)  2.16 us

profile of v7, /device:TPU:32, one launch (start us, length us, event | category | flops | bytes accessed | tf_op | source)
XLA Modules:
  0.0 98.1 jit_solution(6707458183670882639)
XLA Ops:
  0.0 0.8 broadcast_compare_fusion
  0.8 0.7 convert_element_type.70
  1.5 1.5 %fusion = f32[4,32]{1,0:T(4,128)S(1)} fusion(bf16[4,32,4096]{2,1,0:T(8,128)(2,1)} %param.3), kind=kLoop, calls=%fused_computation.8 | loop fusion | flops 1572736 | bytes 1049088 | tf_op jit(solution)/shard_map/reduce_sum | solution.py:40
  3.0 0.3 fusion.28
  3.4 0.5 fusion.26
  3.9 1.5 %fusion.33 = bf16[4,4,8,4096]{3,2,1,0:T(8,128)(2,1)S(1)} fusion(f32[4,32]{1,0:T(4,128)S(1)} %rsqrt_multiply_fusion, bf16[4,32,4096]{2,1,0:T(8,128)(2,1)} %param.3), kind=kLoop, calls=%fused_computation.56 | loop fusion | flops 1572864 | bytes 2097664 | tf_op jit(solution)/shard_map/jit(_where)/broadcast_in_dim | solution.py:190
  5.4 0.5 select_reduce_fusion
  5.8 0.8 slice_bitcast_fusion
  6.7 19.6 %shard_map.37 = bf16[32,4096]{1,0:T(8,128)(2,1)} custom-call(bf16[32,4096]{1,0:T(8,128)(2,1)} %get-tuple-element.16.x_ref), custom_call_target="tpu_custom_call" | custom-call | tf_op jit(solution)/shard_map/pallas_call | solution.py:168
  26.3 1.0 %slice_convert_fusion.5 = (f32[4,8,2048]{2,1,0:T(8,128)S(1)}, f32[4,8,2048]{2,1,0:T(8,128)S(1)}) fusion(bf16[4,8,4096]{2,1,0:T(8,128)(2,1)} %bitcast.36), kind=kLoop, calls=%fused_computation.34 | loop fusion | flops 131072 | bytes 786432 | tf_op jit(solution)/shard_map/convert_element_type | solution.py:47
  27.4 0.3 fusion.1
  27.6 0.2 slice_convert_fusion.1
  27.9 3.1 %add_reduce_fusion.1 = (f32[32,8,2048]{2,1,0:T(8,128)S(1)}, f32[32,8,2048]{2,1,0:T(8,128)S(1)}) fusion(f32[4,32,2048]{2,1,0:T(8,128)S(1)} %get-tuple-element.14, f32[4,8,2048]{2,1,0:T(8,128)S(1)} %get-tuple-element.22, f32[4,32,2048]{2,1,0:T(8,128)S(1)} %get-tuple-element.13, f32[4,8,2048]{2,1,0:T(8,128)S(1)} %get-tuple-element.21), kind=kLoop, calls=%fused_computation.3 | loop fusion | flops 15728640 | bytes 6815744 | tf_op jit(solution)/shard_map/reduce_sum | solution.py:51
  31.0 1.2 %subtract_multiply_fusion = (f32[32,64,512]{2,1,0:T(8,128)S(1)}, f32[32,64,512]{2,1,0:T(8,128)S(1)}) fusion(f32[64,512]{1,0:T(8,128)S(1)} %get-tuple-element.26, f32[32,512]{1,0:T(8,128)S(1)} %get-tuple-element.24, f32[64,512]{1,0:T(8,128)S(1)} %get-tuple-element.25, f32[32,512]{1,0:T(8,128)S(1)} %get-tuple-element.23), kind=kLoop, calls=%fused_computation.5 | loop fusion | flops 9437184 | bytes 8781824 | tf_op jit(solution)/shard_map/mul | solution.py:34
  32.2 1.9 %copy-done.2 = f32[32,64,512]{2,1,0:T(8,128)} copy-done((f32[32,64,512]{2,1,0:T(8,128)}, f32[32,64,512]{2,1,0:T(8,128)S(1)}, u32[]{:S(2)}) %copy-start.2) | copy-done | bytes 4194328
  34.1 2.1 %fusion.6 = f32[256,512]{1,0:T(8,128)S(1)} fusion(f32[2048,512]{1,0:T(8,128)S(1)} %bitcast.34, f32[32,8,2048]{2,1,0:T(8,128)S(1)} %get-tuple-element.12), kind=kOutput, calls=%fused_computation.14 | convolution fusion | flops 1610612736 | bytes 6815744 | tf_op jit(solution)/shard_map/dot_general | solution.py:205
  36.2 2.9 %fusion.10.rx_ref = f32[256,512]{1,0:T(8,128)} fusion(f32[256,512]{1,0:T(8,128)S(1)} %fusion.6, f32[2048,512]{1,0:T(8,128)S(1)} %bitcast.32, f32[32,8,2048]{2,1,0:T(8,128)S(1)} %get-tuple-element.11), kind=kOutput, calls=%fused_computation.19 | convolution fusion | flops 1610743808 | bytes 7340032 | tf_op jit(solution)/shard_map/dot_general | solution.py:203
  39.1 27.7 %shard_map.38 = (bf16[2,8,512]{2,1,0:T(8,128)(2,1)}, bf16[32,4096]{1,0:T(8,128)(2,1)}) custom-call(f32[256,512]{1,0:T(8,128)} %fusion.10.rx_ref, bf16[32,4096]{1,0:T(8,128)(2,1)} %get-tuple-element.15.bx_ref), custom_call_target="tpu_custom_call" | custom-call | tf_op jit(solution)/shard_map/pallas_call | solution.py:168
  66.8 1.2 %slice_convert_fusion.3 = (f32[4,8,2048]{2,1,0:T(8,128)S(1)}, f32[4,8,2048]{2,1,0:T(8,128)S(1)}) fusion(bf16[4,8,4096]{2,1,0:T(8,128)(2,1)} %bitcast.37), kind=kLoop, calls=%fused_computation.32 | loop fusion | flops 131072 | bytes 786432 | tf_op jit(solution)/shard_map/convert_element_type | solution.py:47
  68.0 3.2 %add_reduce_fusion = (f32[32,8,2048]{2,1,0:T(8,128)S(1)}, f32[32,8,2048]{2,1,0:T(8,128)S(1)}) fusion(f32[4,8,2048]{2,1,0:T(8,128)S(1)} %get-tuple-element.20, f32[4,8,2048]{2,1,0:T(8,128)S(1)} %get-tuple-element.19, f32[4,32,2048]{2,1,0:T(8,128)S(1)} %get-tuple-element.14, f32[4,32,2048]{2,1,0:T(8,128)S(1)} %get-tuple-element.13), kind=kLoop, calls=%fused_computation.1 | loop fusion | flops 15728640 | bytes 6815744 | tf_op jit(solution)/shard_map/reduce_sum | solution.py:51
  71.2 2.3 %fusion.2 = f32[256,512]{1,0:T(8,128)S(1)} fusion(f32[2048,512]{1,0:T(8,128)S(1)} %bitcast.35, f32[32,8,2048]{2,1,0:T(8,128)S(1)} %get-tuple-element.10), kind=kOutput, calls=%fused_computation.10 | convolution fusion | flops 1610612736 | bytes 6815744 | tf_op jit(solution)/shard_map/dot_general | solution.py:205
  73.5 3.1 %fusion.13.x_ref = f32[256,512]{1,0:T(8,128)} fusion(f32[256,512]{1,0:T(8,128)S(1)} %fusion.2, f32[2048,512]{1,0:T(8,128)S(1)} %bitcast.33, f32[32,8,2048]{2,1,0:T(8,128)S(1)} %get-tuple-element.9), kind=kOutput, calls=%fused_computation.20 | convolution fusion | flops 1610743808 | bytes 7340032 | tf_op jit(solution)/shard_map/dot_general | solution.py:203
  76.6 20.2 %shard_map.39 = bf16[2,8,512]{2,1,0:T(8,128)(2,1)} custom-call(f32[256,512]{1,0:T(8,128)} %fusion.13.x_ref), custom_call_target="tpu_custom_call" | custom-call | tf_op jit(solution)/shard_map/pallas_call | solution.py:168
  96.8 1.3 %pad_maximum_fusion = bf16[2,2,8,512]{3,2,1,0:T(8,128)(2,1)} fusion(bf16[1,2,8,512]{3,2,1,0:T(8,128)(2,1)} %bitcast.38, bf16[1,2,8,512]{3,2,1,0:T(8,128)(2,1)S(1)} %bitcast.39), kind=kLoop, calls=%fused_computation.48 | loop fusion | flops 16384 | bytes 65536 | tf_op jit(solution)/shard_map/stack | solution.py:217
  (15 shorter events, 0.0 us)
Async XLA Ops:
  0.0 27.3 %copy-start.4 = (bf16[4,32,4096]{2,1,0:T(8,128)(2,1)S(1)}, bf16[4,32,4096]{2,1,0:T(8,128)(2,1)}, u32[]{:S(2)}) copy-start(bf16[4,32,4096]{2,1,0:T(8,128)(2,1)} %param.3) | copy-start | bytes 3145732
  32.2 1.9 %copy-start.2 = (f32[32,64,512]{2,1,0:T(8,128)}, f32[32,64,512]{2,1,0:T(8,128)S(1)}, u32[]{:S(2)}) copy-start(f32[32,64,512]{2,1,0:T(8,128)S(1)} %get-tuple-element.18) | copy-start | bytes 12582916
  32.2 4.0 %copy-start = (f32[32,64,512]{2,1,0:T(8,128)}, f32[32,64,512]{2,1,0:T(8,128)S(1)}, u32[]{:S(2)}) copy-start(f32[32,64,512]{2,1,0:T(8,128)S(1)} %get-tuple-element.17) | copy-start | bytes 12582916
  66.8 4.4 %copy-start.3 = (f32[32,64,512]{2,1,0:T(8,128)S(1)}, f32[32,64,512]{2,1,0:T(8,128)}, u32[]{:S(2)}) copy-start(f32[32,64,512]{2,1,0:T(8,128)} %copy-done.2) | copy-start | bytes 12582916
  71.2 2.3 %copy-start.1 = (f32[32,64,512]{2,1,0:T(8,128)S(1)}, f32[32,64,512]{2,1,0:T(8,128)}, u32[]{:S(2)}) copy-start(f32[32,64,512]{2,1,0:T(8,128)} %copy-done) | copy-start | bytes 12582916
  73.5 23.3 %copy-start.5 = (bf16[2,8,512]{2,1,0:T(8,128)(2,1)S(1)}, bf16[2,8,512]{2,1,0:T(8,128)(2,1)}, u32[]{:S(2)}) copy-start(bf16[2,8,512]{2,1,0:T(8,128)(2,1)} %get-tuple-element.7) | copy-start | bytes 49156

commit v8 on v6

--- a/solution.py
+++ b/solution.py
@@ -126,6 +126,92 @@
     )(value)
 
 
+def start_all_to_all(axis, n, rows_of, landing, send_sem, recv_sem):
+    me = lax.axis_index(axis)
+    copies = []
+    for k in range(1, n):
+        peer = (me + k) % n
+        copy = pltpu.make_async_remote_copy(
+            src_ref=rows_of(peer), dst_ref=landing.at[me], send_sem=send_sem.at[k],
+            recv_sem=recv_sem.at[me], device_id={axis: peer},
+            device_id_type=pl.DeviceIdType.MESH)
+        copy.start()
+        copies.append(copy)
+
+    def wait():
+        for copy in copies:
+            copy.wait_send()
+        for k in range(1, n):
+            source = (me + n - k) % n
+            pltpu.make_async_remote_copy(
+                src_ref=landing.at[source], dst_ref=landing.at[source], send_sem=send_sem.at[k],
+                recv_sem=recv_sem.at[source], device_id={axis: source},
+                device_id_type=pl.DeviceIdType.MESH).wait_recv()
+
+    return wait
+
+
+def columns_of(ref, n):
+    width = ref.shape[1] // n
+    return lambda peer: ref.at[:, pl.ds(pl.multiple_of(peer * width, width), width)]
+
+
+def whiten_broadcast_kernel(axis, n, per_group, spec_ref, q_ref, sb_ref, o_ref, w_ref,
+                            send, parts, mine, gathered, sems):
+    me = lax.axis_index(axis)
+    windows, channels, width = spec_ref.shape
+    bins = width // 2
+    steps = sb_ref.shape[0]
+
+    def weighted(w):
+        values = spec_ref[w].astype(jnp.float32)
+        energy = jnp.sum(values * values, axis=-1, keepdims=True) / bins
+        return values * (q_ref[...] / jnp.sqrt(energy + 1e-06))
+
+    for w in range(windows):
+        block = weighted(w)
+        for k in range(steps):
+            kept = jnp.zeros((SRC, width), jnp.float32)
+            for b in range(per_group):
+                hit = me * per_group + b == sb_ref[k]
+                kept = kept + jnp.where(hit, block[b * SRC:(b + 1) * SRC], 0.0)
+            row = (k * windows + w) * SRC
+            send[row:row + SRC, :] = kept.astype(send.dtype)
+    greet(axis, n, me)
+    columns = columns_of(send, n)
+    parts[me] = columns(me)[...]
+    wait = start_all_to_all(axis, n, columns, parts, sems.at[0], sems.at[1])
+    for w in range(windows):
+        w_ref[w] = weighted(w).astype(w_ref.dtype)
+    wait()
+    mine[...] = jnp.sum(parts[...].astype(jnp.float32), axis=0).astype(mine.dtype)
+    gathered[me] = mine[...]
+    wait = start_all_to_all(axis, n, lambda peer: mine, gathered, sems.at[2], sems.at[3])
+    wait()
+    piece = mine.shape[1]
+    for peer in range(n):
+        o_ref[:, peer * piece:(peer + 1) * piece] = gathered[peer]
+
+
+def whiten_broadcast(spectra, quality, source_block, axis):
+    n = lax.axis_size(axis)
+    windows, channels, width = spectra.shape
+    rows = source_block.shape[0] * windows * SRC
+    chunk = (rows, width // n)
+    vmem = pl.BlockSpec(memory_space=pltpu.VMEM)
+    return pl.pallas_call(
+        functools.partial(whiten_broadcast_kernel, axis, n, channels // SRC),
+        out_shape=(jax.ShapeDtypeStruct((rows, width), jnp.bfloat16),
+                   jax.ShapeDtypeStruct(spectra.shape, jnp.bfloat16)),
+        in_specs=[vmem, vmem, pl.BlockSpec(memory_space=pltpu.SMEM)],
+        out_specs=(vmem, vmem),
+        scratch_shapes=[pltpu.VMEM((rows, width), jnp.bfloat16),
+                        pltpu.VMEM((n,) + chunk, jnp.bfloat16), pltpu.VMEM(chunk, jnp.bfloat16),
+                        pltpu.VMEM((n,) + chunk, jnp.bfloat16), pltpu.SemaphoreType.DMA((4, n))],
+        compiler_params=pltpu.CompilerParams(collective_id=0, has_side_effects=True),
+    )(spectra, quality.astype(jnp.float32).reshape(channels, 1), source_block)
+
+
 def scatter_sum(rows, axis, shape, dtype):
     n = lax.axis_size(axis)
     chunk = (rows.shape[0] // n, rows.shape[1])
@@ -144,19 +230,8 @@
     bins = row_width // 2
     total_windows = window_count * lax.axis_size("win")
     cos_t, sin_t = lag_table(bins, L, 1.0 / math.sqrt(row_width * total_windows))
-    whitened = whiten(spectra, quality)
-    per_group = channel_count // SRC
-    me = lax.axis_index("chan")
-    block_ids = me * per_group + lax.iota(jnp.int32, per_group)
-    chosen = block_ids[None, :] == source_block[:, None]
-    blocks = whitened.reshape(window_count, per_group, SRC, row_width)
-    kept = jnp.sum(
-        jnp.where(chosen[:, None, :, None, None], blocks[None], jnp.zeros((), blocks.dtype)),
-        axis=2, dtype=jnp.float32,
-    ).astype(jnp.bfloat16)
-    sources = broadcast_sum(
-        kept.reshape(STEPS * window_count * SRC, row_width), "chan"
-    ).reshape(STEPS, window_count, SRC, row_width)
+    sources, whitened = whiten_broadcast(spectra, quality, source_block, "chan")
+    sources = sources.reshape(STEPS, window_count, SRC, row_width)
     win_size = lax.axis_size("win")
     per_dest = channel_count // win_size
     reals, imags = [], []

time: 85.2 us -> 83.1 us (0.975)
  other arithmetic: 15.5 us -> 11.4 us
  Pallas kernels: 57.7 us -> 59.1 us
    reduce_sum x2 -> x0, other arithmetic: 2.8 us -> none  [the longest x1 1.61 us: whiten(): energy = jnp.sum(values * values, axis=-1) / bins]
    broadcast_in_dim x1 -> x0, other arithmetic: 1.48 us -> none  [body(): jnp.where(chosen[:, None, :, None, None], blocks[None], jnp.zeros((), blo...]
    pallas_call x1, Pallas kernels: 24.8 us -> 26.3 us  [whiten_broadcast(): pl.pallas_call(functools.partial(whiten_broadcast_kernel, axis, n, channe...]
    convert_element_type x1, other arithmetic: 0.24 us -> 1.43 us  [cross_spectra(): rr = receivers[:, :, None, :bins].astype(jnp.float32)]
    convert_element_type x2 -> x0, other arithmetic: 0.91 us -> none  [the longest x1 0.66 us: whiten(): weights = quality.astype(jnp.float32)[None, :] / jnp.sqrt(energy + 1e-06)]
where the time goes in v8:
time: 83.1 us; the launch traced here: 81.9 us
  Pallas kernels  59.1 us (71%)
  other arithmetic  11.4 us (14%)
  matrix products  8.24 us (10%)
  local copies, waits for them, and re-layouts  3.13 us (4%)
    pallas_call x1, Pallas kernels, scatter_sum(): pl.pallas_call(functools.partial(reduce_kernel, axis, n), out_shape=jax.S...  32.8 us
    pallas_call x1, Pallas kernels, whiten_broadcast(): pl.pallas_call(functools.partial(whiten_broadcast_kernel, axis, n, channe...  26.3 us
    reduce_sum x1, other arithmetic, cross_spectra(): imag_part = jnp.sum(sr * ri - si * rr, axis=0)  6.44 us
    dot_general x1, matrix products, body(): jnp.dot(imag_rows, sin_t, precision=lax.Precision.HIGH, preferred_element...  4.53 us
    dot_general x1, matrix products, body(): jnp.dot(real_rows, cos_t, precision=lax.Precision.HIGH, preferred_element...  3.7 us

profile of v8, /device:TPU:32, one launch (start us, length us, event | category | flops | bytes accessed | tf_op | source)
XLA Modules:
  0.0 81.9 jit_solution(17373741347488878855)
XLA Ops:
  0.0 0.7 convert_bitcast_fusion
  0.7 0.7 copy.6.q_ref
  1.4 0.3 fusion.12
  1.7 0.5 fusion.10
  2.2 26.3 %shard_map.37 = (bf16[64,4096]{1,0:T(8,128)(2,1)}, bf16[4,32,4096]{2,1,0:T(8,128)(2,1)}) custom-call(bf16[4,32,4096]{2,1,0:T(8,128)(2,1)} %spec_ref.1, f32[32,1]{1,0:T(8,128)} %copy.6.q_ref, s32[2]{0:T(128)} %sb_ref.1), custom_call_target="tpu_custom_call" | custom-call | tf_op jit(solution)/shard_map/pallas_call | solution.py:202
  28.5 1.1 %slice_bitcast_fusion = (bf16[4,8,4096]{2,1,0:T(8,128)(2,1)S(1)}, bf16[4,8,4096]{2,1,0:T(8,128)(2,1)S(1)}) fusion(bf16[64,4096]{1,0:T(8,128)(2,1)} %get-tuple-element.7), kind=kLoop, calls=%fused_computation.11 | loop fusion | bytes 1048576 | tf_op jit(solution)/shard_map/squeeze | solution.py:239
  29.6 0.1 slice_convert_fusion.3
  29.7 1.4 %slice_convert_fusion.1 = (f32[4,32,2048]{2,1,0:T(8,128)S(1)}, f32[4,32,2048]{2,1,0:T(8,128)S(1)}) fusion(bf16[4,32,4096]{2,1,0:T(8,128)(2,1)} %get-tuple-element.8), kind=kLoop, calls=%fused_computation.10 | loop fusion | flops 524288 | bytes 3145728 | tf_op jit(solution)/shard_map/convert_element_type | solution.py:49
  31.1 6.4 %subtract_reduce_fusion.1 = (f32[32,8,2048]{2,1,0:T(8,128)S(1)}, f32[32,8,2048]{2,1,0:T(8,128)S(1)}, f32[32,8,2048]{2,1,0:T(8,128)S(1)}, f32[32,8,2048]{2,1,0:T(8,128)S(1)}) fusion(f32[4,32,2048]{2,1,0:T(8,128)S(1)} %get-tuple-element.16, f32[4,8,2048]{2,1,0:T(8,128)S(1)} %get-tuple-element.29, f32[4,32,2048]{2,1,0:T(8,128)S(1)} %get-tuple-element.15, ...), kind=kLoop, calls=%fused_computation.1 | loop fusion | flops 31457280 | bytes 11534336 | tf_op jit(solution)/shard_map/reduce_sum | solution.py:52
  37.6 0.3 pad_maximum_fusion.1
  37.9 0.5 pad_maximum_fusion
  38.3 1.1 %negate_multiply_fusion = (f32[32,64,512]{2,1,0:T(8,128)S(1)}, f32[32,64,512]{2,1,0:T(8,128)S(1)}) fusion(f32[64,512]{1,0:T(8,128)S(1)} %get-tuple-element.28, f32[32,512]{1,0:T(8,128)S(1)} %get-tuple-element.26, f32[64,512]{1,0:T(8,128)S(1)} %get-tuple-element.27, f32[32,512]{1,0:T(8,128)S(1)} %get-tuple-element.25), kind=kLoop, calls=%fused_computation.6 | loop fusion | flops 9437184 | bytes 8781824 | tf_op jit(solution)/shard_map/mul | solution.py:34
  39.5 3.7 %fusion.13 = f32[512,512]{1,0:T(8,128)S(1)} fusion(f32[512,2048]{1,0:T(8,128)S(1)} %bitcast.27, f32[2048,512]{1,0:T(8,128)S(1)} %bitcast.29), kind=kOutput, calls=%fused_computation.41 | convolution fusion | flops 3221225472 | bytes 9437184 | tf_op jit(solution)/shard_map/dot_general | solution.py:245
  43.2 4.5 %convolution_add_fusion.x_ref = f32[512,512]{1,0:T(8,128)} fusion(f32[512,512]{1,0:T(8,128)S(1)} %fusion.13, f32[512,2048]{1,0:T(8,128)S(1)} %bitcast.26, f32[2048,512]{1,0:T(8,128)S(1)} %bitcast.28), kind=kOutput, calls=%fused_computation.8 | convolution fusion | flops 3221487616 | bytes 10485760 | tf_op jit(solution)/shard_map/dot_general | solution.py:248
  47.7 32.8 %shard_map.38 = bf16[2,2,8,512]{3,2,1,0:T(8,128)(2,1)} custom-call(f32[512,512]{1,0:T(8,128)} %convolution_add_fusion.x_ref), custom_call_target="tpu_custom_call" | custom-call | tf_op jit(solution)/shard_map/pallas_call | solution.py:218
  80.5 1.4 %copy.12 = bf16[2,2,8,512]{3,2,1,0:T(8,128)(2,1)} copy(bf16[2,2,8,512]{3,2,1,0:T(8,128)(2,1)} %shard_map.38) | data formatting | bytes 65536
  (2 shorter events, 0.0 us)

commit v9 on v8

--- a/solution.py
+++ b/solution.py
@@ -156,8 +156,8 @@
     return lambda peer: ref.at[:, pl.ds(pl.multiple_of(peer * width, width), width)]
 
 
-def whiten_broadcast_kernel(axis, n, per_group, spec_ref, q_ref, sb_ref, o_ref, w_ref,
-                            send, parts, mine, gathered, sems):
+def whiten_broadcast_kernel(axis, n, per_group, spec_ref, q_ref, sb_ref, sr_ref, si_ref,
+                            rr_ref, ri_ref, send, parts, mine, gathered, sems):
     me = lax.axis_index(axis)
     windows, channels, width = spec_ref.shape
     bins = width // 2
@@ -182,7 +182,9 @@
     parts[me] = columns(me)[...]
     wait = start_all_to_all(axis, n, columns, parts, sems.at[0], sems.at[1])
     for w in range(windows):
-        w_ref[w] = weighted(w).astype(w_ref.dtype)
+        rounded = weighted(w).astype(jnp.bfloat16).astype(jnp.float32)
+        rr_ref[w] = rounded[:, :bins]
+        ri_ref[w] = rounded[:, bins:]
     wait()
     mine[...] = jnp.sum(parts[...].astype(jnp.float32), axis=0).astype(mine.dtype)
     gathered[me] = mine[...]
@@ -190,7 +192,11 @@
     wait()
     piece = mine.shape[1]
     for peer in range(n):
-        o_ref[:, peer * piece:(peer + 1) * piece] = gathered[peer]
+        start = peer * piece
+        if start < bins:
+            sr_ref[:, start:start + piece] = gathered[peer].astype(jnp.float32)
+        else:
+            si_ref[:, start - bins:start - bins + piece] = gathered[peer].astype(jnp.float32)
 
 
 def whiten_broadcast(spectra, quality, source_block, axis):
@@ -201,10 +207,10 @@
     vmem = pl.BlockSpec(memory_space=pltpu.VMEM)
     return pl.pallas_call(
         functools.partial(whiten_broadcast_kernel, axis, n, channels // SRC),
-        out_shape=(jax.ShapeDtypeStruct((rows, width), jnp.bfloat16),
-                   jax.ShapeDtypeStruct(spectra.shape, jnp.bfloat16)),
+        out_shape=(jax.ShapeDtypeStruct((rows, width // 2), jnp.float32),) * 2
+        + (jax.ShapeDtypeStruct((windows, channels, width // 2), jnp.float32),) * 2,
         in_specs=[vmem, vmem, pl.BlockSpec(memory_space=pltpu.SMEM)],
-        out_specs=(vmem, vmem),
+        out_specs=(vmem,) * 4,
         scratch_shapes=[pltpu.VMEM((rows, width), jnp.bfloat16),
                         pltpu.VMEM((n,) + chunk, jnp.bfloat16), pltpu.VMEM(chunk, jnp.bfloat16),
                         pltpu.VMEM((n,) + chunk, jnp.bfloat16), pltpu.SemaphoreType.DMA((4, n))],
@@ -225,18 +231,27 @@
     )(rows)
 
 
+def cross_parts(src_re, src_im, rec_re, rec_im):
+    sr, si = src_re[:, None], src_im[:, None]
+    rr, ri = rec_re[:, :, None], rec_im[:, :, None]
+    real_part = jnp.sum(sr * rr + si * ri, axis=0)
+    imag_part = jnp.sum(sr * ri - si * rr, axis=0)
+    return real_part, imag_part
+
+
 def body(spectra, quality, source_block):
     window_count, channel_count, row_width = spectra.shape
     bins = row_width // 2
     total_windows = window_count * lax.axis_size("win")
     cos_t, sin_t = lag_table(bins, L, 1.0 / math.sqrt(row_width * total_windows))
-    sources, whitened = whiten_broadcast(spectra, quality, source_block, "chan")
-    sources = sources.reshape(STEPS, window_count, SRC, row_width)
+    src_re, src_im, rec_re, rec_im = whiten_broadcast(spectra, quality, source_block, "chan")
+    src_re = src_re.reshape(STEPS, window_count, SRC, bins)
+    src_im = src_im.reshape(STEPS, window_count, SRC, bins)
     win_size = lax.axis_size("win")
     per_dest = channel_count // win_size
     reals, imags = [], []
     for step in range(STEPS):
-        real_part, imag_part = cross_spectra(sources[step], whitened)
+        real_part, imag_part = cross_parts(src_re[step], src_im[step], rec_re, rec_im)
         reals.append(real_part.reshape(win_size, per_dest, SRC, bins))
         imags.append(imag_part.reshape(win_size, per_dest, SRC, bins))
     rows = channel_count * SRC * STEPS

time: 83.1 us -> 83.1 us (level)
    convert_element_type x2 -> x0, other arithmetic: 1.53 us -> none  [the longest x1 1.43 us: cross_spectra(): rr = receivers[:, :, None, :bins].astype(jnp.float32)]
    mul x0 -> x1, local copies, waits for them, and re-layouts: none -> 1.26 us  [cross_parts(): real_part = jnp.sum(sr * rr + si * ri, axis=0)]
    squeeze x1 -> x0, local copies, waits for them, and re-layouts: 1.07 us -> none  [body(): real_part, imag_part = cross_spectra(sources[step], whitened)]
where the time goes in v9:
time: 83.1 us; the launch traced here: 81.9 us
  Pallas kernels  59.6 us (72%)
  other arithmetic  10.8 us (13%)
  matrix products  8.08 us (10%)
  local copies, waits for them, and re-layouts  3.33 us (4%)
    pallas_call x1, Pallas kernels, scatter_sum(): pl.pallas_call(functools.partial(reduce_kernel, axis, n), out_shape=jax.S...  32.8 us
    pallas_call x1, Pallas kernels, whiten_broadcast(): pl.pallas_call(functools.partial(whiten_broadcast_kernel, axis, n, channe...  26.8 us
    reduce_sum x1, other arithmetic, cross_parts(): imag_part = jnp.sum(sr * ri - si * rr, axis=0)  7.13 us
    dot_general x1, matrix products, body(): jnp.dot(imag_rows, sin_t, precision=lax.Precision.HIGH, preferred_element...  4.54 us
    dot_general x1, matrix products, body(): jnp.dot(real_rows, cos_t, precision=lax.Precision.HIGH, preferred_element...  3.54 us

profile of v9, /device:TPU:32, one launch (start us, length us, event | category | flops | bytes accessed | tf_op | source)
XLA Modules:
  0.0 81.9 jit_solution(17780336473766699920)
XLA Ops:
  0.0 0.7 convert_bitcast_fusion
  0.7 0.7 copy.6.q_ref
  1.4 0.3 fusion.12
  1.7 0.5 fusion.10
  2.2 26.8 %shard_map.37 = (f32[64,2048]{1,0:T(8,128)}, f32[64,2048]{1,0:T(8,128)}, f32[4,32,2048]{2,1,0:T(8,128)}, f32[4,32,2048]{2,1,0:T(8,128)}) custom-call(bf16[4,32,4096]{2,1,0:T(8,128)(2,1)} %spec_ref.1, f32[32,1]{1,0:T(8,128)} %copy.6.q_ref, s32[2]{0:T(128)} %sb_ref.1), custom_call_target="tpu_custom_call" | custom-call | tf_op jit(solution)/shard_map/pallas_call | solution.py:208
  29.0 1.3 %slice_bitcast_fusion = (f32[4,8,2048]{2,1,0:T(8,128)S(1)}, f32[4,8,2048]{2,1,0:T(8,128)S(1)}, f32[4,8,2048]{2,1,0:T(8,128)S(1)}, f32[4,8,2048]{2,1,0:T(8,128)S(1)}) fusion(f32[64,2048]{1,0:T(8,128)} %get-tuple-element.11, f32[64,2048]{1,0:T(8,128)} %get-tuple-element.9), kind=kLoop, calls=%fused_computation.9 | loop fusion | bytes 2097152 | tf_op jit(solution)/shard_map/mul | solution.py:237
  30.3 7.1 %subtract_reduce_fusion.1 = (f32[32,8,2048]{2,1,0:T(8,128)S(1)}, f32[32,8,2048]{2,1,0:T(8,128)S(1)}, f32[32,8,2048]{2,1,0:T(8,128)S(1)}, f32[32,8,2048]{2,1,0:T(8,128)S(1)}) fusion(f32[4,32,2048]{2,1,0:T(8,128)} %get-tuple-element.12, f32[4,8,2048]{2,1,0:T(8,128)S(1)} %get-tuple-element.22, f32[4,32,2048]{2,1,0:T(8,128)} %get-tuple-element.10, ...), kind=kLoop, calls=%fused_computation.1 | loop fusion | flops 31457280 | bytes 11534336 | tf_op jit(solution)/shard_map/reduce_sum | solution.py:238
  37.4 0.5 pad_maximum_fusion.1
  37.9 0.5 pad_maximum_fusion
  38.4 1.2 %negate_multiply_fusion = (f32[32,64,512]{2,1,0:T(8,128)S(1)}, f32[32,64,512]{2,1,0:T(8,128)S(1)}) fusion(f32[64,512]{1,0:T(8,128)S(1)} %get-tuple-element.28, f32[32,512]{1,0:T(8,128)S(1)} %get-tuple-element.26, f32[64,512]{1,0:T(8,128)S(1)} %get-tuple-element.27, f32[32,512]{1,0:T(8,128)S(1)} %get-tuple-element.25), kind=kLoop, calls=%fused_computation.6 | loop fusion | flops 9437184 | bytes 8781824 | tf_op jit(solution)/shard_map/mul | solution.py:34
  39.6 3.5 %fusion.13 = f32[512,512]{1,0:T(8,128)S(1)} fusion(f32[512,2048]{1,0:T(8,128)S(1)} %bitcast.31, f32[2048,512]{1,0:T(8,128)S(1)} %bitcast.33), kind=kOutput, calls=%fused_computation.37 | convolution fusion | flops 3221225472 | bytes 9437184 | tf_op jit(solution)/shard_map/dot_general | solution.py:260
  43.2 4.5 %convolution_add_fusion.x_ref = f32[512,512]{1,0:T(8,128)} fusion(f32[512,512]{1,0:T(8,128)S(1)} %fusion.13, f32[512,2048]{1,0:T(8,128)S(1)} %bitcast.30, f32[2048,512]{1,0:T(8,128)S(1)} %bitcast.32), kind=kOutput, calls=%fused_computation.8 | convolution fusion | flops 3221487616 | bytes 10485760 | tf_op jit(solution)/shard_map/dot_general | solution.py:263
  47.7 32.8 %shard_map.38 = bf16[2,2,8,512]{3,2,1,0:T(8,128)(2,1)} custom-call(f32[512,512]{1,0:T(8,128)} %convolution_add_fusion.x_ref), custom_call_target="tpu_custom_call" | custom-call | tf_op jit(solution)/shard_map/pallas_call | solution.py:224
  80.5 1.4 %copy.12 = bf16[2,2,8,512]{3,2,1,0:T(8,128)(2,1)} copy(bf16[2,2,8,512]{3,2,1,0:T(8,128)(2,1)} %shard_map.38) | data formatting | bytes 65536
  (2 shorter events, 0.0 us)

commit v10 on v8

--- a/solution.py
+++ b/solution.py
@@ -163,10 +163,15 @@
     bins = width // 2
     steps = sb_ref.shape[0]
 
+    channel = lax.broadcasted_iota(jnp.int32, (channels, 1), 0)
+    quality = jnp.zeros((channels, 1), jnp.float32)
+    for c in range(channels):
+        quality = jnp.where(channel == c, q_ref[c].astype(jnp.float32), quality)
+
     def weighted(w):
         values = spec_ref[w].astype(jnp.float32)
         energy = jnp.sum(values * values, axis=-1, keepdims=True) / bins
-        return values * (q_ref[...] / jnp.sqrt(energy + 1e-06))
+        return values * (quality / jnp.sqrt(energy + 1e-06))
 
     for w in range(windows):
         block = weighted(w)
@@ -203,13 +208,13 @@
         functools.partial(whiten_broadcast_kernel, axis, n, channels // SRC),
         out_shape=(jax.ShapeDtypeStruct((rows, width), jnp.bfloat16),
                    jax.ShapeDtypeStruct(spectra.shape, jnp.bfloat16)),
-        in_specs=[vmem, vmem, pl.BlockSpec(memory_space=pltpu.SMEM)],
+        in_specs=[vmem, pl.BlockSpec(memory_space=pltpu.SMEM), pl.BlockSpec(memory_space=pltpu.SMEM)],
         out_specs=(vmem, vmem),
         scratch_shapes=[pltpu.VMEM((rows, width), jnp.bfloat16),
                         pltpu.VMEM((n,) + chunk, jnp.bfloat16), pltpu.VMEM(chunk, jnp.bfloat16),
                         pltpu.VMEM((n,) + chunk, jnp.bfloat16), pltpu.SemaphoreType.DMA((4, n))],
         compiler_params=pltpu.CompilerParams(collective_id=0, has_side_effects=True),
-    )(spectra, quality.astype(jnp.float32).reshape(channels, 1), source_block)
+    )(spectra, quality, source_block)
 
 
 def scatter_sum(rows, axis, shape, dtype):

time: 83.1 us -> 81.7 us (0.983)
  no operation moved by 1% of the time
where the time goes in v10:
time: 81.7 us; the launch traced here: 80.5 us
  Pallas kernels  59 us (72%)
  other arithmetic  10.7 us (13%)
  matrix products  8.25 us (10%)
  local copies, waits for them, and re-layouts  2.44 us (3%)
    pallas_call x1, Pallas kernels, scatter_sum(): pl.pallas_call(functools.partial(reduce_kernel, axis, n), out_shape=jax.S...  32.8 us
    pallas_call x1, Pallas kernels, whiten_broadcast(): pl.pallas_call(functools.partial(whiten_broadcast_kernel, axis, n, channe...  26.2 us
    reduce_sum x1, other arithmetic, cross_spectra(): imag_part = jnp.sum(sr * ri - si * rr, axis=0)  6.44 us
    dot_general x1, matrix products, body(): jnp.dot(imag_rows, sin_t, precision=lax.Precision.HIGH, preferred_element...  4.54 us
    dot_general x1, matrix products, body(): jnp.dot(real_rows, cos_t, precision=lax.Precision.HIGH, preferred_element...  3.7 us

profile of v10, /device:TPU:32, one launch (start us, length us, event | category | flops | bytes accessed | tf_op | source)
XLA Modules:
  0.0 80.5 jit_solution(14565723774962679392)
XLA Ops:
  0.0 0.3 fusion.12
  0.4 0.5 fusion.10
  0.9 26.2 %shard_map.37 = (bf16[64,4096]{1,0:T(8,128)(2,1)}, bf16[4,32,4096]{2,1,0:T(8,128)(2,1)}) custom-call(bf16[4,32,4096]{2,1,0:T(8,128)(2,1)} %spec_ref.1, s32[32]{0:T(128)} %q_ref.1, s32[2]{0:T(128)} %sb_ref.1), custom_call_target="tpu_custom_call" | custom-call | tf_op jit(solution)/shard_map/pallas_call | solution.py:207
  27.1 1.1 %slice_bitcast_fusion = (bf16[4,8,4096]{2,1,0:T(8,128)(2,1)S(1)}, bf16[4,8,4096]{2,1,0:T(8,128)(2,1)S(1)}) fusion(bf16[64,4096]{1,0:T(8,128)(2,1)} %get-tuple-element.7), kind=kLoop, calls=%fused_computation.11 | loop fusion | bytes 1048576 | tf_op jit(solution)/shard_map/squeeze | solution.py:244
  28.2 0.1 slice_convert_fusion.3
  28.3 1.4 %slice_convert_fusion.1 = (f32[4,32,2048]{2,1,0:T(8,128)S(1)}, f32[4,32,2048]{2,1,0:T(8,128)S(1)}) fusion(bf16[4,32,4096]{2,1,0:T(8,128)(2,1)} %get-tuple-element.8), kind=kLoop, calls=%fused_computation.10 | loop fusion | flops 524288 | bytes 3145728 | tf_op jit(solution)/shard_map/convert_element_type | solution.py:49
  29.7 6.4 %subtract_reduce_fusion.1 = (f32[32,8,2048]{2,1,0:T(8,128)S(1)}, f32[32,8,2048]{2,1,0:T(8,128)S(1)}, f32[32,8,2048]{2,1,0:T(8,128)S(1)}, f32[32,8,2048]{2,1,0:T(8,128)S(1)}) fusion(f32[4,32,2048]{2,1,0:T(8,128)S(1)} %get-tuple-element.16, f32[4,8,2048]{2,1,0:T(8,128)S(1)} %get-tuple-element.29, f32[4,32,2048]{2,1,0:T(8,128)S(1)} %get-tuple-element.15, ...), kind=kLoop, calls=%fused_computation.1 | loop fusion | flops 31457280 | bytes 11534336 | tf_op jit(solution)/shard_map/reduce_sum | solution.py:52
  36.2 0.3 pad_maximum_fusion.1
  36.5 0.5 pad_maximum_fusion
  37.0 1.1 %negate_multiply_fusion = (f32[32,64,512]{2,1,0:T(8,128)S(1)}, f32[32,64,512]{2,1,0:T(8,128)S(1)}) fusion(f32[64,512]{1,0:T(8,128)S(1)} %get-tuple-element.28, f32[32,512]{1,0:T(8,128)S(1)} %get-tuple-element.26, f32[64,512]{1,0:T(8,128)S(1)} %get-tuple-element.27, f32[32,512]{1,0:T(8,128)S(1)} %get-tuple-element.25), kind=kLoop, calls=%fused_computation.6 | loop fusion | flops 9437184 | bytes 8781824 | tf_op jit(solution)/shard_map/mul | solution.py:34
  38.1 3.7 %fusion.13 = f32[512,512]{1,0:T(8,128)S(1)} fusion(f32[512,2048]{1,0:T(8,128)S(1)} %bitcast.25, f32[2048,512]{1,0:T(8,128)S(1)} %bitcast.27), kind=kOutput, calls=%fused_computation.40 | convolution fusion | flops 3221225472 | bytes 9437184 | tf_op jit(solution)/shard_map/dot_general | solution.py:250
  41.8 4.5 %convolution_add_fusion.x_ref = f32[512,512]{1,0:T(8,128)} fusion(f32[512,512]{1,0:T(8,128)S(1)} %fusion.13, f32[512,2048]{1,0:T(8,128)S(1)} %bitcast.24, f32[2048,512]{1,0:T(8,128)S(1)} %bitcast.26), kind=kOutput, calls=%fused_computation.8 | convolution fusion | flops 3221487616 | bytes 10485760 | tf_op jit(solution)/shard_map/dot_general | solution.py:253
  46.3 32.8 %shard_map.38 = bf16[2,2,8,512]{3,2,1,0:T(8,128)(2,1)} custom-call(f32[512,512]{1,0:T(8,128)} %convolution_add_fusion.x_ref), custom_call_target="tpu_custom_call" | custom-call | tf_op jit(solution)/shard_map/pallas_call | solution.py:223
  79.2 1.4 %copy.9 = bf16[2,2,8,512]{3,2,1,0:T(8,128)(2,1)} copy(bf16[2,2,8,512]{3,2,1,0:T(8,128)(2,1)} %shard_map.38) | data formatting | bytes 65536
  (2 shorter events, 0.0 us)

commit v11 on v10

--- a/solution.py
+++ b/solution.py
@@ -156,8 +156,8 @@
     return lambda peer: ref.at[:, pl.ds(pl.multiple_of(peer * width, width), width)]
 
 
-def whiten_broadcast_kernel(axis, n, per_group, spec_ref, q_ref, sb_ref, o_ref, w_ref,
-                            send, parts, mine, gathered, sems):
+def whiten_broadcast_kernel(axis, n, per_group, factor, spec_ref, q_ref, sb_ref, o_ref, w_ref,
+                            cos_ref, sin_ref, send, parts, mine, gathered, sems):
     me = lax.axis_index(axis)
     windows, channels, width = spec_ref.shape
     bins = width // 2
@@ -192,24 +192,28 @@
     mine[...] = jnp.sum(parts[...].astype(jnp.float32), axis=0).astype(mine.dtype)
     gathered[me] = mine[...]
     wait = start_all_to_all(axis, n, lambda peer: mine, gathered, sems.at[2], sems.at[3])
+    cos_t, sin_t = lag_table(bins, L, factor)
+    cos_ref[...] = cos_t
+    sin_ref[...] = sin_t
     wait()
     piece = mine.shape[1]
     for peer in range(n):
         o_ref[:, peer * piece:(peer + 1) * piece] = gathered[peer]
 
 
-def whiten_broadcast(spectra, quality, source_block, axis):
+def whiten_broadcast(spectra, quality, source_block, axis, factor):
     n = lax.axis_size(axis)
     windows, channels, width = spectra.shape
     rows = source_block.shape[0] * windows * SRC
     chunk = (rows, width // n)
     vmem = pl.BlockSpec(memory_space=pltpu.VMEM)
     return pl.pallas_call(
-        functools.partial(whiten_broadcast_kernel, axis, n, channels // SRC),
+        functools.partial(whiten_broadcast_kernel, axis, n, channels // SRC, factor),
         out_shape=(jax.ShapeDtypeStruct((rows, width), jnp.bfloat16),
-                   jax.ShapeDtypeStruct(spectra.shape, jnp.bfloat16)),
+                   jax.ShapeDtypeStruct(spectra.shape, jnp.bfloat16))
+        + (jax.ShapeDtypeStruct((width // 2, L), jnp.float32),) * 2,
         in_specs=[vmem, pl.BlockSpec(memory_space=pltpu.SMEM), pl.BlockSpec(memory_space=pltpu.SMEM)],
-        out_specs=(vmem, vmem),
+        out_specs=(vmem,) * 4,
         scratch_shapes=[pltpu.VMEM((rows, width), jnp.bfloat16),
                         pltpu.VMEM((n,) + chunk, jnp.bfloat16), pltpu.VMEM(chunk, jnp.bfloat16),
                         pltpu.VMEM((n,) + chunk, jnp.bfloat16), pltpu.SemaphoreType.DMA((4, n))],
@@ -234,8 +238,8 @@
     window_count, channel_count, row_width = spectra.shape
     bins = row_width // 2
     total_windows = window_count * lax.axis_size("win")
-    cos_t, sin_t = lag_table(bins, L, 1.0 / math.sqrt(row_width * total_windows))
-    sources, whitened = whiten_broadcast(spectra, quality, source_block, "chan")
+    sources, whitened, cos_t, sin_t = whiten_broadcast(
+        spectra, quality, source_block, "chan", 1.0 / math.sqrt(row_width * total_windows))
     sources = sources.reshape(STEPS, window_count, SRC, row_width)
     win_size = lax.axis_size("win")
     per_dest = channel_count // win_size

time: 81.7 us -> 83.6 us (1.023)
  Pallas kernels: 59 us -> 61.4 us
  other arithmetic: 10.7 us -> 8.63 us
  local copies, waits for them, and re-layouts: 2.44 us -> 4.14 us
    pallas_call x1, Pallas kernels: 26.2 us -> 28.6 us  [whiten_broadcast(): pl.pallas_call(functools.partial(whiten_broadcast_kernel, axis, n, channe...]
    unnamed x1 -> x5, local copies, waits for them, and re-layouts: 1.38 us -> 3.07 us
    mul x2 -> x0, other arithmetic: 1.12 us -> none  [the longest x1 1.12 us: lag_table(): return (cos_t * factor, -sin_t * factor)]
    cos x2 -> x0, other arithmetic: 0.87 us -> none  [the longest x1 0.53 us: lag_table(): jnp.cos(angle_lo)[None, :, :]]
where the time goes in v11:
time: 83.6 us; the launch traced here: 82.4 us
  Pallas kernels  61.4 us (73%)
  other arithmetic  8.63 us (10%)
  matrix products  8.08 us (10%)
  local copies, waits for them, and re-layouts  4.14 us (5%)
    pallas_call x1, Pallas kernels, scatter_sum(): pl.pallas_call(functools.partial(reduce_kernel, axis, n), out_shape=jax.S...  32.8 us
    pallas_call x1, Pallas kernels, whiten_broadcast(): pl.pallas_call(functools.partial(whiten_broadcast_kernel, axis, n, channe...  28.6 us
    reduce_sum x1, other arithmetic, cross_spectra(): imag_part = jnp.sum(sr * ri - si * rr, axis=0)  6.21 us
    dot_general x1, matrix products, body(): jnp.dot(imag_rows, sin_t, precision=lax.Precision.HIGH, preferred_element...  4.54 us
    dot_general x1, matrix products, body(): jnp.dot(real_rows, cos_t, precision=lax.Precision.HIGH, preferred_element...  3.54 us
    unnamed x5, local copies, waits for them, and re-layouts  3.07 us

profile of v11, /device:TPU:32, one launch (start us, length us, event | category | flops | bytes accessed | tf_op | source)
XLA Modules:
  0.0 82.4 jit_solution(17795563280131803573)
XLA Ops:
  0.0 28.6 %shard_map.37 = (bf16[64,4096]{1,0:T(8,128)(2,1)}, bf16[4,32,4096]{2,1,0:T(8,128)(2,1)}, f32[2048,512]{1,0:T(8,128)}, f32[2048,512]{1,0:T(8,128)}) custom-call(bf16[4,32,4096]{2,1,0:T(8,128)(2,1)} %spec_ref.1, s32[32]{0:T(128)} %q_ref.1, s32[2]{0:T(128)} %sb_ref.1), custom_call_target="tpu_custom_call" | custom-call | tf_op jit(solution)/shard_map/pallas_call | solution.py:210
  28.6 1.1 %slice_bitcast_fusion = (bf16[4,8,4096]{2,1,0:T(8,128)(2,1)S(1)}, bf16[4,8,4096]{2,1,0:T(8,128)(2,1)S(1)}) fusion(bf16[64,4096]{1,0:T(8,128)(2,1)} %get-tuple-element.9), kind=kLoop, calls=%fused_computation.9 | loop fusion | bytes 1048576 | tf_op jit(solution)/shard_map/squeeze | solution.py:248
  29.7 0.1 slice_convert_fusion.3
  29.8 1.4 %slice_convert_fusion.1 = (f32[4,32,2048]{2,1,0:T(8,128)S(1)}, f32[4,32,2048]{2,1,0:T(8,128)S(1)}) fusion(bf16[4,32,4096]{2,1,0:T(8,128)(2,1)} %get-tuple-element.10), kind=kLoop, calls=%fused_computation.8 | loop fusion | flops 524288 | bytes 3145728 | tf_op jit(solution)/shard_map/convert_element_type | solution.py:49
  31.2 6.2 %subtract_reduce_fusion.1 = (f32[32,8,2048]{2,1,0:T(8,128)S(1)}, f32[32,8,2048]{2,1,0:T(8,128)S(1)}, f32[32,8,2048]{2,1,0:T(8,128)S(1)}, f32[32,8,2048]{2,1,0:T(8,128)S(1)}) fusion(f32[4,32,2048]{2,1,0:T(8,128)S(1)} %get-tuple-element.20, f32[4,8,2048]{2,1,0:T(8,128)S(1)} %get-tuple-element.27, f32[4,32,2048]{2,1,0:T(8,128)S(1)} %get-tuple-element.19, ...), kind=kLoop, calls=%fused_computation.1 | loop fusion | flops 31457280 | bytes 11534336 | tf_op jit(solution)/shard_map/reduce_sum | solution.py:52
  37.4 0.5 pad_maximum_fusion.1
  37.9 0.0 copy-start.1
  37.9 0.5 pad_maximum_fusion
  38.4 1.7 %copy-done.1 = f32[2048,512]{1,0:T(8,128)S(1)} copy-done((f32[2048,512]{1,0:T(8,128)S(1)}, f32[2048,512]{1,0:T(8,128)}, u32[]{:S(2)}) %copy-start.1) | copy-done | bytes 4194328
  40.1 0.0 copy-start
  40.1 3.5 %fusion = f32[512,512]{1,0:T(8,128)S(1)} fusion(f32[512,2048]{1,0:T(8,128)S(1)} %bitcast.23, f32[2048,512]{1,0:T(8,128)S(1)} %copy-done.1), kind=kOutput, calls=%fused_computation.15 | convolution fusion | flops 3221225472 | bytes 9437184 | tf_op jit(solution)/shard_map/dot_general | solution.py:254
  43.6 0.0 copy-done
  43.6 4.5 %convolution_add_fusion.x_ref = f32[512,512]{1,0:T(8,128)} fusion(f32[512,512]{1,0:T(8,128)S(1)} %fusion, f32[512,2048]{1,0:T(8,128)S(1)} %bitcast.22, f32[2048,512]{1,0:T(8,128)S(1)} %copy-done), kind=kOutput, calls=%fused_computation.6 | convolution fusion | flops 3221487616 | bytes 10485760 | tf_op jit(solution)/shard_map/dot_general | solution.py:257
  48.2 32.8 %shard_map.38 = bf16[2,2,8,512]{3,2,1,0:T(8,128)(2,1)} custom-call(f32[512,512]{1,0:T(8,128)} %convolution_add_fusion.x_ref), custom_call_target="tpu_custom_call" | custom-call | tf_op jit(solution)/shard_map/pallas_call | solution.py:227
  81.0 1.4 %copy.9 = bf16[2,2,8,512]{3,2,1,0:T(8,128)(2,1)} copy(bf16[2,2,8,512]{3,2,1,0:T(8,128)(2,1)} %shard_map.38) | data formatting | bytes 65536
Async XLA Ops:
  37.9 2.2 %copy-start.1 = (f32[2048,512]{1,0:T(8,128)S(1)}, f32[2048,512]{1,0:T(8,128)}, u32[]{:S(2)}) copy-start(f32[2048,512]{1,0:T(8,128)} %get-tuple-element.11) | copy-start | bytes 12582916
  40.1 3.6 %copy-start = (f32[2048,512]{1,0:T(8,128)S(1)}, f32[2048,512]{1,0:T(8,128)}, u32[]{:S(2)}) copy-start(f32[2048,512]{1,0:T(8,128)} %get-tuple-element.12) | copy-start | bytes 12582916

commit v12 on v10

--- a/solution.py
+++ b/solution.py
@@ -98,16 +98,18 @@
         o_ref[:, peer * width:(peer + 1) * width] = gathered[peer]
 
 
-def reduce_kernel(axis, n, x_ref, o_ref, parts, sems):
+def reduce_kernel(axis, n, x_ref, o_ref, parts, sems, own_sem):
     me = lax.axis_index(axis)
     height = x_ref.shape[0] // n
 
     def rows(peer):
         return x_ref.at[pl.ds(pl.multiple_of(peer * height, height), height)]
 
-    parts[me] = rows(me)[...]
+    own = pltpu.make_async_copy(rows(me), parts.at[me], own_sem.at[0])
+    own.start()
     greet(axis, n, me)
     all_to_all(axis, n, me, rows, parts, sems.at[0], sems.at[1])
+    own.wait()
     total = jnp.sum(parts[...], axis=0).reshape(o_ref.shape)
     o_ref[...] = total.astype(o_ref.dtype)
 
@@ -223,9 +225,10 @@
     return pl.pallas_call(
         functools.partial(reduce_kernel, axis, n),
         out_shape=jax.ShapeDtypeStruct(shape, dtype),
-        in_specs=[pl.BlockSpec(memory_space=pltpu.VMEM)],
+        in_specs=[pl.BlockSpec(memory_space=pl.ANY)],
         out_specs=pl.BlockSpec(memory_space=pltpu.VMEM),
-        scratch_shapes=[pltpu.VMEM((n,) + chunk, rows.dtype), pltpu.SemaphoreType.DMA((2, n))],
+        scratch_shapes=[pltpu.VMEM((n,) + chunk, rows.dtype), pltpu.SemaphoreType.DMA((2, n)),
+                        pltpu.SemaphoreType.DMA((1,))],
         compiler_params=pltpu.CompilerParams(collective_id=1, has_side_effects=True),
     )(rows)
 

time: 81.7 us -> 80.7 us (0.988)
  Pallas kernels: 59 us -> 58 us
    pallas_call x1, Pallas kernels: 32.8 us -> 31.8 us  [scatter_sum(): pl.pallas_call(functools.partial(reduce_kernel, axis, n), out_shape=jax.S...]
where the time goes in v12:
time: 80.7 us; the launch traced here: 79.5 us
  Pallas kernels  58 us (72%)
  other arithmetic  10.7 us (13%)
  matrix products  8.25 us (10%)
  local copies, waits for them, and re-layouts  2.44 us (3%)
    pallas_call x1, Pallas kernels, scatter_sum(): pl.pallas_call(functools.partial(reduce_kernel, axis, n), out_shape=jax.S...  31.8 us
    pallas_call x1, Pallas kernels, whiten_broadcast(): pl.pallas_call(functools.partial(whiten_broadcast_kernel, axis, n, channe...  26.2 us
    reduce_sum x1, other arithmetic, cross_spectra(): imag_part = jnp.sum(sr * ri - si * rr, axis=0)  6.44 us
    dot_general x1, matrix products, body(): jnp.dot(imag_rows, sin_t, precision=lax.Precision.HIGH, preferred_element...  4.54 us
    dot_general x1, matrix products, body(): jnp.dot(real_rows, cos_t, precision=lax.Precision.HIGH, preferred_element...  3.7 us

profile of v12, /device:TPU:32, one launch (start us, length us, event | category | flops | bytes accessed | tf_op | source)
XLA Modules:
  0.0 79.5 jit_solution(3016485264362501450)
XLA Ops:
  0.0 0.3 fusion.12
  0.4 0.5 fusion.10
  0.9 26.2 %shard_map.37 = (bf16[64,4096]{1,0:T(8,128)(2,1)}, bf16[4,32,4096]{2,1,0:T(8,128)(2,1)}) custom-call(bf16[4,32,4096]{2,1,0:T(8,128)(2,1)} %spec_ref.1, s32[32]{0:T(128)} %q_ref.1, s32[2]{0:T(128)} %sb_ref.1), custom_call_target="tpu_custom_call" | custom-call | tf_op jit(solution)/shard_map/pallas_call | solution.py:209
  27.1 1.1 %slice_bitcast_fusion = (bf16[4,8,4096]{2,1,0:T(8,128)(2,1)S(1)}, bf16[4,8,4096]{2,1,0:T(8,128)(2,1)S(1)}) fusion(bf16[64,4096]{1,0:T(8,128)(2,1)} %get-tuple-element.7), kind=kLoop, calls=%fused_computation.11 | loop fusion | bytes 1048576 | tf_op jit(solution)/shard_map/squeeze | solution.py:247
  28.2 0.1 slice_convert_fusion.3
  28.3 1.4 %slice_convert_fusion.1 = (f32[4,32,2048]{2,1,0:T(8,128)S(1)}, f32[4,32,2048]{2,1,0:T(8,128)S(1)}) fusion(bf16[4,32,4096]{2,1,0:T(8,128)(2,1)} %get-tuple-element.8), kind=kLoop, calls=%fused_computation.10 | loop fusion | flops 524288 | bytes 3145728 | tf_op jit(solution)/shard_map/convert_element_type | solution.py:49
  29.7 6.4 %subtract_reduce_fusion.1 = (f32[32,8,2048]{2,1,0:T(8,128)S(1)}, f32[32,8,2048]{2,1,0:T(8,128)S(1)}, f32[32,8,2048]{2,1,0:T(8,128)S(1)}, f32[32,8,2048]{2,1,0:T(8,128)S(1)}) fusion(f32[4,32,2048]{2,1,0:T(8,128)S(1)} %get-tuple-element.16, f32[4,8,2048]{2,1,0:T(8,128)S(1)} %get-tuple-element.29, f32[4,32,2048]{2,1,0:T(8,128)S(1)} %get-tuple-element.15, ...), kind=kLoop, calls=%fused_computation.1 | loop fusion | flops 31457280 | bytes 11534336 | tf_op jit(solution)/shard_map/reduce_sum | solution.py:52
  36.2 0.3 pad_maximum_fusion.1
  36.5 0.5 pad_maximum_fusion
  37.0 1.1 %negate_multiply_fusion = (f32[32,64,512]{2,1,0:T(8,128)S(1)}, f32[32,64,512]{2,1,0:T(8,128)S(1)}) fusion(f32[64,512]{1,0:T(8,128)S(1)} %get-tuple-element.28, f32[32,512]{1,0:T(8,128)S(1)} %get-tuple-element.26, f32[64,512]{1,0:T(8,128)S(1)} %get-tuple-element.27, f32[32,512]{1,0:T(8,128)S(1)} %get-tuple-element.25), kind=kLoop, calls=%fused_computation.6 | loop fusion | flops 9437184 | bytes 8781824 | tf_op jit(solution)/shard_map/mul | solution.py:34
  38.1 3.7 %fusion.13 = f32[512,512]{1,0:T(8,128)S(1)} fusion(f32[512,2048]{1,0:T(8,128)S(1)} %bitcast.25, f32[2048,512]{1,0:T(8,128)S(1)} %bitcast.27), kind=kOutput, calls=%fused_computation.40 | convolution fusion | flops 3221225472 | bytes 9437184 | tf_op jit(solution)/shard_map/dot_general | solution.py:253
  41.8 4.5 %convolution_add_fusion.x_ref = f32[512,512]{1,0:T(8,128)} fusion(f32[512,512]{1,0:T(8,128)S(1)} %fusion.13, f32[512,2048]{1,0:T(8,128)S(1)} %bitcast.24, f32[2048,512]{1,0:T(8,128)S(1)} %bitcast.26), kind=kOutput, calls=%fused_computation.8 | convolution fusion | flops 3221487616 | bytes 10485760 | tf_op jit(solution)/shard_map/dot_general | solution.py:256
  46.3 31.8 %shard_map.38 = bf16[2,2,8,512]{3,2,1,0:T(8,128)(2,1)} custom-call(f32[512,512]{1,0:T(8,128)} %convolution_add_fusion.x_ref), custom_call_target="tpu_custom_call" | custom-call | tf_op jit(solution)/shard_map/pallas_call | solution.py:225
  78.1 1.4 %copy.9 = bf16[2,2,8,512]{3,2,1,0:T(8,128)(2,1)} copy(bf16[2,2,8,512]{3,2,1,0:T(8,128)(2,1)} %shard_map.38) | data formatting | bytes 65536
  (2 shorter events, 0.0 us)

commit v13 on v12

--- a/solution.py
+++ b/solution.py
@@ -53,6 +53,13 @@
     return real_part, imag_part
 
 
+def shifts(n):
+    order = []
+    for k in range(1, n // 2 + 1):
+        order += [k] if k == n - k else [k, n - k]
+    return order
+
+
 def greet(axis, n, me):
     barrier = pltpu.get_barrier_semaphore()
     for k in range(1, n):
@@ -63,7 +70,7 @@
 
 def all_to_all(axis, n, me, rows_of, landing, send_sem, recv_sem):
     copies = []
-    for k in range(1, n):
+    for k in shifts(n):
         peer = (me + k) % n
         copy = pltpu.make_async_remote_copy(
             src_ref=rows_of(peer), dst_ref=landing.at[me], send_sem=send_sem.at[k],
@@ -131,7 +138,7 @@
 def start_all_to_all(axis, n, rows_of, landing, send_sem, recv_sem):
     me = lax.axis_index(axis)
     copies = []
-    for k in range(1, n):
+    for k in shifts(n):
         peer = (me + k) % n
         copy = pltpu.make_async_remote_copy(
             src_ref=rows_of(peer), dst_ref=landing.at[me], send_sem=send_sem.at[k],

time: 80.7 us -> 81.5 us (level); the launches traced: 79.5 us -> 81.3 us
  Pallas kernels: 58 us -> 59.8 us
    pallas_call x1, Pallas kernels: 26.2 us -> 27.3 us  [whiten_broadcast(): pl.pallas_call(functools.partial(whiten_broadcast_kernel, axis, n, channe...]
where the time goes in v13:
time: 81.5 us; the launch traced here: 81.3 us
  Pallas kernels  59.8 us (73%)
  other arithmetic  10.7 us (13%)
  matrix products  8.24 us (10%)
  local copies, waits for them, and re-layouts  2.44 us (3%)
    pallas_call x1, Pallas kernels, scatter_sum(): pl.pallas_call(functools.partial(reduce_kernel, axis, n), out_shape=jax.S...  32.6 us
    pallas_call x1, Pallas kernels, whiten_broadcast(): pl.pallas_call(functools.partial(whiten_broadcast_kernel, axis, n, channe...  27.3 us
    reduce_sum x1, other arithmetic, cross_spectra(): imag_part = jnp.sum(sr * ri - si * rr, axis=0)  6.44 us
    dot_general x1, matrix products, body(): jnp.dot(imag_rows, sin_t, precision=lax.Precision.HIGH, preferred_element...  4.54 us
    dot_general x1, matrix products, body(): jnp.dot(real_rows, cos_t, precision=lax.Precision.HIGH, preferred_element...  3.7 us

profile of v13, /device:TPU:32, one launch (start us, length us, event | category | flops | bytes accessed | tf_op | source)
XLA Modules:
  0.0 81.3 jit_solution(5262232421241696985)
XLA Ops:
  0.0 0.3 fusion.12
  0.4 0.5 fusion.10
  0.9 27.3 %shard_map.37 = (bf16[64,4096]{1,0:T(8,128)(2,1)}, bf16[4,32,4096]{2,1,0:T(8,128)(2,1)}) custom-call(bf16[4,32,4096]{2,1,0:T(8,128)(2,1)} %spec_ref.1, s32[32]{0:T(128)} %q_ref.1, s32[2]{0:T(128)} %sb_ref.1), custom_call_target="tpu_custom_call" | custom-call | tf_op jit(solution)/shard_map/pallas_call | solution.py:216
  28.2 1.1 %slice_bitcast_fusion = (bf16[4,8,4096]{2,1,0:T(8,128)(2,1)S(1)}, bf16[4,8,4096]{2,1,0:T(8,128)(2,1)S(1)}) fusion(bf16[64,4096]{1,0:T(8,128)(2,1)} %get-tuple-element.7), kind=kLoop, calls=%fused_computation.11 | loop fusion | bytes 1048576 | tf_op jit(solution)/shard_map/squeeze | solution.py:254
  29.2 0.1 slice_convert_fusion.3
  29.3 1.4 %slice_convert_fusion.1 = (f32[4,32,2048]{2,1,0:T(8,128)S(1)}, f32[4,32,2048]{2,1,0:T(8,128)S(1)}) fusion(bf16[4,32,4096]{2,1,0:T(8,128)(2,1)} %get-tuple-element.8), kind=kLoop, calls=%fused_computation.10 | loop fusion | flops 524288 | bytes 3145728 | tf_op jit(solution)/shard_map/convert_element_type | solution.py:49
  30.8 6.4 %subtract_reduce_fusion.1 = (f32[32,8,2048]{2,1,0:T(8,128)S(1)}, f32[32,8,2048]{2,1,0:T(8,128)S(1)}, f32[32,8,2048]{2,1,0:T(8,128)S(1)}, f32[32,8,2048]{2,1,0:T(8,128)S(1)}) fusion(f32[4,32,2048]{2,1,0:T(8,128)S(1)} %get-tuple-element.16, f32[4,8,2048]{2,1,0:T(8,128)S(1)} %get-tuple-element.29, f32[4,32,2048]{2,1,0:T(8,128)S(1)} %get-tuple-element.15, ...), kind=kLoop, calls=%fused_computation.1 | loop fusion | flops 31457280 | bytes 11534336 | tf_op jit(solution)/shard_map/reduce_sum | solution.py:52
  37.2 0.3 pad_maximum_fusion.1
  37.5 0.5 pad_maximum_fusion
  38.0 1.1 %negate_multiply_fusion = (f32[32,64,512]{2,1,0:T(8,128)S(1)}, f32[32,64,512]{2,1,0:T(8,128)S(1)}) fusion(f32[64,512]{1,0:T(8,128)S(1)} %get-tuple-element.28, f32[32,512]{1,0:T(8,128)S(1)} %get-tuple-element.26, f32[64,512]{1,0:T(8,128)S(1)} %get-tuple-element.27, f32[32,512]{1,0:T(8,128)S(1)} %get-tuple-element.25), kind=kLoop, calls=%fused_computation.6 | loop fusion | flops 9437184 | bytes 8781824 | tf_op jit(solution)/shard_map/mul | solution.py:34
  39.1 3.7 %fusion.13 = f32[512,512]{1,0:T(8,128)S(1)} fusion(f32[512,2048]{1,0:T(8,128)S(1)} %bitcast.25, f32[2048,512]{1,0:T(8,128)S(1)} %bitcast.27), kind=kOutput, calls=%fused_computation.40 | convolution fusion | flops 3221225472 | bytes 9437184 | tf_op jit(solution)/shard_map/dot_general | solution.py:260
  42.8 4.5 %convolution_add_fusion.x_ref = f32[512,512]{1,0:T(8,128)} fusion(f32[512,512]{1,0:T(8,128)S(1)} %fusion.13, f32[512,2048]{1,0:T(8,128)S(1)} %bitcast.24, f32[2048,512]{1,0:T(8,128)S(1)} %bitcast.26), kind=kOutput, calls=%fused_computation.8 | convolution fusion | flops 3221487616 | bytes 10485760 | tf_op jit(solution)/shard_map/dot_general | solution.py:263
  47.4 32.6 %shard_map.38 = bf16[2,2,8,512]{3,2,1,0:T(8,128)(2,1)} custom-call(f32[512,512]{1,0:T(8,128)} %convolution_add_fusion.x_ref), custom_call_target="tpu_custom_call" | custom-call | tf_op jit(solution)/shard_map/pallas_call | solution.py:232
  80.0 1.4 %copy.9 = bf16[2,2,8,512]{3,2,1,0:T(8,128)(2,1)} copy(bf16[2,2,8,512]{3,2,1,0:T(8,128)(2,1)} %shard_map.38) | data formatting | bytes 65536
  (2 shorter events, 0.0 us)

commit v14 on v12

--- a/solution.py
+++ b/solution.py
@@ -112,6 +112,79 @@
     own.wait()
     total = jnp.sum(parts[...], axis=0).reshape(o_ref.shape)
     o_ref[...] = total.astype(o_ref.dtype)
+
+
+def pair_ring_kernel(axis, ring, x_ref, o_ref, mine, land_a, send_b, land_b, sems_a, sems_b,
+                     own_sems):
+    me = lax.axis_index(axis)
+    z0, xl = me // 2, me % 2
+    height = x_ref.shape[0] // (2 * ring)
+
+    def rows(dest):
+        return x_ref.at[pl.ds(pl.multiple_of(dest * height, height), height)]
+
+    own = []
+    for z in range(ring):
+        copy = pltpu.make_async_copy(rows(2 * z + xl), mine.at[z], own_sems.at[z])
+        copy.start()
+        own.append(copy)
+    barrier = pltpu.get_barrier_semaphore()
+    peers = [2 * z0 + 1 - xl] + [2 * ((z0 + k) % ring) + xl for k in range(1, ring)]
+    for peer in peers:
+        pl.semaphore_signal(barrier, inc=1, device_id={axis: peer},
+                            device_id_type=pl.DeviceIdType.MESH)
+    pl.semaphore_wait(barrier, len(peers))
+    copies = []
+    for z in range(ring):
+        copy = pltpu.make_async_remote_copy(
+            src_ref=rows(2 * z + 1 - xl), dst_ref=land_a.at[z], send_sem=sems_a.at[0, z],
+            recv_sem=sems_a.at[1, z], device_id={axis: peers[0]},
+            device_id_type=pl.DeviceIdType.MESH)
+        copy.start()
+        copies.append(copy)
+    for copy in copies:
+        copy.wait_send()
+    for copy in copies:
+        copy.wait_recv()
+    for copy in own:
+        copy.wait()
+    send_b[...] = mine[...] + land_a[...]
+    copies = []
+    for k in range(1, ring):
+        zp = (z0 + k) % ring
+        copy = pltpu.make_async_remote_copy(
+            src_ref=send_b.at[zp], dst_ref=land_b.at[z0], send_sem=sems_b.at[0, k],
+            recv_sem=sems_b.at[1, z0], device_id={axis: 2 * zp + xl},
+            device_id_type=pl.DeviceIdType.MESH)
+        copy.start()
+        copies.append(copy)
+    for copy in copies:
+        copy.wait_send()
+    for k in range(1, ring):
+        zs = (z0 + ring - k) % ring
+        pltpu.make_async_remote_copy(
+            src_ref=land_b.at[zs], dst_ref=land_b.at[zs], send_sem=sems_b.at[0, k],
+            recv_sem=sems_b.at[1, zs], device_id={axis: 2 * zs + xl},
+            device_id_type=pl.DeviceIdType.MESH).wait_recv()
+    land_b[z0] = send_b[z0]
+    total = jnp.sum(land_b[...], axis=0).reshape(o_ref.shape)
+    o_ref[...] = total.astype(o_ref.dtype)
+
+
+def pair_ring_sum(rows, axis, shape, dtype):
+    n = lax.axis_size(axis)
+    ring = n // 2
+    chunk = (ring, rows.shape[0] // n, rows.shape[1])
+    return pl.pallas_call(
+        functools.partial(pair_ring_kernel, axis, ring),
+        out_shape=jax.ShapeDtypeStruct(shape, dtype),
+        in_specs=[pl.BlockSpec(memory_space=pl.ANY)],
+        out_specs=pl.BlockSpec(memory_space=pltpu.VMEM),
+        scratch_shapes=[pltpu.VMEM(chunk, rows.dtype)] * 4
+        + [pltpu.SemaphoreType.DMA((2, ring)), pltpu.SemaphoreType.DMA((2, ring)),
+           pltpu.SemaphoreType.DMA((ring,))],
+        compiler_params=pltpu.CompilerParams(collective_id=1, has_side_effects=True),
+    )(rows)
 
 
 def broadcast_sum(value, axis):
@@ -256,7 +329,7 @@
     out = out + jnp.dot(
         imag_rows, sin_t, precision=lax.Precision.HIGH, preferred_element_type=jnp.float32
     )
-    return scatter_sum(out, "win", (STEPS, per_dest, SRC, L), jnp.bfloat16)
+    return pair_ring_sum(out, "win", (STEPS, per_dest, SRC, L), jnp.bfloat16)
 
 
 def solution(mesh):

time: 80.7 us -> 81.7 us (1.012)
  no operation moved by 1% of the time
where the time goes in v14:
time: 81.7 us; the launch traced here: 80.3 us
  Pallas kernels  58.8 us (72%)
  other arithmetic  10.7 us (13%)
  matrix products  8.25 us (10%)
  local copies, waits for them, and re-layouts  2.44 us (3%)
    pallas_call x1, Pallas kernels, pair_ring_sum(): pl.pallas_call(functools.partial(pair_ring_kernel, axis, ring), out_shape...  32.6 us
    pallas_call x1, Pallas kernels, whiten_broadcast(): pl.pallas_call(functools.partial(whiten_broadcast_kernel, axis, n, channe...  26.2 us
    reduce_sum x1, other arithmetic, cross_spectra(): imag_part = jnp.sum(sr * ri - si * rr, axis=0)  6.44 us
    dot_general x1, matrix products, body(): jnp.dot(imag_rows, sin_t, precision=lax.Precision.HIGH, preferred_element...  4.54 us
    dot_general x1, matrix products, body(): jnp.dot(real_rows, cos_t, precision=lax.Precision.HIGH, preferred_element...  3.7 us

profile of v14, /device:TPU:32, one launch (start us, length us, event | category | flops | bytes accessed | tf_op | source)
XLA Modules:
  0.0 80.3 jit_solution(18097936139977870910)
XLA Ops:
  0.0 0.3 fusion.12
  0.4 0.5 fusion.10
  0.9 26.2 %shard_map.37 = (bf16[64,4096]{1,0:T(8,128)(2,1)}, bf16[4,32,4096]{2,1,0:T(8,128)(2,1)}) custom-call(bf16[4,32,4096]{2,1,0:T(8,128)(2,1)} %spec_ref.1, s32[32]{0:T(128)} %q_ref.1, s32[2]{0:T(128)} %sb_ref.1), custom_call_target="tpu_custom_call" | custom-call | tf_op jit(solution)/shard_map/pallas_call | solution.py:282
  27.1 1.1 %slice_bitcast_fusion = (bf16[4,8,4096]{2,1,0:T(8,128)(2,1)S(1)}, bf16[4,8,4096]{2,1,0:T(8,128)(2,1)S(1)}) fusion(bf16[64,4096]{1,0:T(8,128)(2,1)} %get-tuple-element.7), kind=kLoop, calls=%fused_computation.11 | loop fusion | bytes 1048576 | tf_op jit(solution)/shard_map/squeeze | solution.py:320
  28.2 0.1 slice_convert_fusion.3
  28.3 1.4 %slice_convert_fusion.1 = (f32[4,32,2048]{2,1,0:T(8,128)S(1)}, f32[4,32,2048]{2,1,0:T(8,128)S(1)}) fusion(bf16[4,32,4096]{2,1,0:T(8,128)(2,1)} %get-tuple-element.8), kind=kLoop, calls=%fused_computation.10 | loop fusion | flops 524288 | bytes 3145728 | tf_op jit(solution)/shard_map/convert_element_type | solution.py:49
  29.7 6.4 %subtract_reduce_fusion.1 = (f32[32,8,2048]{2,1,0:T(8,128)S(1)}, f32[32,8,2048]{2,1,0:T(8,128)S(1)}, f32[32,8,2048]{2,1,0:T(8,128)S(1)}, f32[32,8,2048]{2,1,0:T(8,128)S(1)}) fusion(f32[4,32,2048]{2,1,0:T(8,128)S(1)} %get-tuple-element.16, f32[4,8,2048]{2,1,0:T(8,128)S(1)} %get-tuple-element.29, f32[4,32,2048]{2,1,0:T(8,128)S(1)} %get-tuple-element.15, ...), kind=kLoop, calls=%fused_computation.1 | loop fusion | flops 31457280 | bytes 11534336 | tf_op jit(solution)/shard_map/reduce_sum | solution.py:52
  36.2 0.3 pad_maximum_fusion.1
  36.5 0.5 pad_maximum_fusion
  37.0 1.1 %negate_multiply_fusion = (f32[32,64,512]{2,1,0:T(8,128)S(1)}, f32[32,64,512]{2,1,0:T(8,128)S(1)}) fusion(f32[64,512]{1,0:T(8,128)S(1)} %get-tuple-element.28, f32[32,512]{1,0:T(8,128)S(1)} %get-tuple-element.26, f32[64,512]{1,0:T(8,128)S(1)} %get-tuple-element.27, f32[32,512]{1,0:T(8,128)S(1)} %get-tuple-element.25), kind=kLoop, calls=%fused_computation.6 | loop fusion | flops 9437184 | bytes 8781824 | tf_op jit(solution)/shard_map/mul | solution.py:34
  38.1 3.7 %fusion.13 = f32[512,512]{1,0:T(8,128)S(1)} fusion(f32[512,2048]{1,0:T(8,128)S(1)} %bitcast.25, f32[2048,512]{1,0:T(8,128)S(1)} %bitcast.27), kind=kOutput, calls=%fused_computation.40 | convolution fusion | flops 3221225472 | bytes 9437184 | tf_op jit(solution)/shard_map/dot_general | solution.py:326
  41.8 4.5 %convolution_add_fusion.x_ref = f32[512,512]{1,0:T(8,128)} fusion(f32[512,512]{1,0:T(8,128)S(1)} %fusion.13, f32[512,2048]{1,0:T(8,128)S(1)} %bitcast.24, f32[2048,512]{1,0:T(8,128)S(1)} %bitcast.26), kind=kOutput, calls=%fused_computation.8 | convolution fusion | flops 3221487616 | bytes 10485760 | tf_op jit(solution)/shard_map/dot_general | solution.py:329
  46.3 32.6 %shard_map.38 = bf16[2,2,8,512]{3,2,1,0:T(8,128)(2,1)} custom-call(f32[512,512]{1,0:T(8,128)} %convolution_add_fusion.x_ref), custom_call_target="tpu_custom_call" | custom-call | tf_op jit(solution)/shard_map/pallas_call | solution.py:178
  78.9 1.4 %copy.9 = bf16[2,2,8,512]{3,2,1,0:T(8,128)(2,1)} copy(bf16[2,2,8,512]{3,2,1,0:T(8,128)(2,1)} %shard_map.38) | data formatting | bytes 65536
  (2 shorter events, 0.0 us)

commit v15 on v12

--- a/solution.py
+++ b/solution.py
@@ -108,7 +108,28 @@
     own = pltpu.make_async_copy(rows(me), parts.at[me], own_sem.at[0])
     own.start()
     greet(axis, n, me)
-    all_to_all(axis, n, me, rows, parts, sems.at[0], sems.at[1])
+    half = height // 2
+    copies = []
+    for k in range(1, n):
+        peer = (me + k) % n
+        for h in range(2):
+            copy = pltpu.make_async_remote_copy(
+                src_ref=rows(peer).at[pl.ds(h * half, half)],
+                dst_ref=parts.at[me, pl.ds(h * half, half)], send_sem=sems.at[0, k, h],
+                recv_sem=sems.at[1, me, h], device_id={axis: peer},
+                device_id_type=pl.DeviceIdType.MESH)
+            copy.start()
+            copies.append(copy)
+    for copy in copies:
+        copy.wait_send()
+    for k in range(1, n):
+        source = (me + n - k) % n
+        for h in range(2):
+            pltpu.make_async_remote_copy(
+                src_ref=parts.at[source, pl.ds(h * half, half)],
+                dst_ref=parts.at[source, pl.ds(h * half, half)], send_sem=sems.at[0, k, h],
+                recv_sem=sems.at[1, source, h], device_id={axis: source},
+                device_id_type=pl.DeviceIdType.MESH).wait_recv()
     own.wait()
     total = jnp.sum(parts[...], axis=0).reshape(o_ref.shape)
     o_ref[...] = total.astype(o_ref.dtype)
@@ -227,7 +248,7 @@
         out_shape=jax.ShapeDtypeStruct(shape, dtype),
         in_specs=[pl.BlockSpec(memory_space=pl.ANY)],
         out_specs=pl.BlockSpec(memory_space=pltpu.VMEM),
-        scratch_shapes=[pltpu.VMEM((n,) + chunk, rows.dtype), pltpu.SemaphoreType.DMA((2, n)),
+        scratch_shapes=[pltpu.VMEM((n,) + chunk, rows.dtype), pltpu.SemaphoreType.DMA((2, n, 2)),
                         pltpu.SemaphoreType.DMA((1,))],
         compiler_params=pltpu.CompilerParams(collective_id=1, has_side_effects=True),
     )(rows)

time: 80.7 us -> 81 us (level)
  no operation moved by 1% of the time
where the time goes in v15:
time: 81 us; the launch traced here: 79.8 us
  Pallas kernels  58.3 us (72%)
  other arithmetic  10.7 us (13%)
  matrix products  8.25 us (10%)
  local copies, waits for them, and re-layouts  2.44 us (3%)
    pallas_call x1, Pallas kernels, scatter_sum(): pl.pallas_call(functools.partial(reduce_kernel, axis, n), out_shape=jax.S...  32.1 us
    pallas_call x1, Pallas kernels, whiten_broadcast(): pl.pallas_call(functools.partial(whiten_broadcast_kernel, axis, n, channe...  26.2 us
    reduce_sum x1, other arithmetic, cross_spectra(): imag_part = jnp.sum(sr * ri - si * rr, axis=0)  6.44 us
    dot_general x1, matrix products, body(): jnp.dot(imag_rows, sin_t, precision=lax.Precision.HIGH, preferred_element...  4.54 us
    dot_general x1, matrix products, body(): jnp.dot(real_rows, cos_t, precision=lax.Precision.HIGH, preferred_element...  3.7 us

profile of v15, /device:TPU:32, one launch (start us, length us, event | category | flops | bytes accessed | tf_op | source)
XLA Modules:
  0.0 79.8 jit_solution(7067466647493110164)
XLA Ops:
  0.0 0.3 fusion.12
  0.4 0.5 fusion.10
  0.9 26.2 %shard_map.37 = (bf16[64,4096]{1,0:T(8,128)(2,1)}, bf16[4,32,4096]{2,1,0:T(8,128)(2,1)}) custom-call(bf16[4,32,4096]{2,1,0:T(8,128)(2,1)} %spec_ref.1, s32[32]{0:T(128)} %q_ref.1, s32[2]{0:T(128)} %sb_ref.1), custom_call_target="tpu_custom_call" | custom-call | tf_op jit(solution)/shard_map/pallas_call | solution.py:230
  27.1 1.1 %slice_bitcast_fusion = (bf16[4,8,4096]{2,1,0:T(8,128)(2,1)S(1)}, bf16[4,8,4096]{2,1,0:T(8,128)(2,1)S(1)}) fusion(bf16[64,4096]{1,0:T(8,128)(2,1)} %get-tuple-element.7), kind=kLoop, calls=%fused_computation.11 | loop fusion | bytes 1048576 | tf_op jit(solution)/shard_map/squeeze | solution.py:268
  28.2 0.1 slice_convert_fusion.3
  28.3 1.4 %slice_convert_fusion.1 = (f32[4,32,2048]{2,1,0:T(8,128)S(1)}, f32[4,32,2048]{2,1,0:T(8,128)S(1)}) fusion(bf16[4,32,4096]{2,1,0:T(8,128)(2,1)} %get-tuple-element.8), kind=kLoop, calls=%fused_computation.10 | loop fusion | flops 524288 | bytes 3145728 | tf_op jit(solution)/shard_map/convert_element_type | solution.py:49
  29.7 6.4 %subtract_reduce_fusion.1 = (f32[32,8,2048]{2,1,0:T(8,128)S(1)}, f32[32,8,2048]{2,1,0:T(8,128)S(1)}, f32[32,8,2048]{2,1,0:T(8,128)S(1)}, f32[32,8,2048]{2,1,0:T(8,128)S(1)}) fusion(f32[4,32,2048]{2,1,0:T(8,128)S(1)} %get-tuple-element.16, f32[4,8,2048]{2,1,0:T(8,128)S(1)} %get-tuple-element.29, f32[4,32,2048]{2,1,0:T(8,128)S(1)} %get-tuple-element.15, ...), kind=kLoop, calls=%fused_computation.1 | loop fusion | flops 31457280 | bytes 11534336 | tf_op jit(solution)/shard_map/reduce_sum | solution.py:52
  36.2 0.3 pad_maximum_fusion.1
  36.5 0.5 pad_maximum_fusion
  37.0 1.1 %negate_multiply_fusion = (f32[32,64,512]{2,1,0:T(8,128)S(1)}, f32[32,64,512]{2,1,0:T(8,128)S(1)}) fusion(f32[64,512]{1,0:T(8,128)S(1)} %get-tuple-element.28, f32[32,512]{1,0:T(8,128)S(1)} %get-tuple-element.26, f32[64,512]{1,0:T(8,128)S(1)} %get-tuple-element.27, f32[32,512]{1,0:T(8,128)S(1)} %get-tuple-element.25), kind=kLoop, calls=%fused_computation.6 | loop fusion | flops 9437184 | bytes 8781824 | tf_op jit(solution)/shard_map/mul | solution.py:34
  38.1 3.7 %fusion.13 = f32[512,512]{1,0:T(8,128)S(1)} fusion(f32[512,2048]{1,0:T(8,128)S(1)} %bitcast.25, f32[2048,512]{1,0:T(8,128)S(1)} %bitcast.27), kind=kOutput, calls=%fused_computation.40 | convolution fusion | flops 3221225472 | bytes 9437184 | tf_op jit(solution)/shard_map/dot_general | solution.py:274
  41.8 4.5 %convolution_add_fusion.x_ref = f32[512,512]{1,0:T(8,128)} fusion(f32[512,512]{1,0:T(8,128)S(1)} %fusion.13, f32[512,2048]{1,0:T(8,128)S(1)} %bitcast.24, f32[2048,512]{1,0:T(8,128)S(1)} %bitcast.26), kind=kOutput, calls=%fused_computation.8 | convolution fusion | flops 3221487616 | bytes 10485760 | tf_op jit(solution)/shard_map/dot_general | solution.py:277
  46.3 32.1 %shard_map.38 = bf16[2,2,8,512]{3,2,1,0:T(8,128)(2,1)} custom-call(f32[512,512]{1,0:T(8,128)} %convolution_add_fusion.x_ref), custom_call_target="tpu_custom_call" | custom-call | tf_op jit(solution)/shard_map/pallas_call | solution.py:246
  78.4 1.4 %copy.9 = bf16[2,2,8,512]{3,2,1,0:T(8,128)(2,1)} copy(bf16[2,2,8,512]{3,2,1,0:T(8,128)(2,1)} %shard_map.38) | data formatting | bytes 65536
  (2 shorter events, 0.0 us)

commit v16 on v12

--- a/solution.py
+++ b/solution.py
@@ -256,7 +256,8 @@
     out = out + jnp.dot(
         imag_rows, sin_t, precision=lax.Precision.HIGH, preferred_element_type=jnp.float32
     )
-    return scatter_sum(out, "win", (STEPS, per_dest, SRC, L), jnp.bfloat16)
+    summed = scatter_sum(out, "win", (STEPS, per_dest, SRC, L), jnp.float32)
+    return summed.astype(jnp.bfloat16)
 
 
 def solution(mesh):

time: 80.7 us -> 80.8 us (level)
  other arithmetic: 10.7 us -> 12.2 us
  local copies, waits for them, and re-layouts: 2.44 us -> 1.07 us
    convert_element_type x0 -> x1, other arithmetic: none -> 1.46 us  [body(): return summed.astype(jnp.bfloat16)]
    unnamed x1 -> x0, local copies, waits for them, and re-layouts: 1.38 us -> none
where the time goes in v16:
time: 80.8 us; the launch traced here: 79.6 us
  Pallas kernels  58 us (72%)
  other arithmetic  12.2 us (15%)
  matrix products  8.25 us (10%)
  local copies, waits for them, and re-layouts  1.07 us (1%)
    pallas_call x1, Pallas kernels, scatter_sum(): pl.pallas_call(functools.partial(reduce_kernel, axis, n), out_shape=jax.S...  31.8 us
    pallas_call x1, Pallas kernels, whiten_broadcast(): pl.pallas_call(functools.partial(whiten_broadcast_kernel, axis, n, channe...  26.2 us
    reduce_sum x1, other arithmetic, cross_spectra(): imag_part = jnp.sum(sr * ri - si * rr, axis=0)  6.44 us
    dot_general x1, matrix products, body(): jnp.dot(imag_rows, sin_t, precision=lax.Precision.HIGH, preferred_element...  4.54 us
    dot_general x1, matrix products, body(): jnp.dot(real_rows, cos_t, precision=lax.Precision.HIGH, preferred_element...  3.7 us

profile of v16, /device:TPU:32, one launch (start us, length us, event | category | flops | bytes accessed | tf_op | source)
XLA Modules:
  0.0 79.6 jit_solution(17884392487133549639)
XLA Ops:
  0.0 0.3 fusion.12
  0.4 0.5 fusion.10
  0.9 26.2 %shard_map.37 = (bf16[64,4096]{1,0:T(8,128)(2,1)}, bf16[4,32,4096]{2,1,0:T(8,128)(2,1)}) custom-call(bf16[4,32,4096]{2,1,0:T(8,128)(2,1)} %spec_ref.1, s32[32]{0:T(128)} %q_ref.1, s32[2]{0:T(128)} %sb_ref.1), custom_call_target="tpu_custom_call" | custom-call | tf_op jit(solution)/shard_map/pallas_call | solution.py:209
  27.1 1.1 %slice_bitcast_fusion = (bf16[4,8,4096]{2,1,0:T(8,128)(2,1)S(1)}, bf16[4,8,4096]{2,1,0:T(8,128)(2,1)S(1)}) fusion(bf16[64,4096]{1,0:T(8,128)(2,1)} %get-tuple-element.7), kind=kLoop, calls=%fused_computation.11 | loop fusion | bytes 1048576 | tf_op jit(solution)/shard_map/squeeze | solution.py:247
  28.2 0.1 slice_convert_fusion.3
  28.3 1.4 %slice_convert_fusion.1 = (f32[4,32,2048]{2,1,0:T(8,128)S(1)}, f32[4,32,2048]{2,1,0:T(8,128)S(1)}) fusion(bf16[4,32,4096]{2,1,0:T(8,128)(2,1)} %get-tuple-element.8), kind=kLoop, calls=%fused_computation.10 | loop fusion | flops 524288 | bytes 3145728 | tf_op jit(solution)/shard_map/convert_element_type | solution.py:49
  29.7 6.4 %subtract_reduce_fusion.1 = (f32[32,8,2048]{2,1,0:T(8,128)S(1)}, f32[32,8,2048]{2,1,0:T(8,128)S(1)}, f32[32,8,2048]{2,1,0:T(8,128)S(1)}, f32[32,8,2048]{2,1,0:T(8,128)S(1)}) fusion(f32[4,32,2048]{2,1,0:T(8,128)S(1)} %get-tuple-element.16, f32[4,8,2048]{2,1,0:T(8,128)S(1)} %get-tuple-element.29, f32[4,32,2048]{2,1,0:T(8,128)S(1)} %get-tuple-element.15, ...), kind=kLoop, calls=%fused_computation.1 | loop fusion | flops 31457280 | bytes 11534336 | tf_op jit(solution)/shard_map/reduce_sum | solution.py:52
  36.2 0.3 pad_maximum_fusion.1
  36.5 0.5 pad_maximum_fusion
  37.0 1.1 %negate_multiply_fusion = (f32[32,64,512]{2,1,0:T(8,128)S(1)}, f32[32,64,512]{2,1,0:T(8,128)S(1)}) fusion(f32[64,512]{1,0:T(8,128)S(1)} %get-tuple-element.28, f32[32,512]{1,0:T(8,128)S(1)} %get-tuple-element.26, f32[64,512]{1,0:T(8,128)S(1)} %get-tuple-element.27, f32[32,512]{1,0:T(8,128)S(1)} %get-tuple-element.25), kind=kLoop, calls=%fused_computation.6 | loop fusion | flops 9437184 | bytes 8781824 | tf_op jit(solution)/shard_map/mul | solution.py:34
  38.1 3.7 %fusion.13 = f32[512,512]{1,0:T(8,128)S(1)} fusion(f32[512,2048]{1,0:T(8,128)S(1)} %bitcast.25, f32[2048,512]{1,0:T(8,128)S(1)} %bitcast.27), kind=kOutput, calls=%fused_computation.40 | convolution fusion | flops 3221225472 | bytes 9437184 | tf_op jit(solution)/shard_map/dot_general | solution.py:253
  41.8 4.5 %convolution_add_fusion.x_ref = f32[512,512]{1,0:T(8,128)} fusion(f32[512,512]{1,0:T(8,128)S(1)} %fusion.13, f32[512,2048]{1,0:T(8,128)S(1)} %bitcast.24, f32[2048,512]{1,0:T(8,128)S(1)} %bitcast.26), kind=kOutput, calls=%fused_computation.8 | convolution fusion | flops 3221487616 | bytes 10485760 | tf_op jit(solution)/shard_map/dot_general | solution.py:256
  46.3 31.8 %shard_map.38 = f32[2,2,8,512]{3,2,1,0:T(8,128)} custom-call(f32[512,512]{1,0:T(8,128)} %convolution_add_fusion.x_ref), custom_call_target="tpu_custom_call" | custom-call | tf_op jit(solution)/shard_map/pallas_call | solution.py:225
  78.2 1.5 %convert_element_type.61 = bf16[2,2,8,512]{3,2,1,0:T(8,128)(2,1)} convert(f32[2,2,8,512]{3,2,1,0:T(8,128)} %shard_map.38) | non-fusion elementwise | flops 16384 | bytes 98304 | tf_op jit(solution)/shard_map/convert_element_type | solution.py:260
  (2 shorter events, 0.0 us)

commit v17 on v12

--- a/solution.py
+++ b/solution.py
@@ -176,12 +176,16 @@
         return values * (quality / jnp.sqrt(energy + 1e-06))
 
     for w in range(windows):
-        block = weighted(w)
+        raw = spec_ref[w].astype(jnp.float32)
         for k in range(steps):
-            kept = jnp.zeros((SRC, width), jnp.float32)
+            picked = jnp.zeros((SRC, width), jnp.float32)
+            gain = jnp.zeros((SRC, 1), jnp.float32)
             for b in range(per_group):
                 hit = me * per_group + b == sb_ref[k]
-                kept = kept + jnp.where(hit, block[b * SRC:(b + 1) * SRC], 0.0)
+                picked = picked + jnp.where(hit, raw[b * SRC:(b + 1) * SRC], 0.0)
+                gain = gain + jnp.where(hit, quality[b * SRC:(b + 1) * SRC], 0.0)
+            energy = jnp.sum(picked * picked, axis=-1, keepdims=True) / bins
+            kept = picked * (gain / jnp.sqrt(energy + 1e-06))
             row = (k * windows + w) * SRC
             send[row:row + SRC, :] = kept.astype(send.dtype)
     greet(axis, n, me)

time: 80.7 us -> 80.6 us (level)
  no operation moved by 1% of the time
where the time goes in v17:
time: 80.6 us; the launch traced here: 79.4 us
  Pallas kernels  57.9 us (72%)
  other arithmetic  10.7 us (13%)
  matrix products  8.24 us (10%)
  local copies, waits for them, and re-layouts  2.44 us (3%)
    pallas_call x1, Pallas kernels, scatter_sum(): pl.pallas_call(functools.partial(reduce_kernel, axis, n), out_shape=jax.S...  31.8 us
    pallas_call x1, Pallas kernels, whiten_broadcast(): pl.pallas_call(functools.partial(whiten_broadcast_kernel, axis, n, channe...  26.1 us
    reduce_sum x1, other arithmetic, cross_spectra(): imag_part = jnp.sum(sr * ri - si * rr, axis=0)  6.44 us
    dot_general x1, matrix products, body(): jnp.dot(imag_rows, sin_t, precision=lax.Precision.HIGH, preferred_element...  4.53 us
    dot_general x1, matrix products, body(): jnp.dot(real_rows, cos_t, precision=lax.Precision.HIGH, preferred_element...  3.7 us

profile of v17, /device:TPU:32, one launch (start us, length us, event | category | flops | bytes accessed | tf_op | source)
XLA Modules:
  0.0 79.4 jit_solution(3841729119572696241)
XLA Ops:
  0.0 0.3 fusion.12
  0.4 0.5 fusion.10
  0.9 26.1 %shard_map.37 = (bf16[64,4096]{1,0:T(8,128)(2,1)}, bf16[4,32,4096]{2,1,0:T(8,128)(2,1)}) custom-call(bf16[4,32,4096]{2,1,0:T(8,128)(2,1)} %spec_ref.1, s32[32]{0:T(128)} %q_ref.1, s32[2]{0:T(128)} %sb_ref.1), custom_call_target="tpu_custom_call" | custom-call | tf_op jit(solution)/shard_map/pallas_call | solution.py:213
  27.0 1.1 %slice_bitcast_fusion = (bf16[4,8,4096]{2,1,0:T(8,128)(2,1)S(1)}, bf16[4,8,4096]{2,1,0:T(8,128)(2,1)S(1)}) fusion(bf16[64,4096]{1,0:T(8,128)(2,1)} %get-tuple-element.7), kind=kLoop, calls=%fused_computation.11 | loop fusion | bytes 1048576 | tf_op jit(solution)/shard_map/squeeze | solution.py:251
  28.1 0.1 slice_convert_fusion.3
  28.2 1.4 %slice_convert_fusion.1 = (f32[4,32,2048]{2,1,0:T(8,128)S(1)}, f32[4,32,2048]{2,1,0:T(8,128)S(1)}) fusion(bf16[4,32,4096]{2,1,0:T(8,128)(2,1)} %get-tuple-element.8), kind=kLoop, calls=%fused_computation.10 | loop fusion | flops 524288 | bytes 3145728 | tf_op jit(solution)/shard_map/convert_element_type | solution.py:49
  29.6 6.4 %subtract_reduce_fusion.1 = (f32[32,8,2048]{2,1,0:T(8,128)S(1)}, f32[32,8,2048]{2,1,0:T(8,128)S(1)}, f32[32,8,2048]{2,1,0:T(8,128)S(1)}, f32[32,8,2048]{2,1,0:T(8,128)S(1)}) fusion(f32[4,32,2048]{2,1,0:T(8,128)S(1)} %get-tuple-element.16, f32[4,8,2048]{2,1,0:T(8,128)S(1)} %get-tuple-element.29, f32[4,32,2048]{2,1,0:T(8,128)S(1)} %get-tuple-element.15, ...), kind=kLoop, calls=%fused_computation.1 | loop fusion | flops 31457280 | bytes 11534336 | tf_op jit(solution)/shard_map/reduce_sum | solution.py:52
  36.1 0.3 pad_maximum_fusion.1
  36.4 0.5 pad_maximum_fusion
  36.9 1.1 %negate_multiply_fusion = (f32[32,64,512]{2,1,0:T(8,128)S(1)}, f32[32,64,512]{2,1,0:T(8,128)S(1)}) fusion(f32[64,512]{1,0:T(8,128)S(1)} %get-tuple-element.28, f32[32,512]{1,0:T(8,128)S(1)} %get-tuple-element.26, f32[64,512]{1,0:T(8,128)S(1)} %get-tuple-element.27, f32[32,512]{1,0:T(8,128)S(1)} %get-tuple-element.25), kind=kLoop, calls=%fused_computation.6 | loop fusion | flops 9437184 | bytes 8781824 | tf_op jit(solution)/shard_map/mul | solution.py:34
  38.0 3.7 %fusion.13 = f32[512,512]{1,0:T(8,128)S(1)} fusion(f32[512,2048]{1,0:T(8,128)S(1)} %bitcast.25, f32[2048,512]{1,0:T(8,128)S(1)} %bitcast.27), kind=kOutput, calls=%fused_computation.40 | convolution fusion | flops 3221225472 | bytes 9437184 | tf_op jit(solution)/shard_map/dot_general | solution.py:257
  41.7 4.5 %convolution_add_fusion.x_ref = f32[512,512]{1,0:T(8,128)} fusion(f32[512,512]{1,0:T(8,128)S(1)} %fusion.13, f32[512,2048]{1,0:T(8,128)S(1)} %bitcast.24, f32[2048,512]{1,0:T(8,128)S(1)} %bitcast.26), kind=kOutput, calls=%fused_computation.8 | convolution fusion | flops 3221487616 | bytes 10485760 | tf_op jit(solution)/shard_map/dot_general | solution.py:260
  46.2 31.8 %shard_map.38 = bf16[2,2,8,512]{3,2,1,0:T(8,128)(2,1)} custom-call(f32[512,512]{1,0:T(8,128)} %convolution_add_fusion.x_ref), custom_call_target="tpu_custom_call" | custom-call | tf_op jit(solution)/shard_map/pallas_call | solution.py:229
  78.0 1.4 %copy.9 = bf16[2,2,8,512]{3,2,1,0:T(8,128)(2,1)} copy(bf16[2,2,8,512]{3,2,1,0:T(8,128)(2,1)} %shard_map.38) | data formatting | bytes 65536
  (2 shorter events, 0.0 us)

commit v18 on v12

--- a/solution.py
+++ b/solution.py
@@ -175,6 +175,10 @@
         energy = jnp.sum(values * values, axis=-1, keepdims=True) / bins
         return values * (quality / jnp.sqrt(energy + 1e-06))
 
+    barrier = pltpu.get_barrier_semaphore()
+    for k in range(1, n):
+        pl.semaphore_signal(barrier, inc=1, device_id={axis: (me + k) % n},
+                            device_id_type=pl.DeviceIdType.MESH)
     for w in range(windows):
         block = weighted(w)
         for k in range(steps):
@@ -184,7 +188,7 @@
                 kept = kept + jnp.where(hit, block[b * SRC:(b + 1) * SRC], 0.0)
             row = (k * windows + w) * SRC
             send[row:row + SRC, :] = kept.astype(send.dtype)
-    greet(axis, n, me)
+    pl.semaphore_wait(barrier, n - 1)
     columns = columns_of(send, n)
     parts[me] = columns(me)[...]
     wait = start_all_to_all(axis, n, columns, parts, sems.at[0], sems.at[1])

time: 80.7 us -> 80 us (level)
  no operation moved by 1% of the time
where the time goes in v18:
time: 80 us; the launch traced here: 78.9 us
  Pallas kernels  57.4 us (72%)
  other arithmetic  10.7 us (13%)
  matrix products  8.25 us (10%)
  local copies, waits for them, and re-layouts  2.44 us (3%)
    pallas_call x1, Pallas kernels, scatter_sum(): pl.pallas_call(functools.partial(reduce_kernel, axis, n), out_shape=jax.S...  31.8 us
    pallas_call x1, Pallas kernels, whiten_broadcast(): pl.pallas_call(functools.partial(whiten_broadcast_kernel, axis, n, channe...  25.6 us
    reduce_sum x1, other arithmetic, cross_spectra(): imag_part = jnp.sum(sr * ri - si * rr, axis=0)  6.44 us
    dot_general x1, matrix products, body(): jnp.dot(imag_rows, sin_t, precision=lax.Precision.HIGH, preferred_element...  4.54 us
    dot_general x1, matrix products, body(): jnp.dot(real_rows, cos_t, precision=lax.Precision.HIGH, preferred_element...  3.7 us

profile of v18, /device:TPU:32, one launch (start us, length us, event | category | flops | bytes accessed | tf_op | source)
XLA Modules:
  0.0 78.9 jit_solution(4545897892579791993)
XLA Ops:
  0.0 0.3 fusion.12
  0.4 0.5 fusion.10
  0.9 25.6 %shard_map.37 = (bf16[64,4096]{1,0:T(8,128)(2,1)}, bf16[4,32,4096]{2,1,0:T(8,128)(2,1)}) custom-call(bf16[4,32,4096]{2,1,0:T(8,128)(2,1)} %spec_ref.1, s32[32]{0:T(128)} %q_ref.1, s32[2]{0:T(128)} %sb_ref.1), custom_call_target="tpu_custom_call" | custom-call | tf_op jit(solution)/shard_map/pallas_call | solution.py:213
  26.5 1.1 %slice_bitcast_fusion = (bf16[4,8,4096]{2,1,0:T(8,128)(2,1)S(1)}, bf16[4,8,4096]{2,1,0:T(8,128)(2,1)S(1)}) fusion(bf16[64,4096]{1,0:T(8,128)(2,1)} %get-tuple-element.7), kind=kLoop, calls=%fused_computation.11 | loop fusion | bytes 1048576 | tf_op jit(solution)/shard_map/squeeze | solution.py:251
  27.5 0.1 slice_convert_fusion.3
  27.7 1.4 %slice_convert_fusion.1 = (f32[4,32,2048]{2,1,0:T(8,128)S(1)}, f32[4,32,2048]{2,1,0:T(8,128)S(1)}) fusion(bf16[4,32,4096]{2,1,0:T(8,128)(2,1)} %get-tuple-element.8), kind=kLoop, calls=%fused_computation.10 | loop fusion | flops 524288 | bytes 3145728 | tf_op jit(solution)/shard_map/convert_element_type | solution.py:49
  29.1 6.4 %subtract_reduce_fusion.1 = (f32[32,8,2048]{2,1,0:T(8,128)S(1)}, f32[32,8,2048]{2,1,0:T(8,128)S(1)}, f32[32,8,2048]{2,1,0:T(8,128)S(1)}, f32[32,8,2048]{2,1,0:T(8,128)S(1)}) fusion(f32[4,32,2048]{2,1,0:T(8,128)S(1)} %get-tuple-element.16, f32[4,8,2048]{2,1,0:T(8,128)S(1)} %get-tuple-element.29, f32[4,32,2048]{2,1,0:T(8,128)S(1)} %get-tuple-element.15, ...), kind=kLoop, calls=%fused_computation.1 | loop fusion | flops 31457280 | bytes 11534336 | tf_op jit(solution)/shard_map/reduce_sum | solution.py:52
  35.5 0.3 pad_maximum_fusion.1
  35.8 0.5 pad_maximum_fusion
  36.3 1.1 %negate_multiply_fusion = (f32[32,64,512]{2,1,0:T(8,128)S(1)}, f32[32,64,512]{2,1,0:T(8,128)S(1)}) fusion(f32[64,512]{1,0:T(8,128)S(1)} %get-tuple-element.28, f32[32,512]{1,0:T(8,128)S(1)} %get-tuple-element.26, f32[64,512]{1,0:T(8,128)S(1)} %get-tuple-element.27, f32[32,512]{1,0:T(8,128)S(1)} %get-tuple-element.25), kind=kLoop, calls=%fused_computation.6 | loop fusion | flops 9437184 | bytes 8781824 | tf_op jit(solution)/shard_map/mul | solution.py:34
  37.4 3.7 %fusion.13 = f32[512,512]{1,0:T(8,128)S(1)} fusion(f32[512,2048]{1,0:T(8,128)S(1)} %bitcast.25, f32[2048,512]{1,0:T(8,128)S(1)} %bitcast.27), kind=kOutput, calls=%fused_computation.40 | convolution fusion | flops 3221225472 | bytes 9437184 | tf_op jit(solution)/shard_map/dot_general | solution.py:257
  41.1 4.5 %convolution_add_fusion.x_ref = f32[512,512]{1,0:T(8,128)} fusion(f32[512,512]{1,0:T(8,128)S(1)} %fusion.13, f32[512,2048]{1,0:T(8,128)S(1)} %bitcast.24, f32[2048,512]{1,0:T(8,128)S(1)} %bitcast.26), kind=kOutput, calls=%fused_computation.8 | convolution fusion | flops 3221487616 | bytes 10485760 | tf_op jit(solution)/shard_map/dot_general | solution.py:260
  45.7 31.8 %shard_map.38 = bf16[2,2,8,512]{3,2,1,0:T(8,128)(2,1)} custom-call(f32[512,512]{1,0:T(8,128)} %convolution_add_fusion.x_ref), custom_call_target="tpu_custom_call" | custom-call | tf_op jit(solution)/shard_map/pallas_call | solution.py:229
  77.5 1.4 %copy.9 = bf16[2,2,8,512]{3,2,1,0:T(8,128)(2,1)} copy(bf16[2,2,8,512]{3,2,1,0:T(8,128)(2,1)} %shard_map.38) | data formatting | bytes 65536
  (2 shorter events, 0.0 us)
